TPU v7x, 32 devices: a whole 2x2x4 slice. The times are simulated.
32 devices in a mesh: dp: 2 (over x), expert: 16 (over z, y, core).
Axes of the slice: x: 2, y: 2, z: 4, core: 2. Of those that a mesh axis runs over, the one named last changes fastest.
Arguments:
- tokens: bfloat16 [2, 256, 2048], P('dp', 'expert'), may hold values from -6 to 6
- cotangent: bfloat16 [2, 256, 2048], P('dp', 'expert'), may hold values from -1.5 to 1.5
- routes: int32 [2, 256], P(None, 'expert'), may hold values from 0 to 15, as said below
- gate_prob: bfloat16 [2, 256], P(None, 'expert'), may hold values from 0.19921875 to 1
- w_gate: bfloat16 [16, 768, 2048], P('expert', 'dp'), may hold values from -0.125 to 0.125
- w_up: bfloat16 [16, 768, 2048], P('expert', 'dp'), may hold values from -0.125 to 0.125
- w_down: bfloat16 [16, 768, 2048], P('expert', 'dp'), may hold values from -0.21875 to 0.21875
Outputs:
- grad_tokens: bfloat16 [2, 256, 2048], P('dp', 'expert')
- grad_prob: float32 [2, 256], P('dp', 'expert')
- grad_w_gate: bfloat16 [16, 768, 2048], P('expert', 'dp')
- grad_w_up: bfloat16 [16, 768, 2048], P('expert', 'dp')
- grad_w_down: bfloat16 [16, 768, 2048], P('expert', 'dp')
Inputs may be any that keep to these rules, and one draw needn't show every extreme that they name: `routes`: one expert, the same for the whole micro-batch, is named by exactly 4 of the 16 tokens of every device (tokens[d, e * 16 : (e + 1) * 16] for each d and e). Of the 32 tokens with one index e of the expert axis, at most 3 name any other single expert, and one other expert, the same for every e, is named by exactly 3 of them.
All inputs are finite; a program needn't handle non-finite values.
Results may differ from a plain program's by a relative error of at most 0.0065.
Values may be sent and summed in bfloat16 or wider, within the bound.
No kernel may reach another device: no remote copies, remote signals or barrier semaphores. Data moves between devices by JAX's collectives and lax.ppermute only.
A program may use at most 64 MiB of HBM per device.

v0:
```python
import jax
import jax.numpy as jnp
from jax import lax
from jax.sharding import PartitionSpec as P


def broadcast(value, axis, root):
    mine = lax.axis_index(axis) == root
    return lax.psum(jnp.where(mine, value, jnp.zeros_like(value)), axis)


def silu_parts(gate_pre):
    sigma = jax.nn.sigmoid(gate_pre)
    return (gate_pre * sigma, sigma * (1.0 + gate_pre * (1.0 - sigma)))


def expert_terms(rows_x, rows_dy, rows_p, gate_w, up_w, down_w):
    gate_pre = jnp.einsum("rd,hd->rh", rows_x, gate_w, preferred_element_type=jnp.float32)
    up_pre = jnp.einsum("rd,hd->rh", rows_x, up_w, preferred_element_type=jnp.float32)
    swish_val, swish_slope = silu_parts(gate_pre)
    active = swish_val * up_pre
    weight = rows_p.astype(jnp.float32)[:, None]
    scaled_act = (weight * active).astype(jnp.bfloat16)
    back_proj = jnp.einsum("rd,hd->rh", rows_dy, down_w, preferred_element_type=jnp.float32)
    d_active = weight * back_proj
    d_gate = (d_active * up_pre * swish_slope).astype(jnp.bfloat16)
    d_up = (d_active * swish_val).astype(jnp.bfloat16)
    prob_part = jnp.sum(active * back_proj, axis=1).astype(jnp.bfloat16)
    feature_part = jnp.dot(d_gate, gate_w, preferred_element_type=jnp.float32)
    feature_part = (feature_part + jnp.dot(d_up, up_w, preferred_element_type=jnp.float32)).astype(
        jnp.bfloat16
    )
    weight_grads = (
        jnp.einsum("rh,rd->hd", d_gate, rows_x, preferred_element_type=jnp.float32),
        jnp.einsum("rh,rd->hd", d_up, rows_x, preferred_element_type=jnp.float32),
        jnp.einsum("rh,rd->hd", scaled_act, rows_dy, preferred_element_type=jnp.float32),
    )
    return (weight_grads, feature_part, prob_part)


def body(tokens, cotangent, routes, gate_prob, w_gate, w_up, w_down):
    groups = lax.axis_size("dp")
    experts = lax.axis_size("expert")
    tok_dev = tokens.shape[1]
    features = tokens.shape[2]
    group_size = groups * tok_dev
    hot_each = tok_dev // 4
    capacity = 4 * groups * (tok_dev - hot_each) // (3 * experts - 3) + 1
    slot_total = experts * capacity
    hot_rows = groups * hot_each
    all_x, all_dy = (
        lax.all_gather(tokens, "dp", axis=0, tiled=True),
        lax.all_gather(cotangent, "dp", axis=0, tiled=True),
    )
    flat_x = all_x.reshape(group_size, features)
    flat_dy = all_dy.reshape(group_size, features)
    flat_route = routes.reshape(group_size)
    flat_prob = gate_prob.reshape(group_size)
    expert_ids = jnp.arange(experts, dtype=jnp.int32)
    onehot = (flat_route[:, None] == expert_ids[None, :]).astype(jnp.int32)
    counts = jnp.sum(onehot, axis=0)
    hot_id = jnp.argmax(counts)
    is_hot = flat_route == hot_id
    earlier = jnp.cumsum(onehot, axis=0) - onehot
    slot_rank = jnp.sum(earlier * onehot, axis=1)
    slot_index = jnp.where(is_hot, slot_total, flat_route * capacity + slot_rank)
    hot_rank = jnp.cumsum(is_hot.astype(jnp.int32)) - 1
    hot_index = jnp.where(is_hot, hot_rank, hot_rows)
    token_ids = jnp.arange(1, group_size + 1, dtype=jnp.int32)
    slot_source = jnp.zeros((slot_total,), jnp.int32).at[slot_index].set(token_ids, mode="drop")
    hot_source = jnp.zeros((hot_rows,), jnp.int32).at[hot_index].set(token_ids, mode="drop")
    slot_pick = jnp.clip(slot_source - 1, 0, group_size - 1)
    hot_take = jnp.clip(hot_source - 1, 0, group_size - 1)
    send_x = flat_x[slot_pick]
    send_dy = flat_dy[slot_pick]
    send_prob = jnp.where(
        slot_source > 0, flat_prob[slot_pick], jnp.zeros((slot_total,), flat_prob.dtype)
    )
    hot_x = flat_x[hot_take]
    hot_dy = flat_dy[hot_take]
    hot_prob = jnp.where(
        hot_source > 0, flat_prob[hot_take], jnp.zeros((hot_rows,), flat_prob.dtype)
    )
    got_x = lax.all_to_all(send_x, "expert", split_axis=0, concat_axis=0, tiled=True)
    got_dy = lax.all_to_all(send_dy, "expert", split_axis=0, concat_axis=0, tiled=True)
    got_prob = lax.all_to_all(send_prob, "expert", split_axis=0, concat_axis=0, tiled=True)
    own_grads, own_feature, own_gate = expert_terms(
        got_x, got_dy, got_prob, w_gate[0], w_up[0], w_down[0]
    )
    back_feature = lax.all_to_all(own_feature, "expert", split_axis=0, concat_axis=0, tiled=True)
    back_gate = lax.all_to_all(own_gate, "expert", split_axis=0, concat_axis=0, tiled=True)
    own_grads, back_feature, back_gate = (own_grads, back_feature, back_gate)
    partial_grads, hot_feature, hot_gate = expert_terms(
        hot_x,
        hot_dy,
        hot_prob,
        broadcast(w_gate, "expert", hot_id)[0],
        broadcast(w_up, "expert", hot_id)[0],
        broadcast(w_down, "expert", hot_id)[0],
    )
    summed = lax.psum((partial_grads[0], partial_grads[1], partial_grads[2]), "expert")
    hot_sums, hot_feature, hot_gate = (summed, hot_feature, hot_gate)
    reg_pick = jnp.clip(slot_index, 0, slot_total - 1)
    hot_pick = jnp.clip(hot_index, 0, hot_rows - 1)
    feature_tok = jnp.where(is_hot[:, None], hot_feature[hot_pick], back_feature[reg_pick]).astype(
        jnp.float32
    )
    prob_tok = jnp.where(is_hot, hot_gate[hot_pick], back_gate[reg_pick]).astype(jnp.float32)
    token_sum, prob_sum = (
        lax.psum_scatter(
            feature_tok.reshape(groups, tok_dev, features).astype(jnp.bfloat16),
            "dp",
            scatter_dimension=0,
            tiled=True,
        ).astype(jnp.float32),
        lax.psum_scatter(
            prob_tok.reshape(groups, tok_dev).astype(jnp.bfloat16),
            "dp",
            scatter_dimension=0,
            tiled=True,
        ).astype(jnp.float32),
    )
    is_owner = lax.axis_index("expert") == hot_id
    grad_w_gate = jnp.where(is_owner, hot_sums[0], own_grads[0]).astype(jnp.bfloat16)[None]
    grad_w_up = jnp.where(is_owner, hot_sums[1], own_grads[1]).astype(jnp.bfloat16)[None]
    grad_w_down = jnp.where(is_owner, hot_sums[2], own_grads[2]).astype(jnp.bfloat16)[None]
    return (token_sum.astype(jnp.bfloat16), prob_sum, grad_w_gate, grad_w_up, grad_w_down)


def solution(mesh):
    in_specs = (
        P("dp", "expert", None),
        P("dp", "expert", None),
        P(None, "expert"),
        P(None, "expert"),
        P("expert", "dp", None),
        P("expert", "dp", None),
        P("expert", "dp", None),
    )
    out_specs = (
        P("dp", "expert", None),
        P("dp", "expert"),
        P("expert", "dp", None),
        P("expert", "dp", None),
        P("expert", "dp", None),
    )
    return jax.shard_map(body, mesh=mesh, in_specs=in_specs, out_specs=out_specs, check_vma=False)
```

profile of v0, /device:TPU:1, one launch (start us, length us, event | category | flops | bytes accessed | tf_op | source)
XLA Modules:
  0.0 404.0 jit_solution(10849968538770951406)
XLA Ops:
  7.2 0.8 eq.59
  7.9 0.7 broadcast_multiply_fusion
  9.6 1.2 broadcast_compare_fusion
  11.0 0.7 reshape.175
  12.2 0.7 scatter_custom_fusion.1
  12.9 0.8 gather_fusion.4
  13.7 0.7 all_to_all.49
  14.4 7.3 %all-to-all-start = ((bf16[16,3,1]{1,2,0:T(2,128)(2,1)}), bf16[16,3,1]{1,2,0:T(2,128)(2,1)S(1)}, u32[]{:S(2)}, u32[]{:S(2)}) async-start(bf16[16,3,1]{1,2,0:T(2,128)(2,1)} %all_to_all.49), calls=%async_computation | async-start | bytes 16384 | tf_op jit(solution)/shard_map/all_to_all | solution.py:86
  22.4 4.6 %all_gather.7 = bf16[2,16,2048]{2,1,0:T(8,128)(2,1)S(1)} all-gather(bf16[1,16,2048]{2,1,0:T(8,128)(2,1)} %param.7), channel_id=1, replica_groups=mesh['dp'=2,'expert'=16] {'dp'}, dimensions={0}, use_global_device_ids=true | all-gather | bytes 196608 | tf_op jit(solution)/shard_map/all_gather | solution.py:52
  26.9 1.9 select_bitcast_fusion
  28.8 0.7 gather_fusion.6
  29.5 0.9 all_to_all.41
  30.4 6.6 %all-to-all-start.2 = ((bf16[16,3,2048]{2,1,0:T(4,128)(2,1)}), bf16[16,3,2048]{2,1,0:T(4,128)(2,1)}, u32[]{:S(2)}, u32[]{:S(2)}) async-start(bf16[16,3,2048]{2,1,0:T(4,128)(2,1)} %all_to_all.41), calls=%async_computation.2 | async-start | bytes 524288 | tf_op jit(solution)/shard_map/all_to_all | solution.py:84
  37.0 1.2 select_bitcast_fusion.2
  39.1 4.3 %all_gather.6 = bf16[2,16,2048]{2,1,0:T(8,128)(2,1)S(1)} all-gather(bf16[1,16,2048]{2,1,0:T(8,128)(2,1)S(1)} %copy-done.15), channel_id=1, replica_groups=mesh['dp'=2,'expert'=16] {'dp'}, dimensions={0}, use_global_device_ids=true | all-gather | bytes 196608 | tf_op jit(solution)/shard_map/all_gather | solution.py:53
  43.4 0.7 gather_fusion.5
  44.1 0.8 all_to_all.38
  45.0 1.6 all-to-all-done.2
  46.6 5.2 %all-to-all-start.1 = ((bf16[16,3,2048]{2,1,0:T(4,128)(2,1)}), bf16[16,3,2048]{2,1,0:T(4,128)(2,1)}, u32[]{:S(2)}, u32[]{:S(2)}) async-start(bf16[16,3,2048]{2,1,0:T(4,128)(2,1)} %all_to_all.38), calls=%async_computation.1 | async-start | bytes 524288 | tf_op jit(solution)/shard_map/all_to_all | solution.py:85
  51.9 1.8 all_to_all.43
  53.7 11.6 %all-to-all-done.1 = bf16[16,3,2048]{2,1,0:T(4,128)(2,1)} async-done(((bf16[16,3,2048]{2,1,0:T(4,128)(2,1)}), bf16[16,3,2048]{2,1,0:T(4,128)(2,1)}, u32[]{:S(2)}, u32[]{:S(2)}) %all-to-all-start.1) | async-done | bytes 196640 | tf_op jit(solution)/shard_map/all_to_all | solution.py:85
  65.3 1.8 all_to_all.40
  67.1 1.6 fusion.7
  68.7 1.5 fusion.10
  70.3 1.3 multiply_reduce_fusion
  71.6 0.7 convert_element_type.107
  72.3 4.5 %all-to-all-start.4 = ((bf16[16,3,1]{1,2,0:T(2,128)(2,1)}), bf16[16,3,1]{1,2,0:T(2,128)(2,1)S(1)}, u32[]{:S(2)}, u32[]{:S(2)}) async-start(bf16[16,3,1]{1,2,0:T(2,128)(2,1)} %convert_element_type.107), calls=%async_computation.5 | async-start | bytes 16384 | tf_op jit(solution)/shard_map/all_to_all | solution.py:91
  76.8 1.2 fusion.5
  78.4 0.8 all_to_all.44
  79.2 3.6 all-to-all-done.4
  82.8 4.1 %all-to-all-start.3 = ((bf16[16,3,2048]{2,1,0:T(4,128)(2,1)}), bf16[16,3,2048]{2,1,0:T(4,128)(2,1)S(1)}, u32[]{:S(2)}, u32[]{:S(2)}) async-start(bf16[16,3,2048]{2,1,0:T(4,128)(2,1)} %all_to_all.44), calls=%async_computation.3 | async-start | bytes 524288 | tf_op jit(solution)/shard_map/all_to_all | solution.py:90
  89.6 0.7 gather_fusion.9
  90.4 6.5 %all-to-all-done.3 = bf16[16,3,2048]{2,1,0:T(4,128)(2,1)S(1)} async-done(((bf16[16,3,2048]{2,1,0:T(4,128)(2,1)}), bf16[16,3,2048]{2,1,0:T(4,128)(2,1)S(1)}, u32[]{:S(2)}, u32[]{:S(2)}) %all-to-all-start.3) | async-done | bytes 196640 | tf_op jit(solution)/shard_map/all_to_all | solution.py:90
  97.7 67.8 %all-reduce.6.cloned.1.call-done = (bf16[384,2048]{1,0:T(8,128)(2,1)}, bf16[384,2048]{1,0:T(8,128)(2,1)}, bf16[384,2048]{1,0:T(8,128)(2,1)}) async-done(((bf16[384,2048]{1,0:T(8,128)(2,1)}, bf16[384,2048]{1,0:T(8,128)(2,1)}, bf16[384,2048]{1,0:T(8,128)(2,1)}), (bf16[384,2048]{1,0:T(8,128)(2,1)}, bf16[384,2048]{1,0:T(8,128)(2,1)}, bf16[384,2048]{1,0:T(8,128)(2,1)})) %all-reduce.6.cloned.1.call-update) | async-done | bytes 4718608 | tf_op jit(solution)/shard_map/psum | solution.py:9
  165.5 2.0 fusion.35
  168.1 0.7 fusion.24
  168.8 0.7 copy-done.11
  170.6 2.3 fusion.37
  172.9 2.3 fusion.38
  175.6 0.7 gather_fusion.8
  176.9 3.8 all-reduce
  180.7 1.3 gather_fusion.3
  182.0 1.7 broadcast_select_fusion
  183.7 206.9 %all-reduce.7 = (bf16[384,2048]{1,0:T(8,128)(2,1)}, bf16[384,2048]{1,0:T(8,128)(2,1)}, bf16[384,2048]{1,0:T(8,128)(2,1)}) all-reduce(f32[384,2048]{1,0:T(8,128)} %fusion.37, f32[384,2048]{1,0:T(8,128)} %fusion.38, f32[384,2048]{1,0:T(8,128)S(1)} %fusion.24), channel_id=1, replica_groups=mesh['dp'=2,'expert'=16] {'expert'}, use_global_device_ids=true, to_apply=%region_14.15 | all-reduce | flops 2359296 | bytes 14155776 | tf_op jit(solution)/shard_map/psum | solution.py:101
  390.6 1.7 fusion
  392.4 1.7 fusion.1
  394.1 1.2 dynamic-slice_convert_fusion
  395.3 1.8 fusion.2
  (81 shorter events, 9.3 us)
Async XLA Ops:
  14.4 15.9 %all-to-all-start = ((bf16[16,3,1]{1,2,0:T(2,128)(2,1)}), bf16[16,3,1]{1,2,0:T(2,128)(2,1)S(1)}, u32[]{:S(2)}, u32[]{:S(2)}) async-start(bf16[16,3,1]{1,2,0:T(2,128)(2,1)} %all_to_all.49), calls=%async_computation | async-start | bytes 16384 | tf_op jit(solution)/shard_map/all_to_all | solution.py:86
  28.8 8.2 %copy-start.4 = (bf16[1,384,2048]{2,1,0:T(8,128)(2,1)S(1)}, bf16[1,384,2048]{2,1,0:T(8,128)(2,1)}, u32[]{:S(2)}) copy-start(bf16[1,384,2048]{2,1,0:T(8,128)(2,1)} %param.13) | copy-start | bytes 4718596
  30.4 16.2 %all-to-all-start.2 = ((bf16[16,3,2048]{2,1,0:T(4,128)(2,1)}), bf16[16,3,2048]{2,1,0:T(4,128)(2,1)}, u32[]{:S(2)}, u32[]{:S(2)}) async-start(bf16[16,3,2048]{2,1,0:T(4,128)(2,1)} %all_to_all.41), calls=%async_computation.2 | async-start | bytes 524288 | tf_op jit(solution)/shard_map/all_to_all | solution.py:84
  37.0 128.6 %all-reduce.6.cloned.1.call-start = ((), (), s32[]{:S(2)}) async-start(), calls=%async_computation.7 | async-start | bytes 9437184 | tf_op jit(solution)/shard_map/psum | solution.py:9
  38.3 0.8 copy-start.15
  43.4 23.7 %copy-start = (bf16[1,384,2048]{2,1,0:T(8,128)(2,1)S(1)}, bf16[1,384,2048]{2,1,0:T(8,128)(2,1)}, u32[]{:S(2)}) copy-start(bf16[1,384,2048]{2,1,0:T(8,128)(2,1)} %param.11) | copy-start | bytes 4718596
  45.0 23.8 %copy-start.1 = (bf16[1,384,2048]{2,1,0:T(8,128)(2,1)S(1)}, bf16[1,384,2048]{2,1,0:T(8,128)(2,1)}, u32[]{:S(2)}) copy-start(bf16[1,384,2048]{2,1,0:T(8,128)(2,1)} %param.12) | copy-start | bytes 4718596
  46.6 18.7 %all-to-all-start.1 = ((bf16[16,3,2048]{2,1,0:T(4,128)(2,1)}), bf16[16,3,2048]{2,1,0:T(4,128)(2,1)}, u32[]{:S(2)}, u32[]{:S(2)}) async-start(bf16[16,3,2048]{2,1,0:T(4,128)(2,1)} %all_to_all.38), calls=%async_computation.1 | async-start | bytes 524288 | tf_op jit(solution)/shard_map/all_to_all | solution.py:85
  67.1 3.2 copy-start.5
  67.1 3.2 copy-start.7
  70.3 1.3 copy-start.12
  72.3 10.5 %all-to-all-start.4 = ((bf16[16,3,1]{1,2,0:T(2,128)(2,1)}), bf16[16,3,1]{1,2,0:T(2,128)(2,1)S(1)}, u32[]{:S(2)}, u32[]{:S(2)}) async-start(bf16[16,3,1]{1,2,0:T(2,128)(2,1)} %convert_element_type.107), calls=%async_computation.5 | async-start | bytes 16384 | tf_op jit(solution)/shard_map/all_to_all | solution.py:91
  78.4 10.4 %copy-start.17 = (u32[32]{0:T(128)S(1)}, u32[32]{0:T(128)}, u32[]{:S(2)}) copy-start(u32[32]{0:T(128)} %constant.62) | copy-start | bytes 388
  82.8 14.1 %all-to-all-start.3 = ((bf16[16,3,2048]{2,1,0:T(4,128)(2,1)}), bf16[16,3,2048]{2,1,0:T(4,128)(2,1)S(1)}, u32[]{:S(2)}, u32[]{:S(2)}) async-start(bf16[16,3,2048]{2,1,0:T(4,128)(2,1)} %all_to_all.44), calls=%async_computation.3 | async-start | bytes 524288 | tf_op jit(solution)/shard_map/all_to_all | solution.py:90
  86.9 310.2 %reduce-scatter.2.cloned.1.call-start = ((), (), s32[]{:S(2)}) async-start(), calls=%async_computation.6 | async-start | bytes 196608 | tf_op jit(solution)/shard_map/reduce_scatter | solution.py:110
  165.5 2.0 copy-start.2
  168.1 1.4 copy-start.11
  168.8 1.5 copy-start.3
  175.2 1.1 copy-start.16
  183.7 206.9 %copy-start.6 = (bf16[48,2048]{1,0:T(8,128)(2,1)S(1)}, bf16[48,2048]{1,0:T(8,128)(2,1)}, u32[]{:S(2)}) copy-start(bf16[48,2048]{1,0:T(8,128)(2,1)} %all_to_all.43) | copy-start | bytes 589828
  183.7 206.9 %copy-start.14 = (bf16[48,384]{1,0:T(8,128)(2,1)S(1)}, bf16[48,384]{1,0:T(8,128)(2,1)}, u32[]{:S(2)}) copy-start(bf16[48,384]{1,0:T(8,128)(2,1)} %get-tuple-element.22) | copy-start | bytes 110596
  390.6 1.7 copy-start.10
  392.4 2.9 copy-start.8
  392.4 2.9 copy-start.9
  392.4 2.9 copy-start.13
Sparse Core Ops, SparseCore 0:
  42.3 123.1 all-reduce.5
  183.8 11.7 reduce-scatter.1
where the time goes:
time: 405 us; the launch traced here: 404 us
  blocking collectives  220 us (54%)
  waiting for transfers between devices  91.2 us (23%)
  starting transfers between devices  27.8 us (7%)
  local copies, waits for them, and re-layouts  20.4 us (5%)
  matrix products  20.4 us (5%)
  between operations  14.9 us (4%)
  other arithmetic  9.78 us (2%)
    psum x1, blocking collectives, body(): lax.psum((partial_grads[0], partial_grads[1], partial_grads[2]), 'expert')  207 us
    psum x1, waiting for transfers between devices, broadcast(): return lax.psum(jnp.where(mine, value, jnp.zeros_like(value)), axis)  67.8 us
    all_to_all x1, waiting for transfers between devices, body(): lax.all_to_all(send_dy, 'expert', split_axis=0, concat_axis=0, tiled=True)  11.6 us
  transfers between devices with their start and end apart: 7, of which 5 were waited for; matrix products, arithmetic and copies ran while one was open for 6% of the time, Pallas kernels for 0%

commit v1 on v0

v1 whole, which is shorter than its diff:
```python
import jax
import jax.numpy as jnp
from jax import lax
from jax.sharding import PartitionSpec as P

AXES = ("dp", "expert")
LANES = 128


def body(tokens, cotangent, routes, gate_prob, w_gate, w_up, w_down):
    groups = lax.axis_size("dp")
    experts = lax.axis_size("expert")
    tok_dev = tokens.shape[1]
    features = tokens.shape[2]
    slots = tok_dev // 4
    rows = groups * experts * slots
    f32, bf16 = jnp.float32, jnp.bfloat16
    mine = lax.axis_index("dp")

    route = lax.dynamic_index_in_dim(routes, mine, 0, keepdims=False)
    prob = lax.dynamic_index_in_dim(gate_prob, mine, 0, keepdims=False)
    token_ids = jnp.arange(tok_dev, dtype=jnp.int32)
    same = route[:, None] == route[None, :]
    earlier = same & (token_ids[None, :] < token_ids[:, None])
    rank = jnp.sum(earlier.astype(jnp.int32), axis=1)
    slot = route * slots + rank
    slot_ids = jnp.arange(experts * slots, dtype=jnp.int32)
    pick = (slot[:, None] == slot_ids[None, :]).astype(bf16)

    packed = jnp.concatenate(
        [tokens[0], cotangent[0], jnp.broadcast_to(prob[:, None], (tok_dev, LANES))], axis=1
    )
    send = jnp.dot(pick.T, packed, preferred_element_type=f32).astype(bf16)
    send = send.reshape(1, experts, slots, packed.shape[1])
    send = jnp.broadcast_to(send, (groups,) + send.shape[1:])
    send = send.reshape(groups * experts, slots, packed.shape[1])
    got = lax.all_to_all(send, AXES, split_axis=0, concat_axis=0, tiled=True)
    got = got.reshape(rows, packed.shape[1])
    rows_x = got[:, :features]
    rows_dy = got[:, features : 2 * features]
    weight = got[:, 2 * features : 2 * features + 1].astype(f32)

    gate_w, up_w, down_w = w_gate[0], w_up[0], w_down[0]
    gate_pre = jnp.einsum("rd,hd->rh", rows_x, gate_w, preferred_element_type=f32)
    up_pre = jnp.einsum("rd,hd->rh", rows_x, up_w, preferred_element_type=f32)
    back_proj = jnp.einsum("rd,hd->rh", rows_dy, down_w, preferred_element_type=f32)
    sigma = jax.nn.sigmoid(gate_pre)
    swish = gate_pre * sigma
    slope = sigma * (1.0 + gate_pre * (1.0 - sigma))
    active = swish * up_pre
    scaled_act = (weight * active).astype(bf16)
    d_active = weight * back_proj
    d_gate = (d_active * up_pre * slope).astype(bf16)
    d_up = (d_active * swish).astype(bf16)
    prob_part = jnp.sum(active * back_proj, axis=1, keepdims=True).astype(bf16)
    feature_part = jnp.dot(d_gate, gate_w, preferred_element_type=f32)
    feature_part = feature_part + jnp.dot(d_up, up_w, preferred_element_type=f32)
    reply = jnp.concatenate(
        [feature_part.astype(bf16), jnp.broadcast_to(prob_part, (rows, LANES))], axis=1
    )
    reply = reply.reshape(groups * experts, slots, features + LANES)
    back = lax.all_to_all(reply, AXES, split_axis=0, concat_axis=0, tiled=True)
    back = back.reshape(rows, features + LANES)
    total = jnp.dot(jnp.tile(pick, (1, groups)), back, preferred_element_type=f32)

    grad_w_gate = jnp.einsum("rh,rd->hd", d_gate, rows_x, preferred_element_type=f32)
    grad_w_up = jnp.einsum("rh,rd->hd", d_up, rows_x, preferred_element_type=f32)
    grad_w_down = jnp.einsum("rh,rd->hd", scaled_act, rows_dy, preferred_element_type=f32)
    return (
        total[None, :, :features].astype(bf16),
        total[None, :, features],
        grad_w_gate.astype(bf16)[None],
        grad_w_up.astype(bf16)[None],
        grad_w_down.astype(bf16)[None],
    )


def solution(mesh):
    in_specs = (
        P("dp", "expert", None),
        P("dp", "expert", None),
        P(None, "expert"),
        P(None, "expert"),
        P("expert", "dp", None),
        P("expert", "dp", None),
        P("expert", "dp", None),
    )
    out_specs = (
        P("dp", "expert", None),
        P("dp", "expert"),
        P("expert", "dp", None),
        P("expert", "dp", None),
        P("expert", "dp", None),
    )
    return jax.shard_map(body, mesh=mesh, in_specs=in_specs, out_specs=out_specs, check_vma=False)
```

time: 405 us -> 70.3 us (0.17)
  blocking collectives: 220 us -> 35.5 us
  waiting for transfers between devices: 91.2 us -> 10.7 us
  starting transfers between devices: 27.8 us -> 2.6 us
  between operations: 14.9 us -> 0.78 us
  local copies, waits for them, and re-layouts: 20.4 us -> 6.83 us
  matrix products: 20.4 us -> 11.7 us
  other arithmetic: 9.78 us -> 1.09 us
    psum x1 -> x0, blocking collectives: 207 us -> none  [body(): lax.psum((partial_grads[0], partial_grads[1], partial_grads[2]), 'expert')]
    psum x1 -> x0, waiting for transfers between devices: 67.8 us -> none  [broadcast(): return lax.psum(jnp.where(mine, value, jnp.zeros_like(value)), axis)]
    all_to_all x0 -> x1, blocking collectives: none -> 35.5 us  [body(): got = lax.all_to_all(send, AXES, split_axis=0, concat_axis=0, tiled=True)]
    all_to_all x5 -> x1, starting transfers between devices: 27.7 us -> 2.6 us  [body(): back = lax.all_to_all(reply, AXES, split_axis=0, concat_axis=0, tiled=True)]
    all_to_all x5 -> x1, waiting for transfers between devices: 23.3 us -> 10.7 us  [body(): back = lax.all_to_all(reply, AXES, split_axis=0, concat_axis=0, tiled=True)]
    all_gather x2 -> x0, blocking collectives: 8.87 us -> none  [the longest x1 4.55 us: body(): lax.all_gather(tokens, 'dp', axis=0, tiled=True)]
    dot_general x16 -> x10, matrix products: 20.4 us -> 11.7 us  [the longest x1 2.1 us: body(): up_pre = jnp.einsum('rd,hd->rh', rows_x, up_w, preferred_element_type=f32)]
    gather x12 -> x0, local copies, waits for them, and re-layouts: 7.5 us -> none  [the longest x1 1.3 us: body(): hot_feature[hot_pick]]
  transfers between devices with their start and end apart: 7 -> 1, of which waited for: 5 -> 1; matrix products, arithmetic and copies ran while one was open for 6% -> 8% of each run, Pallas kernels for 0% -> 0%
where the time goes in v1:
time: 70.3 us; the launch traced here: 69.2 us
  blocking collectives  35.5 us (50%)
  matrix products  11.7 us (17%)
  waiting for transfers between devices  10.7 us (15%)
  local copies, waits for them, and re-layouts  6.83 us (10%)
  starting transfers between devices  2.6 us (4%)
  other arithmetic  1.09 us (2%)
  between operations  0.78 us (1%)
    all_to_all x1, blocking collectives, body(): got = lax.all_to_all(send, AXES, split_axis=0, concat_axis=0, tiled=True)  35.5 us
    all_to_all x1, waiting for transfers between devices, body(): back = lax.all_to_all(reply, AXES, split_axis=0, concat_axis=0, tiled=True)  10.7 us
    all_to_all x1, starting transfers between devices, body(): back = lax.all_to_all(reply, AXES, split_axis=0, concat_axis=0, tiled=True)  2.6 us
    dot_general x1, matrix products, body(): up_pre = jnp.einsum('rd,hd->rh', rows_x, up_w, preferred_element_type=f32)  2.1 us
    dot_general x1, matrix products, body(): jnp.einsum('rh,rd->hd', scaled_act, rows_dy, preferred_element_type=f32)  1.8 us
    dot_general x1, matrix products, body(): jnp.einsum('rh,rd->hd', d_up, rows_x, preferred_element_type=f32)  1.74 us
    dot_general x1, matrix products, body(): jnp.einsum('rh,rd->hd', d_gate, rows_x, preferred_element_type=f32)  1.74 us
  transfers between devices with their start and end apart: 1, of which 1 were waited for; matrix products, arithmetic and copies ran while one was open for 8% of the time, Pallas kernels for 0%

profile of v1, /device:TPU:1, one launch (start us, length us, event | category | flops | bytes accessed | tf_op | source)
XLA Modules:
  0.0 69.2 jit_solution(16495721779561169750)
XLA Ops:
  0.6 0.0 copy-start
  0.7 0.8 %dynamic-slice_bitcast_fusion = bf16[16]{0:T(256)(128)(2,1)S(1)} fusion(bf16[2,16]{1,0:T(2,128)(2,1)} %param.10, s32[]{:T(128)S(6)} %select_n.6), kind=kLoop, calls=%fused_computation.48 | loop fusion | bytes 68 | tf_op jit(solution)/shard_map/broadcast_in_dim | solution.py:31
  1.4 0.7 dynamic-slice_bitcast_fusion.1
  2.1 0.2 convert_reduce_fusion.1
  2.3 0.7 multiply_add_fusion
  3.0 0.1 broadcast_in_dim.17
  3.1 1.3 %convolution_convert_fusion = bf16[64,4224]{1,0:T(8,128)(2,1)S(1)} fusion(bf16[16,128]{1,0:T(8,128)(2,1)S(1)} %broadcast_in_dim.17, bf16[16,2048]{1,0:T(8,128)(2,1)} %bitcast.40, bf16[16,2048]{1,0:T(8,128)(2,1)} %bitcast.41, s32[16]{0:T(128)S(1)} %multiply_add_fusion), kind=kOutput, calls=%fused_computation | convolution fusion | flops 9327616 | bytes 675904 | tf_op jit(solution)/shard_map/dot_general | solution.py:33
  4.4 0.1 broadcast_in_dim.18
  4.5 0.3 broadcast_in_dim.19
  4.8 35.5 %all_to_all.10 = bf16[32,4,4224]{2,1,0:T(4,128)(2,1)} all-to-all(bf16[32,4,4224]{2,1,0:T(4,128)(2,1)S(1)} %bitcast.39), channel_id=1, replica_groups=mesh['dp'=2,'expert'=16] {'dp','expert'}, dimensions={0} | all-to-all | bytes 2162688 | tf_op jit(solution)/shard_map/all_to_all | solution.py:37
  40.3 1.3 %reshape.64 = bf16[128,4224]{1,0:T(8,128)(2,1)S(1)} reshape(bf16[32,4,4224]{2,1,0:T(4,128)(2,1)} %all_to_all.10) | data formatting | bytes 2162688 | tf_op jit(solution)/shard_map/reshape | solution.py:38
  41.6 0.0 copy-start.2
  41.7 0.1 convert_reduce_fusion
  41.8 2.1 %fusion.9 = f32[128,384]{1,0:T(8,128)S(1)} fusion(bf16[1,384,2048]{2,1,0:T(8,128)(2,1)} %param.12, bf16[128,4224]{1,0:T(8,128)(2,1)S(1)} %reshape.64), kind=kOutput, calls=%fused_computation.14 | convolution fusion | flops 201326592 | bytes 2293760 | tf_op jit(solution)/shard_map/rd,hd->rh/dot_general | solution.py:45
  43.9 0.0 copy-done.2
  43.9 0.6 fusion.11
  44.5 0.0 copy-done
  44.5 1.4 %multiply_convert_fusion.2 = (bf16[128,384]{1,0:T(8,128)(2,1)S(1)}, bf16[128]{0:T(256)(128)(2,1)S(1)}, bf16[128,384]{1,0:T(8,128)(2,1)S(1)}, f32[128,384]{1,0:T(8,128)}) fusion(f32[128,384]{1,0:T(8,128)S(1)} %fusion.9, f32[128,384]{1,0:T(8,128)S(1)} %fusion.11, f32[128]{0:T(128)S(1)} %convert_reduce_fusion, bf16[1,384,2048]{2,1,0:T(8,128)(2,1)S(1)} %copy-done, ...), kind=kOutput, calls=%fused_computation.28 | convolution fusion | flops 202162048 | bytes 2884352 | tf_op jit(solution)/shard_map/rd,hd->rh/dot_general | solution.py:44
  45.9 0.0 copy-start.3
  45.9 0.0 copy-start.1
  45.9 0.4 fusion.4
  46.3 1.0 %copy-done.1 = bf16[1,384,2048]{2,1,0:T(8,128)(2,1)S(1)} copy-done((bf16[1,384,2048]{2,1,0:T(8,128)(2,1)S(1)}, bf16[1,384,2048]{2,1,0:T(8,128)(2,1)}, u32[]{:S(2)}) %copy-start.1) | copy-done | bytes 1572888
  47.3 0.4 fusion.3
  47.7 0.0 copy-done.3
  47.8 0.1 broadcast_in_dim.20
  47.9 0.9 %reshape.65 = bf16[32,4,2176]{2,1,0:T(4,128)(2,1)} reshape(bf16[128,2176]{1,0:T(8,128)(2,1)S(1)} %pad_maximum_fusion) | data formatting | bytes 1114112 | tf_op jit(solution)/shard_map/reshape | solution.py:61
  48.8 2.6 %all-to-all-start.1 = ((bf16[32,4,2176]{2,1,0:T(4,128)(2,1)}), bf16[32,4,2176]{2,1,0:T(4,128)(2,1)S(1)}, u32[]{:S(2)}, u32[]{:S(2)}) async-start(bf16[32,4,2176]{2,1,0:T(4,128)(2,1)} %reshape.65), calls=%async_computation.1 | async-start | bytes 1114112 | tf_op jit(solution)/shard_map/all_to_all | solution.py:62
  51.4 0.1 fusion.28
  51.5 0.1 tile.10
  51.6 0.0 copy-start.4
  51.6 1.7 %fusion.1 = bf16[1,384,2048]{2,1,0:T(8,128)(2,1)} fusion(bf16[128,384]{1,0:T(8,128)(2,1)S(1)} %get-tuple-element.7, bf16[128,4224]{1,0:T(8,128)(2,1)S(1)} %reshape.64), kind=kOutput, calls=%fused_computation.5 | convolution fusion | flops 202113024 | bytes 2195456 | tf_op jit(solution)/shard_map/rh,rd->hd/dot_general | solution.py:67
  53.3 0.0 copy-done.4
  53.3 0.0 copy-start.5
  53.4 1.7 %fusion = bf16[1,384,2048]{2,1,0:T(8,128)(2,1)} fusion(bf16[128,384]{1,0:T(8,128)(2,1)S(1)} %copy-done.4, bf16[128,4224]{1,0:T(8,128)(2,1)S(1)} %reshape.64), kind=kOutput, calls=%fused_computation.4 | convolution fusion | flops 202113024 | bytes 2195456 | tf_op jit(solution)/shard_map/rh,rd->hd/dot_general | solution.py:66
  55.1 0.0 copy-done.5
  55.1 1.8 %fusion.2 = bf16[1,384,2048]{2,1,0:T(8,128)(2,1)} fusion(bf16[128,4224]{1,0:T(8,128)(2,1)S(1)} %reshape.64, f32[128]{0:T(128)S(1)} %convert_reduce_fusion, f32[128,384]{1,0:T(8,128)S(1)} %fusion.9, f32[128,384]{1,0:T(8,128)S(1)} %copy-done.5), kind=kOutput, calls=%fused_computation.6 | convolution fusion | flops 202457088 | bytes 2490880 | tf_op jit(solution)/shard_map/rh,rd->hd/dot_general | solution.py:68
  56.9 10.7 %all-to-all-done.1 = bf16[32,4,2176]{2,1,0:T(4,128)(2,1)S(1)} async-done(((bf16[32,4,2176]{2,1,0:T(4,128)(2,1)}), bf16[32,4,2176]{2,1,0:T(4,128)(2,1)S(1)}, u32[]{:S(2)}, u32[]{:S(2)}) %all-to-all-start.1) | async-done | bytes 557088 | tf_op jit(solution)/shard_map/all_to_all | solution.py:62
  67.6 0.1 reshape.66
  67.7 0.2 fusion.33
  67.9 0.6 slice_reduce_fusion
  68.5 0.6 fusion.27
  (2 shorter events, 0.1 us)
Async XLA Ops:
  0.6 43.9 %copy-start = (bf16[1,384,2048]{2,1,0:T(8,128)(2,1)S(1)}, bf16[1,384,2048]{2,1,0:T(8,128)(2,1)}, u32[]{:S(2)}) copy-start(bf16[1,384,2048]{2,1,0:T(8,128)(2,1)} %param.11) | copy-start | bytes 4718596
  41.6 2.2 %copy-start.2 = (bf16[1,384,2048]{2,1,0:T(8,128)(2,1)S(1)}, bf16[1,384,2048]{2,1,0:T(8,128)(2,1)}, u32[]{:S(2)}) copy-start(bf16[1,384,2048]{2,1,0:T(8,128)(2,1)} %param.13) | copy-start | bytes 4718596
  45.9 1.9 %copy-start.3 = (bf16[128,384]{1,0:T(8,128)(2,1)}, bf16[128,384]{1,0:T(8,128)(2,1)S(1)}, u32[]{:S(2)}) copy-start(bf16[128,384]{1,0:T(8,128)(2,1)S(1)} %get-tuple-element.5) | copy-start | bytes 294916
  45.9 1.4 %copy-start.1 = (bf16[1,384,2048]{2,1,0:T(8,128)(2,1)S(1)}, bf16[1,384,2048]{2,1,0:T(8,128)(2,1)}, u32[]{:S(2)}) copy-start(bf16[1,384,2048]{2,1,0:T(8,128)(2,1)} %param.12) | copy-start | bytes 4718596
  48.8 18.7 %all-to-all-start.1 = ((bf16[32,4,2176]{2,1,0:T(4,128)(2,1)}), bf16[32,4,2176]{2,1,0:T(4,128)(2,1)S(1)}, u32[]{:S(2)}, u32[]{:S(2)}) async-start(bf16[32,4,2176]{2,1,0:T(4,128)(2,1)} %reshape.65), calls=%async_computation.1 | async-start | bytes 1114112 | tf_op jit(solution)/shard_map/all_to_all | solution.py:62
  51.6 1.7 %copy-start.4 = (bf16[128,384]{1,0:T(8,128)(2,1)S(1)}, bf16[128,384]{1,0:T(8,128)(2,1)}, u32[]{:S(2)}) copy-start(bf16[128,384]{1,0:T(8,128)(2,1)} %copy-done.3) | copy-start | bytes 294916
  53.3 1.7 %copy-start.5 = (f32[128,384]{1,0:T(8,128)S(1)}, f32[128,384]{1,0:T(8,128)}, u32[]{:S(2)}) copy-start(f32[128,384]{1,0:T(8,128)} %get-tuple-element.8) | copy-start | bytes 589828

commit v2 on v1

v2 whole, which is shorter than its diff:
```python
import jax
import jax.numpy as jnp
from jax import lax
from jax.experimental import pallas as pl
from jax.experimental.pallas import tpu as pltpu
from jax.sharding import PartitionSpec as P

AXES = ("dp", "expert")
LANES = 128
F32, BF16 = jnp.float32, jnp.bfloat16
VMEM = pl.BlockSpec(memory_space=pltpu.VMEM)
SMEM = pl.BlockSpec(memory_space=pltpu.SMEM)


def dot(a, b, dims):
    return lax.dot_general(a, b, ((dims[:1], dims[1:]), ((), ())), preferred_element_type=F32)


def pack_kernel(slots, mine_ref, route_s, route_v, prob_v, tok_ref, cot_ref, send_ref, pick_ref):
    mine = mine_ref[0]
    tok_dev, features = tok_ref.shape
    block = pick_ref.shape[0]
    groups = send_ref.shape[0] // block
    own = lax.broadcasted_iota(jnp.int32, route_v.shape, 0) == mine
    route = jnp.sum(jnp.where(own, route_v[...], 0), axis=0, keepdims=True)
    prob = jnp.sum(jnp.where(own, prob_v[...].astype(F32), 0.0), axis=0, keepdims=True)
    token = lax.broadcasted_iota(jnp.int32, (1, tok_dev), 1)
    rank = jnp.zeros((1, tok_dev), jnp.int32)
    for t in range(tok_dev):
        rank += ((route == route_s[mine, t]) & (token > t)).astype(jnp.int32)
    target = route * (2 * slots) + rank
    row = lax.broadcasted_iota(jnp.int32, (block, tok_dev), 0)
    pick_x = (row == target).astype(F32)
    pick_y = (row == target + slots).astype(F32)
    weight = jnp.sum(pick_x * prob, axis=1, keepdims=True)
    pick_x, pick_y = pick_x.astype(BF16), pick_y.astype(BF16)
    pick_ref[:, :tok_dev] = pick_x
    pick_ref[:, tok_dev:] = pick_y
    sent = dot(pick_x, tok_ref[...], (1, 0)) + dot(pick_y, cot_ref[...], (1, 0))
    sent = sent.astype(BF16)
    weight = jnp.broadcast_to(weight, (block, LANES)).astype(BF16)
    for g in range(groups):
        send_ref[g * block : (g + 1) * block, :features] = sent
        send_ref[g * block : (g + 1) * block, features:] = weight


def expert_kernel(slots, chunk, got_ref, gate_ref, up_ref, down_ref, reply_ref, dg_ref, du_ref, sa_ref):
    features = gate_ref.shape[1]
    half = features // 2

    @pl.loop(0, got_ref.shape[0] // chunk)
    def _(step):
        at = pl.ds(pl.multiple_of(step * chunk, chunk), chunk)
        data = got_ref[at, :features]
        weight = got_ref[at, features : features + 1].astype(F32)
        gate_pre = dot(data, gate_ref[...], (1, 1))
        up_pre = dot(data, up_ref[...], (1, 1))
        back_proj = dot(data, down_ref[...], (1, 1))
        back_proj = pltpu.roll(back_proj, chunk - slots, 0)
        sigma = jax.nn.sigmoid(gate_pre)
        swish = gate_pre * sigma
        slope = sigma * (1.0 + gate_pre * (1.0 - sigma))
        active = swish * up_pre
        scaled = weight * active
        d_active = weight * back_proj
        d_gate = d_active * up_pre * slope
        d_up = d_active * swish
        part = jnp.sum(active * back_proj, axis=1, keepdims=True)
        dg, dg_low = d_gate.astype(BF16), pltpu.roll(d_gate, slots, 0).astype(BF16)
        du, du_low = d_up.astype(BF16), pltpu.roll(d_up, slots, 0).astype(BF16)
        dg_ref[at, :] = dg
        du_ref[at, :] = du
        sa_ref[at, :] = pltpu.roll(scaled, slots, 0).astype(BF16)
        grad = dot(dg, gate_ref[:, :half], (1, 0)) + dot(du, up_ref[:, :half], (1, 0))
        grad += dot(dg_low, gate_ref[:, half:], (1, 0)) + dot(du_low, up_ref[:, half:], (1, 0))
        reply_ref[at, :half] = grad.astype(BF16)
        reply_ref[at, half:] = jnp.broadcast_to(part, (chunk, LANES)).astype(BF16)


def unpack_kernel(pick_ref, back_ref, tok_ref, prob_ref):
    tok_dev, features = tok_ref.shape
    half = features // 2
    total = dot(pick_ref[...], back_ref[...], (1, 0))
    tok_ref[:, :half] = total[:tok_dev, :half].astype(BF16)
    tok_ref[:, half:] = total[tok_dev:, :half].astype(BF16)
    part = total[:tok_dev, half:]
    here = lax.broadcasted_iota(jnp.int32, part.shape, 0)
    diagonal = here == lax.broadcasted_iota(jnp.int32, part.shape, 1)
    part = jnp.sum(jnp.where(diagonal, part, 0.0), axis=0, keepdims=True)
    prob_ref[...] = part[:, :tok_dev]


def call(kernel, in_specs, outs, *args):
    return pl.pallas_call(
        kernel,
        in_specs=in_specs,
        out_specs=[VMEM] * len(outs),
        out_shape=[jax.ShapeDtypeStruct(s, d) for s, d in outs],
        compiler_params=pltpu.CompilerParams(vmem_limit_bytes=48 << 20),
    )(*args)


def body(tokens, cotangent, routes, gate_prob, w_gate, w_up, w_down):
    groups = lax.axis_size("dp")
    experts = lax.axis_size("expert")
    _, tok_dev, features = tokens.shape
    hidden = w_gate.shape[1]
    half = features // 2
    slots = tok_dev // 4
    block = experts * 2 * slots
    rows = groups * block
    chunk = min(rows, 256)
    mine = lax.axis_index("dp").astype(jnp.int32).reshape(1)

    send, pick = call(
        lambda *refs: pack_kernel(slots, *refs),
        [SMEM, SMEM, VMEM, VMEM, VMEM, VMEM],
        [((rows, features + LANES), BF16), ((block, 2 * tok_dev), BF16)],
        mine, routes, routes, gate_prob, tokens[0], cotangent[0],
    )
    got = lax.all_to_all(send, AXES, split_axis=0, concat_axis=0, tiled=True)
    reply, d_gate, d_up, scaled_act = call(
        lambda *refs: expert_kernel(slots, chunk, *refs),
        [VMEM] * 4,
        [((rows, half + LANES), BF16)] + [((rows, hidden), BF16)] * 3,
        got, w_gate[0], w_up[0], w_down[0],
    )
    back = lax.all_to_all(reply, AXES, split_axis=0, concat_axis=0, tiled=True)
    grad_tokens, grad_prob = call(
        unpack_kernel,
        [VMEM] * 2,
        [((tok_dev, features), BF16), ((1, tok_dev), F32)],
        jnp.tile(pick.T, (1, groups)), back,
    )
    data = got[:, :features]
    weight_grads = [
        jnp.einsum("rh,rd->hd", left, data, preferred_element_type=F32).astype(BF16)[None]
        for left in (d_gate, d_up, scaled_act)
    ]
    return (grad_tokens[None], grad_prob, *weight_grads)


def solution(mesh):
    in_specs = (
        P("dp", "expert", None),
        P("dp", "expert", None),
        P(None, "expert"),
        P(None, "expert"),
        P("expert", "dp", None),
        P("expert", "dp", None),
        P("expert", "dp", None),
    )
    out_specs = (
        P("dp", "expert", None),
        P("dp", "expert"),
        P("expert", "dp", None),
        P("expert", "dp", None),
        P("expert", "dp", None),
    )
    return jax.shard_map(body, mesh=mesh, in_specs=in_specs, out_specs=out_specs, check_vma=False)
```

time: 70.3 us -> 68.9 us (0.980)
  Pallas kernels: 0 us -> 7.1 us
  matrix products: 11.7 us -> 5.22 us
  local copies, waits for them, and re-layouts: 6.83 us -> 4.64 us
  other arithmetic: 1.09 us -> 0 us
  waiting for transfers between devices: 10.7 us -> 11.5 us
    pallas_call x0 -> x3, Pallas kernels: none -> 7.1 us  [call(): pl.pallas_call(kernel, in_specs=in_specs, out_specs=[VMEM] * len(outs), o...]
    dot_general x10 -> x3, matrix products: 11.7 us -> 5.22 us  [body(): jnp.einsum('rh,rd->hd', left, data, preferred_element_type=F32).astype(BF16)]
    unnamed x12 -> x13, local copies, waits for them, and re-layouts: 1.03 us -> 4.54 us
    reshape x3 -> x0, local copies, waits for them, and re-layouts: 2.4 us -> none  [the longest x1 1.35 us: body(): got = got.reshape(rows, packed.shape[1])]
    broadcast_in_dim x5 -> x0, local copies, waits for them, and re-layouts: 1.34 us -> none  [the longest x2 0.85 us: body(): jnp.broadcast_to(prob[:, None], (tok_dev, LANES))]
    all_to_all x1, waiting for transfers between devices: 10.7 us -> 11.5 us  [body(): back = lax.all_to_all(reply, AXES, split_axis=0, concat_axis=0, tiled=True)]
where the time goes in v2:
time: 68.9 us; the launch traced here: 67.7 us
  blocking collectives  36 us (52%)
  waiting for transfers between devices  11.5 us (17%)
  Pallas kernels  7.1 us (10%)
  matrix products  5.22 us (8%)
  local copies, waits for them, and re-layouts  4.64 us (7%)
  starting transfers between devices  2.61 us (4%)
  between operations  0.69 us (1%)
    all_to_all x1, blocking collectives, body(): got = lax.all_to_all(send, AXES, split_axis=0, concat_axis=0, tiled=True)  36 us
    all_to_all x1, waiting for transfers between devices, body(): back = lax.all_to_all(reply, AXES, split_axis=0, concat_axis=0, tiled=True)  11.5 us
    pallas_call x3, Pallas kernels, call(): pl.pallas_call(kernel, in_specs=in_specs, out_specs=[VMEM] * len(outs), o...  7.1 us
    dot_general x3, matrix products, body(): jnp.einsum('rh,rd->hd', left, data, preferred_element_type=F32).astype(BF16)  5.22 us
    unnamed x13, local copies, waits for them, and re-layouts  4.54 us
    all_to_all x1, starting transfers between devices, body(): back = lax.all_to_all(reply, AXES, split_axis=0, concat_axis=0, tiled=True)  2.61 us
  transfers between devices with their start and end apart: 1, of which 1 were waited for; matrix products, arithmetic and copies ran while one was open for 8% of the time, Pallas kernels for 0%

profile of v2, /device:TPU:1, one launch (start us, length us, event | category | flops | bytes accessed | tf_op | source)
XLA Modules:
  0.0 67.7 jit_solution(13736478818050578242)
XLA Ops:
  0.6 0.0 copy-start
  0.6 0.0 copy-start.2
  0.7 0.9 %copy-done.2 = bf16[1,16,2048]{2,1,0:T(8,128)(2,1)S(1)} copy-done((bf16[1,16,2048]{2,1,0:T(8,128)(2,1)S(1)}, bf16[1,16,2048]{2,1,0:T(8,128)(2,1)}, u32[]{:S(2)}) %copy-start.2) | copy-done | bytes 65560
  1.6 0.0 copy-start.3
  1.6 0.8 %copy-done.3 = bf16[1,16,2048]{2,1,0:T(8,128)(2,1)S(1)} copy-done((bf16[1,16,2048]{2,1,0:T(8,128)(2,1)S(1)}, bf16[1,16,2048]{2,1,0:T(8,128)(2,1)}, u32[]{:S(2)}) %copy-start.3) | copy-done | bytes 65560
  2.4 0.0 copy-start.4
  2.4 0.7 copy-done.4
  3.1 0.0 copy-start.5
  3.1 0.7 copy-done.5
  3.8 1.0 %shard_map.110 = (bf16[256,2176]{1,0:T(8,128)(2,1)S(1)}, bf16[128,32]{1,0:T(8,128)(2,1)S(1)}) custom-call(s32[1]{0:T(128)} %bitcast.refs_0_, s32[2,16]{1,0:T(2,128)S(1)} %copy-done.4, s32[2,16]{1,0:T(2,128)S(1)} %copy-done.4, bf16[2,16]{1,0:T(2,128)(2,1)S(1)} %copy-done.5, bf16[16,2048]{1,0:T(8,128)(2,1)S(1)} %bitcast.34, bf16[16,2048]{1,0:T(8,128)(2,1)S(1)} %bitcast.35), custom_call_target="tpu_custom_call" | custom-call | tf_op jit(solution)/shard_map/pallas_call | solution.py:94
  4.8 36.0 %all_to_all.22 = bf16[32,8,2176]{2,1,0:T(8,128)(2,1)S(1)} all-to-all(bf16[32,8,2176]{2,1,0:T(8,128)(2,1)S(1)} %bitcast.32), channel_id=1, replica_groups=mesh['dp'=2,'expert'=16] {'dp','expert'}, dimensions={0} | all-to-all | bytes 2228224 | tf_op jit(solution)/shard_map/all_to_all | solution.py:121
  40.7 0.0 copy-done
  40.7 0.0 copy-start.1
  40.7 1.4 %copy-done.1 = bf16[1,384,2048]{2,1,0:T(8,128)(2,1)S(1)} copy-done((bf16[1,384,2048]{2,1,0:T(8,128)(2,1)S(1)}, bf16[1,384,2048]{2,1,0:T(8,128)(2,1)}, u32[]{:S(2)}) %copy-start.1) | copy-done | bytes 1572888
  42.2 5.3 %shard_map.111 = (bf16[256,1152]{1,0:T(8,128)(2,1)}, bf16[256,384]{1,0:T(8,128)(2,1)S(1)}, bf16[256,384]{1,0:T(8,128)(2,1)S(1)}, bf16[256,384]{1,0:T(8,128)(2,1)S(1)}) custom-call(bf16[256,2176]{1,0:T(8,128)(2,1)S(1)} %bitcast.25, bf16[384,2048]{1,0:T(8,128)(2,1)S(1)} %bitcast.30, bf16[384,2048]{1,0:T(8,128)(2,1)S(1)} %bitcast.31, bf16[384,2048]{1,0:T(8,128)(2,1)} %bitcast.37), custom_call_target="tpu_custom_call" | custom-call | tf_op jit(solution)/shard_map/pallas_call | solution.py:94
  47.4 2.6 %all-to-all-start.1 = ((bf16[32,8,1152]{2,1,0:T(8,128)(2,1)}), bf16[32,8,1152]{2,1,0:T(8,128)(2,1)S(1)}, u32[]{:S(2)}, u32[]{:S(2)}) async-start(bf16[32,8,1152]{2,1,0:T(8,128)(2,1)} %bitcast.9), calls=%async_computation.1 | async-start | bytes 1179648 | tf_op jit(solution)/shard_map/all_to_all | solution.py:128
  50.1 0.1 copy.12
  50.2 1.7 %fusion = bf16[1,384,2048]{2,1,0:T(8,128)(2,1)} fusion(bf16[256,384]{1,0:T(8,128)(2,1)S(1)} %get-tuple-element.18, bf16[256,2176]{1,0:T(8,128)(2,1)S(1)} %bitcast.26), kind=kOutput, calls=%fused_computation.3 | convolution fusion | flops 403439616 | bytes 2818048 | tf_op jit(solution)/shard_map/rh,rd->hd/dot_general | solution.py:137
  51.9 1.7 %fusion.1 = bf16[1,384,2048]{2,1,0:T(8,128)(2,1)} fusion(bf16[256,384]{1,0:T(8,128)(2,1)S(1)} %get-tuple-element.19, bf16[256,2176]{1,0:T(8,128)(2,1)S(1)} %bitcast.27), kind=kOutput, calls=%fused_computation.4 | convolution fusion | flops 403439616 | bytes 2818048 | tf_op jit(solution)/shard_map/rh,rd->hd/dot_general | solution.py:137
  53.7 1.7 %fusion.2 = bf16[1,384,2048]{2,1,0:T(8,128)(2,1)} fusion(bf16[256,384]{1,0:T(8,128)(2,1)S(1)} %get-tuple-element.20, bf16[256,2176]{1,0:T(8,128)(2,1)S(1)} %bitcast.28), kind=kOutput, calls=%fused_computation.5 | convolution fusion | flops 403439616 | bytes 2818048 | tf_op jit(solution)/shard_map/rh,rd->hd/dot_general | solution.py:137
  55.4 11.5 %all-to-all-done.1 = bf16[32,8,1152]{2,1,0:T(8,128)(2,1)S(1)} async-done(((bf16[32,8,1152]{2,1,0:T(8,128)(2,1)}), bf16[32,8,1152]{2,1,0:T(8,128)(2,1)S(1)}, u32[]{:S(2)}, u32[]{:S(2)}) %all-to-all-start.1) | async-done | bytes 589856 | tf_op jit(solution)/shard_map/all_to_all | solution.py:128
  66.9 0.8 %shard_map.112 = (bf16[16,2048]{1,0:T(8,128)(2,1)}, f32[1,16]{1,0:T(1,128)}) custom-call(bf16[32,256]{1,0:T(8,128)(2,1)S(1)} %bitcast.33, bf16[256,1152]{1,0:T(8,128)(2,1)S(1)} %bitcast.29), custom_call_target="tpu_custom_call" | custom-call | tf_op jit(solution)/shard_map/pallas_call | solution.py:94
  (2 shorter events, 0.0 us)
Async XLA Ops:
  0.6 40.1 %copy-start = (bf16[1,384,2048]{2,1,0:T(8,128)(2,1)S(1)}, bf16[1,384,2048]{2,1,0:T(8,128)(2,1)}, u32[]{:S(2)}) copy-start(bf16[1,384,2048]{2,1,0:T(8,128)(2,1)} %param.11) | copy-start | bytes 4718596
  0.6 1.0 %copy-start.2 = (bf16[1,16,2048]{2,1,0:T(8,128)(2,1)S(1)}, bf16[1,16,2048]{2,1,0:T(8,128)(2,1)}, u32[]{:S(2)}) copy-start(bf16[1,16,2048]{2,1,0:T(8,128)(2,1)} %param.7) | copy-start | bytes 196612
  1.6 0.8 %copy-start.3 = (bf16[1,16,2048]{2,1,0:T(8,128)(2,1)S(1)}, bf16[1,16,2048]{2,1,0:T(8,128)(2,1)}, u32[]{:S(2)}) copy-start(bf16[1,16,2048]{2,1,0:T(8,128)(2,1)} %param.8) | copy-start | bytes 196612
  2.4 0.7 %copy-start.4 = (s32[2,16]{1,0:T(2,128)S(1)}, s32[2,16]{1,0:T(2,128)}, u32[]{:S(2)}) copy-start(s32[2,16]{1,0:T(2,128)} %refs_2_.1) | copy-start | bytes 388
  3.1 0.7 copy-start.5
  40.7 1.4 %copy-start.1 = (bf16[1,384,2048]{2,1,0:T(8,128)(2,1)S(1)}, bf16[1,384,2048]{2,1,0:T(8,128)(2,1)}, u32[]{:S(2)}) copy-start(bf16[1,384,2048]{2,1,0:T(8,128)(2,1)} %param.12) | copy-start | bytes 4718596
  47.4 19.4 %all-to-all-start.1 = ((bf16[32,8,1152]{2,1,0:T(8,128)(2,1)}), bf16[32,8,1152]{2,1,0:T(8,128)(2,1)S(1)}, u32[]{:S(2)}, u32[]{:S(2)}) async-start(bf16[32,8,1152]{2,1,0:T(8,128)(2,1)} %bitcast.9), calls=%async_computation.1 | async-start | bytes 1179648 | tf_op jit(solution)/shard_map/all_to_all | solution.py:128

commit v3 on v2

--- a/solution.py
+++ b/solution.py
@@ -9,25 +9,34 @@
 LANES = 128
 F32, BF16 = jnp.float32, jnp.bfloat16
 VMEM = pl.BlockSpec(memory_space=pltpu.VMEM)
-SMEM = pl.BlockSpec(memory_space=pltpu.SMEM)
+HBM = pl.BlockSpec(memory_space=pltpu.HBM)
 
 
 def dot(a, b, dims):
     return lax.dot_general(a, b, ((dims[:1], dims[1:]), ((), ())), preferred_element_type=F32)
 
 
-def pack_kernel(slots, mine_ref, route_s, route_v, prob_v, tok_ref, cot_ref, send_ref, pick_ref):
-    mine = mine_ref[0]
+def pack_kernel(slots, *refs):
+    ins, (send_ref, pick_ref), kept, bufs, sems = refs[:7], refs[7:9], refs[9:12], refs[12:16], refs[16]
+    copies = [
+        pltpu.make_async_copy(a, b, sems.at[i]) for i, (a, b) in enumerate(zip(ins, bufs + kept))
+    ]
+    for copy in copies:
+        copy.start()
+    route_v, prob_v, tok_ref, cot_ref = bufs
     tok_dev, features = tok_ref.shape
     block = pick_ref.shape[0]
     groups = send_ref.shape[0] // block
+    mine = lax.axis_index("dp")
     own = lax.broadcasted_iota(jnp.int32, route_v.shape, 0) == mine
+    copies[0].wait()
     route = jnp.sum(jnp.where(own, route_v[...], 0), axis=0, keepdims=True)
+    copies[1].wait()
     prob = jnp.sum(jnp.where(own, prob_v[...].astype(F32), 0.0), axis=0, keepdims=True)
-    token = lax.broadcasted_iota(jnp.int32, (1, tok_dev), 1)
-    rank = jnp.zeros((1, tok_dev), jnp.int32)
-    for t in range(tok_dev):
-        rank += ((route == route_s[mine, t]) & (token > t)).astype(jnp.int32)
+    here = lax.broadcasted_iota(jnp.int32, (tok_dev, tok_dev), 0)
+    there = lax.broadcasted_iota(jnp.int32, (tok_dev, tok_dev), 1)
+    column = jnp.sum(jnp.where(here == there, route, 0), axis=1, keepdims=True)
+    rank = jnp.sum(((column == route) & (here < there)).astype(jnp.int32), axis=0, keepdims=True)
     target = route * (2 * slots) + rank
     row = lax.broadcasted_iota(jnp.int32, (block, tok_dev), 0)
     pick_x = (row == target).astype(F32)
@@ -36,12 +45,16 @@
     pick_x, pick_y = pick_x.astype(BF16), pick_y.astype(BF16)
     pick_ref[:, :tok_dev] = pick_x
     pick_ref[:, tok_dev:] = pick_y
+    copies[2].wait()
+    copies[3].wait()
     sent = dot(pick_x, tok_ref[...], (1, 0)) + dot(pick_y, cot_ref[...], (1, 0))
     sent = sent.astype(BF16)
     weight = jnp.broadcast_to(weight, (block, LANES)).astype(BF16)
     for g in range(groups):
         send_ref[g * block : (g + 1) * block, :features] = sent
         send_ref[g * block : (g + 1) * block, features:] = weight
+    for copy in copies[4:]:
+        copy.wait()
 
 
 def expert_kernel(slots, chunk, got_ref, gate_ref, up_ref, down_ref, reply_ref, dg_ref, du_ref, sa_ref):
@@ -90,12 +103,23 @@
     prob_ref[...] = part[:, :tok_dev]
 
 
-def call(kernel, in_specs, outs, *args):
+def near(shape, dtype=BF16):
+    small = shape[0] * shape[1] <= 1 << 20
+    return pltpu.VMEM(shape, dtype) if small else jax.ShapeDtypeStruct(shape, dtype)
+
+
+def fetched(array):
+    small = array.size <= 1 << 20
+    return pltpu.with_memory_space_constraint(array, pltpu.VMEM) if small else array
+
+
+def call(kernel, in_specs, outs, *args, scratch=()):
     return pl.pallas_call(
         kernel,
         in_specs=in_specs,
+        scratch_shapes=scratch,
         out_specs=[VMEM] * len(outs),
-        out_shape=[jax.ShapeDtypeStruct(s, d) for s, d in outs],
+        out_shape=outs,
         compiler_params=pltpu.CompilerParams(vmem_limit_bytes=48 << 20),
     )(*args)
 
@@ -110,26 +134,29 @@
     block = experts * 2 * slots
     rows = groups * block
     chunk = min(rows, 256)
-    mine = lax.axis_index("dp").astype(jnp.int32).reshape(1)
+    operands = (routes, gate_prob, tokens[0], cotangent[0], w_gate[0], w_up[0], w_down[0])
 
-    send, pick = call(
+    send, pick, *weights = call(
         lambda *refs: pack_kernel(slots, *refs),
-        [SMEM, SMEM, VMEM, VMEM, VMEM, VMEM],
-        [((rows, features + LANES), BF16), ((block, 2 * tok_dev), BF16)],
-        mine, routes, routes, gate_prob, tokens[0], cotangent[0],
+        [HBM] * 7,
+        [near((rows, features + LANES)), near((block, 2 * tok_dev))]
+        + [near((hidden, features))] * 3,
+        *[pltpu.with_memory_space_constraint(a, pltpu.HBM) for a in operands],
+        scratch=[pltpu.VMEM(a.shape, a.dtype) for a in operands[:4]]
+        + [pltpu.SemaphoreType.DMA((7,))],
     )
     got = lax.all_to_all(send, AXES, split_axis=0, concat_axis=0, tiled=True)
     reply, d_gate, d_up, scaled_act = call(
         lambda *refs: expert_kernel(slots, chunk, *refs),
         [VMEM] * 4,
-        [((rows, half + LANES), BF16)] + [((rows, hidden), BF16)] * 3,
-        got, w_gate[0], w_up[0], w_down[0],
+        [near((rows, half + LANES))] + [near((rows, hidden))] * 3,
+        *[fetched(a) for a in (got, *weights)],
     )
     back = lax.all_to_all(reply, AXES, split_axis=0, concat_axis=0, tiled=True)
     grad_tokens, grad_prob = call(
         unpack_kernel,
         [VMEM] * 2,
-        [((tok_dev, features), BF16), ((1, tok_dev), F32)],
+        [jax.ShapeDtypeStruct((tok_dev, features), BF16), jax.ShapeDtypeStruct((1, tok_dev), F32)],
         jnp.tile(pick.T, (1, groups)), back,
     )
     data = got[:, :features]

time: 68.9 us -> 64.3 us (0.933)
  local copies, waits for them, and re-layouts: 4.64 us -> 0.1 us
    unnamed x13 -> x1, local copies, waits for them, and re-layouts: 4.54 us -> 0.01 us
where the time goes in v3:
time: 64.3 us; the launch traced here: 63.3 us
  blocking collectives  36 us (56%)
  waiting for transfers between devices  11.5 us (18%)
  Pallas kernels  7.26 us (11%)
  matrix products  5.22 us (8%)
  starting transfers between devices  2.61 us (4%)
  between operations  0.67 us (1%)
    all_to_all x1, blocking collectives, body(): got = lax.all_to_all(send, AXES, split_axis=0, concat_axis=0, tiled=True)  36 us
    all_to_all x1, waiting for transfers between devices, body(): back = lax.all_to_all(reply, AXES, split_axis=0, concat_axis=0, tiled=True)  11.5 us
    pallas_call x3, Pallas kernels, call(): pl.pallas_call(kernel, in_specs=in_specs, scratch_shapes=scratch, out_spe...  7.26 us
    dot_general x3, matrix products, body(): jnp.einsum('rh,rd->hd', left, data, preferred_element_type=F32).astype(BF16)  5.22 us
    all_to_all x1, starting transfers between devices, body(): back = lax.all_to_all(reply, AXES, split_axis=0, concat_axis=0, tiled=True)  2.61 us
  transfers between devices with their start and end apart: 1, of which 1 were waited for; matrix products, arithmetic and copies ran while one was open for 8% of the time, Pallas kernels for 0%

profile of v3, /device:TPU:1, one launch (start us, length us, event | category | flops | bytes accessed | tf_op | source)
XLA Modules:
  0.0 63.3 jit_solution(17683942996235280671)
XLA Ops:
  0.6 2.5 %shard_map.110 = (bf16[256,2176]{1,0:T(8,128)(2,1)S(1)}, bf16[128,32]{1,0:T(8,128)(2,1)S(1)}, bf16[384,2048]{1,0:T(8,128)(2,1)S(1)}, bf16[384,2048]{1,0:T(8,128)(2,1)S(1)}, bf16[384,2048]{1,0:T(8,128)(2,1)S(1)}) custom-call(s32[2,16]{1,0:T(2,128)} %refs_0_.1, bf16[2,16]{1,0:T(2,128)(2,1)} %refs_1_.1, bf16[16,2048]{1,0:T(8,128)(2,1)} %bitcast.35, ...), custom_call_target="tpu_custom_call" | custom-call | tf_op jit(solution)/shard_map/pallas_call | solution.py:117
  3.2 36.0 %all_to_all.22 = bf16[32,8,2176]{2,1,0:T(8,128)(2,1)S(1)} all-to-all(bf16[32,8,2176]{2,1,0:T(8,128)(2,1)S(1)} %bitcast.29), channel_id=1, replica_groups=mesh['dp'=2,'expert'=16] {'dp','expert'}, dimensions={0} | all-to-all | bytes 2228224 | tf_op jit(solution)/shard_map/all_to_all | solution.py:148
  39.1 3.9 %shard_map.111 = (bf16[256,1152]{1,0:T(8,128)(2,1)}, bf16[256,384]{1,0:T(8,128)(2,1)S(1)}, bf16[256,384]{1,0:T(8,128)(2,1)S(1)}, bf16[256,384]{1,0:T(8,128)(2,1)S(1)}) custom-call(bf16[256,2176]{1,0:T(8,128)(2,1)S(1)} %bitcast.24, bf16[384,2048]{1,0:T(8,128)(2,1)S(1)} %get-tuple-element.18.refs_1_, bf16[384,2048]{1,0:T(8,128)(2,1)S(1)} %get-tuple-element.19.refs_2_, ...), custom_call_target="tpu_custom_call" | custom-call | tf_op jit(solution)/shard_map/pallas_call | solution.py:117
  43.0 2.6 %all-to-all-start.1 = ((bf16[32,8,1152]{2,1,0:T(8,128)(2,1)}), bf16[32,8,1152]{2,1,0:T(8,128)(2,1)S(1)}, u32[]{:S(2)}, u32[]{:S(2)}) async-start(bf16[32,8,1152]{2,1,0:T(8,128)(2,1)} %bitcast.8), calls=%async_computation.1 | async-start | bytes 1179648 | tf_op jit(solution)/shard_map/all_to_all | solution.py:155
  45.7 0.1 copy.12
  45.8 1.7 %fusion = bf16[1,384,2048]{2,1,0:T(8,128)(2,1)} fusion(bf16[256,384]{1,0:T(8,128)(2,1)S(1)} %get-tuple-element.24, bf16[256,2176]{1,0:T(8,128)(2,1)S(1)} %bitcast.25), kind=kOutput, calls=%fused_computation.3 | convolution fusion | flops 403439616 | bytes 2818048 | tf_op jit(solution)/shard_map/rh,rd->hd/dot_general | solution.py:164
  47.5 1.7 %fusion.1 = bf16[1,384,2048]{2,1,0:T(8,128)(2,1)} fusion(bf16[256,384]{1,0:T(8,128)(2,1)S(1)} %get-tuple-element.25, bf16[256,2176]{1,0:T(8,128)(2,1)S(1)} %bitcast.26), kind=kOutput, calls=%fused_computation.4 | convolution fusion | flops 403439616 | bytes 2818048 | tf_op jit(solution)/shard_map/rh,rd->hd/dot_general | solution.py:164
  49.3 1.7 %fusion.2 = bf16[1,384,2048]{2,1,0:T(8,128)(2,1)} fusion(bf16[256,384]{1,0:T(8,128)(2,1)S(1)} %get-tuple-element.26, bf16[256,2176]{1,0:T(8,128)(2,1)S(1)} %bitcast.27), kind=kOutput, calls=%fused_computation.5 | convolution fusion | flops 403439616 | bytes 2818048 | tf_op jit(solution)/shard_map/rh,rd->hd/dot_general | solution.py:164
  51.0 11.5 %all-to-all-done.1 = bf16[32,8,1152]{2,1,0:T(8,128)(2,1)S(1)} async-done(((bf16[32,8,1152]{2,1,0:T(8,128)(2,1)}), bf16[32,8,1152]{2,1,0:T(8,128)(2,1)S(1)}, u32[]{:S(2)}, u32[]{:S(2)}) %all-to-all-start.1) | async-done | bytes 589856 | tf_op jit(solution)/shard_map/all_to_all | solution.py:155
  62.5 0.8 %shard_map.112 = (bf16[16,2048]{1,0:T(8,128)(2,1)}, f32[1,16]{1,0:T(1,128)}) custom-call(bf16[32,256]{1,0:T(8,128)(2,1)S(1)} %bitcast.30, bf16[256,1152]{1,0:T(8,128)(2,1)S(1)} %bitcast.28), custom_call_target="tpu_custom_call" | custom-call | tf_op jit(solution)/shard_map/pallas_call | solution.py:117
  (2 shorter events, 0.0 us)
Async XLA Ops:
  43.0 19.4 %all-to-all-start.1 = ((bf16[32,8,1152]{2,1,0:T(8,128)(2,1)}), bf16[32,8,1152]{2,1,0:T(8,128)(2,1)S(1)}, u32[]{:S(2)}, u32[]{:S(2)}) async-start(bf16[32,8,1152]{2,1,0:T(8,128)(2,1)} %bitcast.8), calls=%async_computation.1 | async-start | bytes 1179648 | tf_op jit(solution)/shard_map/all_to_all | solution.py:155

commit v4 on v3

v4 whole, which is shorter than its diff:
```python
import math

import jax
import jax.numpy as jnp
from jax import lax
from jax.experimental import pallas as pl
from jax.experimental.pallas import tpu as pltpu
from jax.sharding import Mesh
from jax.sharding import PartitionSpec as P

HALF_AXES = ("dp", "low")
ALL_AXES = ("dp", "low", "top")
LANES = 128
F32, BF16 = jnp.float32, jnp.bfloat16
VMEM = pl.BlockSpec(memory_space=pltpu.VMEM)
HBM = pl.BlockSpec(memory_space=pltpu.HBM)


def dot(a, b, dims):
    return lax.dot_general(a, b, ((dims[:1], dims[1:]), ((), ())), preferred_element_type=F32)


def square(size):
    return tuple(lax.broadcasted_iota(jnp.int32, (size, size), axis) for axis in (0, 1))


def join_kernel(route_hbm, prob_hbm, tok_hbm, cot_hbm, out_ref, route_v, prob_v, sems):
    tok_dev, features = tok_hbm.shape
    small = [
        pltpu.make_async_copy(route_hbm, route_v, sems.at[0]),
        pltpu.make_async_copy(prob_hbm, prob_v, sems.at[1]),
    ]
    large = [
        pltpu.make_async_copy(tok_hbm, out_ref.at[pl.ds(0, tok_dev), pl.ds(0, features)], sems.at[2]),
        pltpu.make_async_copy(cot_hbm, out_ref.at[pl.ds(tok_dev, tok_dev), pl.ds(0, features)], sems.at[3]),
    ]
    for copy in small + large:
        copy.start()
    own = lax.broadcasted_iota(jnp.int32, route_v.shape, 0) == lax.axis_index("dp")
    here, there = square(tok_dev)
    for copy in small:
        copy.wait()
    route = jnp.sum(jnp.where(own, route_v[...].astype(F32), 0.0), axis=0, keepdims=True)
    prob = jnp.sum(jnp.where(own, prob_v[...].astype(F32), 0.0), axis=0, keepdims=True)
    route = jnp.sum(jnp.where(here == there, route, 0.0), axis=1, keepdims=True)
    prob = jnp.sum(jnp.where(here == there, prob, 0.0), axis=1, keepdims=True)
    lane = lax.broadcasted_iota(jnp.int32, (tok_dev, LANES), 1)
    tail = jnp.where(lane == 0, prob, jnp.where(lane == 1, route, 0.0))
    out_ref[:tok_dev, features:] = tail.astype(BF16)
    out_ref[tok_dev:, features:] = jnp.zeros((tok_dev, LANES), BF16)
    for copy in large:
        copy.wait()


def slots_of(rows_ref, tok_dev, features, half):
    here, there = square(tok_dev)
    column = rows_ref[:tok_dev, features + 1 : features + 2].astype(F32)
    row = jnp.sum(jnp.where(here == there, column, 0.0), axis=0, keepdims=True)
    rank = jnp.sum(jnp.where((column == row) & (here < there), 1.0, 0.0), axis=0, keepdims=True)
    route, rank = row.astype(jnp.int32), rank.astype(jnp.int32)
    upper = (route >= half).astype(jnp.int32)
    return upper, route - half * upper, rank


def pack_kernel(slots, own_ref, other_ref, gate_hbm, up_hbm, send_ref, pick_ref, gate_ref, up_ref, sems):
    copies = [
        pltpu.make_async_copy(gate_hbm, gate_ref, sems.at[0]),
        pltpu.make_async_copy(up_hbm, up_ref, sems.at[1]),
    ]
    for copy in copies:
        copy.start()
    tok_dev = own_ref.shape[0] // 2
    features = own_ref.shape[1] - LANES
    block = pick_ref.shape[0]
    groups = send_ref.shape[0] // block
    half = block // (4 * slots)
    top = lax.axis_index("top")
    place = lax.broadcasted_iota(jnp.int32, (block, tok_dev), 0)
    sent = jnp.zeros((block, features + LANES), F32)
    for rows_ref, origin in ((own_ref, top), (other_ref, 1 - top)):
        upper, low, rank = slots_of(rows_ref, tok_dev, features, half)
        target = low * (4 * slots) + origin * (2 * slots) + rank
        target = jnp.where(upper == top, target, -2 * slots)
        pick = [(place == target + shift).astype(F32) for shift in (0, slots)]
        sent += dot(jnp.concatenate(pick, axis=1).astype(BF16), rows_ref[...], (1, 0))
        if rows_ref is own_ref:
            target = (low * 2 + upper) * (2 * slots) + rank
            pick = [(place == target + shift).astype(F32) for shift in (0, slots)]
            pick_ref[...] = jnp.concatenate(pick, axis=1).astype(BF16)
    sent = sent.astype(BF16)
    for g in range(groups):
        send_ref[g * block : (g + 1) * block, :] = sent
    for copy in copies:
        copy.wait()


def expert_kernel(slots, chunk, got_ref, gate_ref, up_ref, down_hbm, *refs):
    reply_ref, dg_ref, du_ref, sa_ref, down_ref, sem = refs
    down_copy = pltpu.make_async_copy(down_hbm, down_ref, sem)
    down_copy.start()
    features = gate_ref.shape[1]
    half = features // 2

    @pl.loop(0, got_ref.shape[0] // chunk)
    def _(step):
        at = pl.ds(pl.multiple_of(step * chunk, chunk), chunk)
        data = got_ref[at, :features]
        weight = got_ref[at, features : features + 1].astype(F32)
        gate_pre = dot(data, gate_ref[...], (1, 1))
        up_pre = dot(data, up_ref[...], (1, 1))

        @pl.when(step == 0)
        def _():
            down_copy.wait()

        back_proj = dot(data, down_ref[...], (1, 1))
        back_proj = pltpu.roll(back_proj, chunk - slots, 0)
        sigma = jax.nn.sigmoid(gate_pre)
        swish = gate_pre * sigma
        slope = sigma * (1.0 + gate_pre * (1.0 - sigma))
        active = swish * up_pre
        scaled = weight * active
        d_active = weight * back_proj
        d_gate = d_active * up_pre * slope
        d_up = d_active * swish
        part = jnp.sum(active * back_proj, axis=1, keepdims=True)
        dg, dg_low = d_gate.astype(BF16), pltpu.roll(d_gate, slots, 0).astype(BF16)
        du, du_low = d_up.astype(BF16), pltpu.roll(d_up, slots, 0).astype(BF16)
        dg_ref[at, :] = dg
        du_ref[at, :] = du
        sa_ref[at, :] = pltpu.roll(scaled, slots, 0).astype(BF16)
        grad = dot(dg, gate_ref[:, :half], (1, 0)) + dot(du, up_ref[:, :half], (1, 0))
        grad += dot(dg_low, gate_ref[:, half:], (1, 0)) + dot(du_low, up_ref[:, half:], (1, 0))
        reply_ref[at, :half] = grad.astype(BF16)
        reply_ref[at, half:] = jnp.broadcast_to(part, (chunk, LANES)).astype(BF16)


def unpack_kernel(pick_ref, back_ref, tok_ref, prob_ref):
    tok_dev, features = tok_ref.shape
    half = features // 2
    total = dot(pick_ref[...], back_ref[...], (1, 0))
    tok_ref[:, :half] = total[:tok_dev, :half].astype(BF16)
    tok_ref[:, half:] = total[tok_dev:, :half].astype(BF16)
    part = total[:tok_dev, half:]
    here = lax.broadcasted_iota(jnp.int32, part.shape, 0)
    diagonal = here == lax.broadcasted_iota(jnp.int32, part.shape, 1)
    part = jnp.sum(jnp.where(diagonal, part, 0.0), axis=0, keepdims=True)
    prob_ref[...] = part[:, :tok_dev]


def near(shape, dtype=BF16):
    small = shape[0] * shape[1] <= 1 << 20
    return pltpu.VMEM(shape, dtype) if small else jax.ShapeDtypeStruct(shape, dtype)


def fetched(array):
    small = array.size <= 1 << 20
    return pltpu.with_memory_space_constraint(array, pltpu.VMEM) if small else array


def far(*arrays):
    return [pltpu.with_memory_space_constraint(a, pltpu.HBM) for a in arrays]


def call(kernel, in_specs, outs, *args, scratch=()):
    return pl.pallas_call(
        kernel,
        in_specs=in_specs,
        scratch_shapes=scratch,
        out_specs=[VMEM] * len(outs),
        out_shape=outs,
        compiler_params=pltpu.CompilerParams(vmem_limit_bytes=(16 if all(math.prod(o.shape) <= 1 << 20 for o in outs) else 48) << 20),
    )(*args)


def body(tokens, cotangent, routes, gate_prob, w_gate, w_up, w_down):
    groups = lax.axis_size("dp")
    experts = 2 * lax.axis_size("low")
    _, tok_dev, features = tokens.shape
    hidden = w_gate.shape[1]
    half = features // 2
    slots = tok_dev // 4
    block = experts * 2 * slots
    rows = groups * block
    chunk = min(rows, 256)
    width = features + LANES

    (own,) = call(
        join_kernel,
        [HBM] * 4,
        [near((2 * tok_dev, width))],
        *far(routes, gate_prob, tokens[0], cotangent[0]),
        scratch=[
            pltpu.VMEM(routes.shape, routes.dtype),
            pltpu.VMEM(gate_prob.shape, gate_prob.dtype),
            pltpu.SemaphoreType.DMA((4,)),
        ],
    )
    other = lax.ppermute(own, "top", [(0, 1), (1, 0)])
    send, pick, gate_near, up_near = call(
        lambda *refs: pack_kernel(slots, *refs),
        [VMEM] * 2 + [HBM] * 2,
        [near((rows, width)), near((block, 2 * tok_dev))] + [near((hidden, features))] * 2,
        fetched(own), fetched(other), *far(w_gate[0], w_up[0]),
        scratch=[pltpu.SemaphoreType.DMA((2,))],
    )
    got = lax.all_to_all(send, HALF_AXES, split_axis=0, concat_axis=0, tiled=True)
    reply, d_gate, d_up, scaled_act = call(
        lambda *refs: expert_kernel(slots, chunk, *refs),
        [VMEM] * 3 + [HBM],
        [near((rows, half + LANES))] + [near((rows, hidden))] * 3,
        fetched(got), fetched(gate_near), fetched(up_near), *far(w_down[0]),
        scratch=[pltpu.VMEM((hidden, features), BF16), pltpu.SemaphoreType.DMA(())],
    )
    back = lax.all_to_all(reply, ALL_AXES, split_axis=0, concat_axis=0, tiled=True)
    grad_tokens, grad_prob = call(
        unpack_kernel,
        [VMEM] * 2,
        [jax.ShapeDtypeStruct((tok_dev, features), BF16), jax.ShapeDtypeStruct((1, tok_dev), F32)],
        jnp.tile(pick.T, (1, groups)), back,
    )
    data = got[:, :features]
    weight_grads = [
        jnp.einsum("rh,rd->hd", left, data, preferred_element_type=F32).astype(BF16)[None]
        for left in (d_gate, d_up, scaled_act)
    ]
    return (grad_tokens[None], grad_prob, *weight_grads)


def solution(mesh):
    groups, experts = (mesh.shape[axis] for axis in ("dp", "expert"))
    split = Mesh(mesh.devices.reshape(groups, 2, experts // 2), ("dp", "top", "low"))
    expert = ("top", "low")
    in_specs = (
        P("dp", expert, None),
        P("dp", expert, None),
        P(None, expert),
        P(None, expert),
        P(expert, "dp", None),
        P(expert, "dp", None),
        P(expert, "dp", None),
    )
    out_specs = (
        P("dp", expert, None),
        P("dp", expert),
        P(expert, "dp", None),
        P(expert, "dp", None),
        P(expert, "dp", None),
    )
    return jax.shard_map(body, mesh=split, in_specs=in_specs, out_specs=out_specs, check_vma=False)
```

time: 64.3 us -> 62.6 us (0.974); the launches traced: 63.3 us -> 62.3 us
  blocking collectives: 36 us -> 21.1 us
  waiting for transfers between devices: 11.5 us -> 18.5 us
  starting transfers between devices: 2.61 us -> 7.45 us
  Pallas kernels: 7.26 us -> 9.29 us
    all_to_all x1, blocking collectives: 36 us -> 21.1 us  [body(): lax.all_to_all(send, HALF_AXES, split_axis=0, concat_axis=0, tiled=True)]
    ppermute x0 -> x1, waiting for transfers between devices: none -> 6.38 us  [body(): other = lax.ppermute(own, 'top', [(0, 1), (1, 0)])]
    ppermute x0 -> x1, starting transfers between devices: none -> 3.2 us  [body(): other = lax.ppermute(own, 'top', [(0, 1), (1, 0)])]
    pallas_call x3 -> x4, Pallas kernels: 7.26 us -> 9.29 us  [call(): pl.pallas_call(kernel, in_specs=in_specs, scratch_shapes=scratch, out_spe...]
    all_to_all x1, starting transfers between devices: 2.61 us -> 4.25 us  [body(): lax.all_to_all(reply, ALL_AXES, split_axis=0, concat_axis=0, tiled=True)]
  transfers between devices with their start and end apart: 1 -> 2, of which waited for: 1 -> 2; matrix products, arithmetic and copies ran while one was open for 8% -> 9% of each run, Pallas kernels for 0% -> 0%
where the time goes in v4:
time: 62.6 us; the launch traced here: 62.3 us
  blocking collectives  21.1 us (34%)
  waiting for transfers between devices  18.5 us (30%)
  Pallas kernels  9.29 us (15%)
  starting transfers between devices  7.45 us (12%)
  matrix products  5.22 us (8%)
  between operations  0.68 us (1%)
    all_to_all x1, blocking collectives, body(): lax.all_to_all(send, HALF_AXES, split_axis=0, concat_axis=0, tiled=True)  21.1 us
    all_to_all x1, waiting for transfers between devices, body(): lax.all_to_all(reply, ALL_AXES, split_axis=0, concat_axis=0, tiled=True)  12.1 us
    pallas_call x4, Pallas kernels, call(): pl.pallas_call(kernel, in_specs=in_specs, scratch_shapes=scratch, out_spe...  9.29 us
    ppermute x1, waiting for transfers between devices, body(): other = lax.ppermute(own, 'top', [(0, 1), (1, 0)])  6.38 us
    dot_general x3, matrix products, body(): jnp.einsum('rh,rd->hd', left, data, preferred_element_type=F32).astype(BF16)  5.22 us
    all_to_all x1, starting transfers between devices, body(): lax.all_to_all(reply, ALL_AXES, split_axis=0, concat_axis=0, tiled=True)  4.25 us
    ppermute x1, starting transfers between devices, body(): other = lax.ppermute(own, 'top', [(0, 1), (1, 0)])  3.2 us
  transfers between devices with their start and end apart: 2, of which 2 were waited for; matrix products, arithmetic and copies ran while one was open for 9% of the time, Pallas kernels for 0%

profile of v4, /device:TPU:1, one launch (start us, length us, event | category | flops | bytes accessed | tf_op | source)
XLA Modules:
  0.0 62.3 jit_solution(192060204331231068)
XLA Ops:
  0.6 0.9 %shard_map.110.refs_0_ = bf16[32,2176]{1,0:T(8,128)(2,1)S(1)} custom-call(s32[2,16]{1,0:T(2,128)} %route_hbm.1, bf16[2,16]{1,0:T(2,128)(2,1)} %prob_hbm.1, bf16[16,2048]{1,0:T(8,128)(2,1)} %bitcast.36, bf16[16,2048]{1,0:T(8,128)(2,1)} %bitcast.37), custom_call_target="tpu_custom_call" | custom-call | tf_op jit(solution)/shard_map/pallas_call | solution.py:166
  1.6 3.2 %collective-permute-start = (bf16[32,2176]{1,0:T(8,128)(2,1)S(1)}, bf16[32,2176]{1,0:T(8,128)(2,1)S(1)}, u32[]{:S(2)}, u32[]{:S(2)}) collective-permute-start(bf16[32,2176]{1,0:T(8,128)(2,1)S(1)} %shard_map.110.refs_0_), channel_id=1, source_target_pairs={{0,8},{8,0},{1,9},{9,1},{2,10},{10,2},{3,11},{11,3},{4,12},{12,4},... | collective-permute-start | bytes 417800 | tf_op jit(solution)/shard_map/ppermute | solution.py:199
  4.8 6.4 %collective-permute-done.refs_1_ = bf16[32,2176]{1,0:T(8,128)(2,1)S(1)} collective-permute-done((bf16[32,2176]{1,0:T(8,128)(2,1)S(1)}, bf16[32,2176]{1,0:T(8,128)(2,1)S(1)}, u32[]{:S(2)}, u32[]{:S(2)}) %collective-permute-start) | collective-permute-done | bytes 139296 | tf_op jit(solution)/shard_map/ppermute | solution.py:199
  11.2 2.1 %shard_map.111 = (bf16[256,2176]{1,0:T(8,128)(2,1)S(1)}, bf16[128,32]{1,0:T(8,128)(2,1)S(1)}, bf16[384,2048]{1,0:T(8,128)(2,1)S(1)}, bf16[384,2048]{1,0:T(8,128)(2,1)S(1)}) custom-call(bf16[32,2176]{1,0:T(8,128)(2,1)S(1)} %shard_map.110.refs_0_, bf16[32,2176]{1,0:T(8,128)(2,1)S(1)} %collective-permute-done.refs_1_, bf16[384,2048]{1,0:T(8,128)(2,1)} %bitcast.32, ...), custom_call_target="tpu_custom_call" | custom-call | tf_op jit(solution)/shard_map/pallas_call | solution.py:166
  13.3 21.1 %all_to_all.22 = bf16[16,16,2176]{2,1,0:T(8,128)(2,1)S(1)} all-to-all(bf16[16,16,2176]{2,1,0:T(8,128)(2,1)S(1)} %bitcast.29), channel_id=1, replica_groups=mesh['dp'=2,'top'=2,'low'=8] {'dp','low'}, dimensions={0} | all-to-all | bytes 2228224 | tf_op jit(solution)/shard_map/all_to_all | solution.py:207
  34.4 5.4 %shard_map.112 = (bf16[256,1152]{1,0:T(8,128)(2,1)}, bf16[256,384]{1,0:T(8,128)(2,1)S(1)}, bf16[256,384]{1,0:T(8,128)(2,1)S(1)}, bf16[256,384]{1,0:T(8,128)(2,1)S(1)}) custom-call(bf16[256,2176]{1,0:T(8,128)(2,1)S(1)} %bitcast.24, bf16[384,2048]{1,0:T(8,128)(2,1)S(1)} %get-tuple-element.17.refs_1_, bf16[384,2048]{1,0:T(8,128)(2,1)S(1)} %get-tuple-element.18.refs_2_, ...), custom_call_target="tpu_custom_call" | custom-call | tf_op jit(solution)/shard_map/pallas_call | solution.py:166
  39.8 4.3 %all-to-all-start.1 = ((bf16[32,8,1152]{2,1,0:T(8,128)(2,1)}), bf16[32,8,1152]{2,1,0:T(8,128)(2,1)S(1)}, u32[]{:S(2)}, u32[]{:S(2)}) async-start(bf16[32,8,1152]{2,1,0:T(8,128)(2,1)} %bitcast.8), calls=%async_computation.1 | async-start | bytes 1179648 | tf_op jit(solution)/shard_map/all_to_all | solution.py:215
  44.1 0.1 copy.12
  44.2 1.7 %fusion = bf16[1,384,2048]{2,1,0:T(8,128)(2,1)} fusion(bf16[256,384]{1,0:T(8,128)(2,1)S(1)} %get-tuple-element.22, bf16[256,2176]{1,0:T(8,128)(2,1)S(1)} %bitcast.25), kind=kOutput, calls=%fused_computation.3 | convolution fusion | flops 403439616 | bytes 2818048 | tf_op jit(solution)/shard_map/rh,rd->hd/dot_general | solution.py:224
  46.0 1.7 %fusion.1 = bf16[1,384,2048]{2,1,0:T(8,128)(2,1)} fusion(bf16[256,384]{1,0:T(8,128)(2,1)S(1)} %get-tuple-element.23, bf16[256,2176]{1,0:T(8,128)(2,1)S(1)} %bitcast.26), kind=kOutput, calls=%fused_computation.4 | convolution fusion | flops 403439616 | bytes 2818048 | tf_op jit(solution)/shard_map/rh,rd->hd/dot_general | solution.py:224
  47.7 1.7 %fusion.2 = bf16[1,384,2048]{2,1,0:T(8,128)(2,1)} fusion(bf16[256,384]{1,0:T(8,128)(2,1)S(1)} %get-tuple-element.24, bf16[256,2176]{1,0:T(8,128)(2,1)S(1)} %bitcast.27), kind=kOutput, calls=%fused_computation.5 | convolution fusion | flops 403439616 | bytes 2818048 | tf_op jit(solution)/shard_map/rh,rd->hd/dot_general | solution.py:224
  49.4 12.1 %all-to-all-done.1 = bf16[32,8,1152]{2,1,0:T(8,128)(2,1)S(1)} async-done(((bf16[32,8,1152]{2,1,0:T(8,128)(2,1)}), bf16[32,8,1152]{2,1,0:T(8,128)(2,1)S(1)}, u32[]{:S(2)}, u32[]{:S(2)}) %all-to-all-start.1) | async-done | bytes 589856 | tf_op jit(solution)/shard_map/all_to_all | solution.py:215
  61.5 0.8 %shard_map.113 = (bf16[16,2048]{1,0:T(8,128)(2,1)}, f32[1,16]{1,0:T(1,128)}) custom-call(bf16[32,256]{1,0:T(8,128)(2,1)S(1)} %bitcast.30, bf16[256,1152]{1,0:T(8,128)(2,1)S(1)} %bitcast.28), custom_call_target="tpu_custom_call" | custom-call | tf_op jit(solution)/shard_map/pallas_call | solution.py:166
  (2 shorter events, 0.0 us)
Async XLA Ops:
  1.6 9.6 %collective-permute-start = (bf16[32,2176]{1,0:T(8,128)(2,1)S(1)}, bf16[32,2176]{1,0:T(8,128)(2,1)S(1)}, u32[]{:S(2)}, u32[]{:S(2)}) collective-permute-start(bf16[32,2176]{1,0:T(8,128)(2,1)S(1)} %shard_map.110.refs_0_), channel_id=1, source_target_pairs={{0,8},{8,0},{1,9},{9,1},{2,10},{10,2},{3,11},{11,3},{4,12},{12,4},... | collective-permute-start | bytes 417800 | tf_op jit(solution)/shard_map/ppermute | solution.py:199
  39.8 21.7 %all-to-all-start.1 = ((bf16[32,8,1152]{2,1,0:T(8,128)(2,1)}), bf16[32,8,1152]{2,1,0:T(8,128)(2,1)S(1)}, u32[]{:S(2)}, u32[]{:S(2)}) async-start(bf16[32,8,1152]{2,1,0:T(8,128)(2,1)} %bitcast.8), calls=%async_computation.1 | async-start | bytes 1179648 | tf_op jit(solution)/shard_map/all_to_all | solution.py:215

commit v5 on v4

--- a/solution.py
+++ b/solution.py
@@ -62,13 +62,17 @@
     return upper, route - half * upper, rank
 
 
-def pack_kernel(slots, own_ref, other_ref, gate_hbm, up_hbm, send_ref, pick_ref, gate_ref, up_ref, sems):
-    copies = [
-        pltpu.make_async_copy(gate_hbm, gate_ref, sems.at[0]),
-        pltpu.make_async_copy(up_hbm, up_ref, sems.at[1]),
-    ]
+def load_kernel(*refs):
+    ins, outs, sems = refs[:3], refs[3:6], refs[6]
+    copies = [pltpu.make_async_copy(a, b, sems.at[i]) for i, (a, b) in enumerate(zip(ins, outs))]
     for copy in copies:
         copy.start()
+    for copy in copies:
+        copy.wait()
+
+
+def pack_kernel(slots, own_ref, other_ref, w0, w1, w2, send_ref, pick_ref):
+    del w0, w1, w2
     tok_dev = own_ref.shape[0] // 2
     features = own_ref.shape[1] - LANES
     block = pick_ref.shape[0]
@@ -90,14 +94,10 @@
     sent = sent.astype(BF16)
     for g in range(groups):
         send_ref[g * block : (g + 1) * block, :] = sent
-    for copy in copies:
-        copy.wait()
-
-
-def expert_kernel(slots, chunk, got_ref, gate_ref, up_ref, down_hbm, *refs):
-    reply_ref, dg_ref, du_ref, sa_ref, down_ref, sem = refs
-    down_copy = pltpu.make_async_copy(down_hbm, down_ref, sem)
-    down_copy.start()
+
+
+def expert_kernel(slots, chunk, got_ref, gate_ref, up_ref, down_ref, *refs):
+    reply_ref, dg_ref, du_ref, sa_ref = refs
     features = gate_ref.shape[1]
     half = features // 2
 
@@ -108,11 +108,6 @@
         weight = got_ref[at, features : features + 1].astype(F32)
         gate_pre = dot(data, gate_ref[...], (1, 1))
         up_pre = dot(data, up_ref[...], (1, 1))
-
-        @pl.when(step == 0)
-        def _():
-            down_copy.wait()
-
         back_proj = dot(data, down_ref[...], (1, 1))
         back_proj = pltpu.roll(back_proj, chunk - slots, 0)
         sigma = jax.nn.sigmoid(gate_pre)
@@ -162,13 +157,14 @@
     return [pltpu.with_memory_space_constraint(a, pltpu.HBM) for a in arrays]
 
 
-def call(kernel, in_specs, outs, *args, scratch=()):
+def call(kernel, in_specs, outs, *args, scratch=(), cost=None):
     return pl.pallas_call(
         kernel,
         in_specs=in_specs,
         scratch_shapes=scratch,
         out_specs=[VMEM] * len(outs),
         out_shape=outs,
+        cost_estimate=cost,
         compiler_params=pltpu.CompilerParams(vmem_limit_bytes=(16 if all(math.prod(o.shape) <= 1 << 20 for o in outs) else 48) << 20),
     )(*args)
 
@@ -197,20 +193,27 @@
         ],
     )
     other = lax.ppermute(own, "top", [(0, 1), (1, 0)])
-    send, pick, gate_near, up_near = call(
+    weights = call(
+        load_kernel,
+        [HBM] * 3,
+        [near((hidden, features))] * 3,
+        *far(w_gate[0], w_up[0], w_down[0]),
+        scratch=[pltpu.SemaphoreType.DMA((3,))],
+        cost=pl.CostEstimate(flops=0, transcendentals=0, bytes_accessed=12 * hidden * features),
+    )
+    weights = [fetched(a) for a in weights]
+    send, pick = call(
         lambda *refs: pack_kernel(slots, *refs),
-        [VMEM] * 2 + [HBM] * 2,
-        [near((rows, width)), near((block, 2 * tok_dev))] + [near((hidden, features))] * 2,
-        fetched(own), fetched(other), *far(w_gate[0], w_up[0]),
-        scratch=[pltpu.SemaphoreType.DMA((2,))],
+        [VMEM] * 5,
+        [near((rows, width)), near((block, 2 * tok_dev))],
+        fetched(own), fetched(other), *weights,
     )
     got = lax.all_to_all(send, HALF_AXES, split_axis=0, concat_axis=0, tiled=True)
     reply, d_gate, d_up, scaled_act = call(
         lambda *refs: expert_kernel(slots, chunk, *refs),
-        [VMEM] * 3 + [HBM],
+        [VMEM] * 4,
         [near((rows, half + LANES))] + [near((rows, hidden))] * 3,
-        fetched(got), fetched(gate_near), fetched(up_near), *far(w_down[0]),
-        scratch=[pltpu.VMEM((hidden, features), BF16), pltpu.SemaphoreType.DMA(())],
+        fetched(got), *weights,
     )
     back = lax.all_to_all(reply, ALL_AXES, split_axis=0, concat_axis=0, tiled=True)
     grad_tokens, grad_prob = call(

time: 62.6 us -> 59.6 us (0.952)
  waiting for transfers between devices: 18.5 us -> 16.1 us
  Pallas kernels: 9.29 us -> 8.64 us
    ppermute x1, waiting for transfers between devices: 6.38 us -> 4 us  [body(): other = lax.ppermute(own, 'top', [(0, 1), (1, 0)])]
    pallas_call x4 -> x5, Pallas kernels: 9.29 us -> 8.64 us  [call(): pl.pallas_call(kernel, in_specs=in_specs, scratch_shapes=scratch, out_spe...]
  transfers between devices with their start and end apart: 2 -> 2, of which waited for: 2 -> 2; matrix products, arithmetic and copies ran while one was open for 9% -> 9% of each run, Pallas kernels for 0% -> 4%
where the time goes in v5:
time: 59.6 us; the launch traced here: 59.3 us
  blocking collectives  21.1 us (35%)
  waiting for transfers between devices  16.1 us (27%)
  Pallas kernels  8.64 us (14%)
  starting transfers between devices  7.44 us (12%)
  matrix products  5.22 us (9%)
  between operations  0.68 us (1%)
    all_to_all x1, blocking collectives, body(): lax.all_to_all(send, HALF_AXES, split_axis=0, concat_axis=0, tiled=True)  21.1 us
    all_to_all x1, waiting for transfers between devices, body(): lax.all_to_all(reply, ALL_AXES, split_axis=0, concat_axis=0, tiled=True)  12.1 us
    pallas_call x5, Pallas kernels, call(): pl.pallas_call(kernel, in_specs=in_specs, scratch_shapes=scratch, out_spe...  8.64 us
    dot_general x3, matrix products, body(): jnp.einsum('rh,rd->hd', left, data, preferred_element_type=F32).astype(BF16)  5.22 us
    all_to_all x1, starting transfers between devices, body(): lax.all_to_all(reply, ALL_AXES, split_axis=0, concat_axis=0, tiled=True)  4.23 us
    ppermute x1, waiting for transfers between devices, body(): other = lax.ppermute(own, 'top', [(0, 1), (1, 0)])  4 us
    ppermute x1, starting transfers between devices, body(): other = lax.ppermute(own, 'top', [(0, 1), (1, 0)])  3.2 us
  transfers between devices with their start and end apart: 2, of which 2 were waited for; matrix products, arithmetic and copies ran while one was open for 9% of the time, Pallas kernels for 4%

profile of v5, /device:TPU:1, one launch (start us, length us, event | category | flops | bytes accessed | tf_op | source)
XLA Modules:
  0.0 59.3 jit_solution(4072381708745206450)
XLA Ops:
  0.6 0.9 %shard_map.110.refs_0_ = bf16[32,2176]{1,0:T(8,128)(2,1)S(1)} custom-call(s32[2,16]{1,0:T(2,128)} %route_hbm.1, bf16[2,16]{1,0:T(2,128)(2,1)} %prob_hbm.1, bf16[16,2048]{1,0:T(8,128)(2,1)} %bitcast.36, bf16[16,2048]{1,0:T(8,128)(2,1)} %bitcast.37), custom_call_target="tpu_custom_call" | custom-call | tf_op jit(solution)/shard_map/pallas_call | solution.py:161
  1.6 3.2 %collective-permute-start = (bf16[32,2176]{1,0:T(8,128)(2,1)S(1)}, bf16[32,2176]{1,0:T(8,128)(2,1)S(1)}, u32[]{:S(2)}, u32[]{:S(2)}) collective-permute-start(bf16[32,2176]{1,0:T(8,128)(2,1)S(1)} %shard_map.110.refs_0_), channel_id=1, source_target_pairs={{0,8},{8,0},{1,9},{9,1},{2,10},{10,2},{3,11},{11,3},{4,12},{12,4},... | collective-permute-start | bytes 417800 | tf_op jit(solution)/shard_map/ppermute | solution.py:195
  4.8 2.4 %shard_map.111 = (bf16[384,2048]{1,0:T(8,128)(2,1)S(1)}, bf16[384,2048]{1,0:T(8,128)(2,1)S(1)}, bf16[384,2048]{1,0:T(8,128)(2,1)S(1)}) custom-call(bf16[384,2048]{1,0:T(8,128)(2,1)} %bitcast.32, bf16[384,2048]{1,0:T(8,128)(2,1)} %bitcast.33, bf16[384,2048]{1,0:T(8,128)(2,1)} %bitcast.34), custom_call_target="tpu_custom_call" | custom-call | bytes 9437184 | tf_op jit(solution)/shard_map/pallas_call | solution.py:161
  7.2 4.0 %collective-permute-done.refs_1_ = bf16[32,2176]{1,0:T(8,128)(2,1)S(1)} collective-permute-done((bf16[32,2176]{1,0:T(8,128)(2,1)S(1)}, bf16[32,2176]{1,0:T(8,128)(2,1)S(1)}, u32[]{:S(2)}, u32[]{:S(2)}) %collective-permute-start) | collective-permute-done | bytes 139296 | tf_op jit(solution)/shard_map/ppermute | solution.py:195
  11.2 0.6 shard_map.112
  11.8 21.1 %all_to_all.22 = bf16[16,16,2176]{2,1,0:T(8,128)(2,1)S(1)} all-to-all(bf16[16,16,2176]{2,1,0:T(8,128)(2,1)S(1)} %bitcast.29), channel_id=1, replica_groups=mesh['dp'=2,'top'=2,'low'=8] {'dp','low'}, dimensions={0} | all-to-all | bytes 2228224 | tf_op jit(solution)/shard_map/all_to_all | solution.py:211
  32.9 3.9 %shard_map.113 = (bf16[256,1152]{1,0:T(8,128)(2,1)}, bf16[256,384]{1,0:T(8,128)(2,1)S(1)}, bf16[256,384]{1,0:T(8,128)(2,1)S(1)}, bf16[256,384]{1,0:T(8,128)(2,1)S(1)}) custom-call(bf16[256,2176]{1,0:T(8,128)(2,1)S(1)} %bitcast.24, bf16[384,2048]{1,0:T(8,128)(2,1)S(1)} %get-tuple-element.16.refs_2_.refs_1_, ...), custom_call_target="tpu_custom_call" | custom-call | tf_op jit(solution)/shard_map/pallas_call | solution.py:161
  36.8 4.2 %all-to-all-start.1 = ((bf16[32,8,1152]{2,1,0:T(8,128)(2,1)}), bf16[32,8,1152]{2,1,0:T(8,128)(2,1)S(1)}, u32[]{:S(2)}, u32[]{:S(2)}) async-start(bf16[32,8,1152]{2,1,0:T(8,128)(2,1)} %bitcast.8), calls=%async_computation.1 | async-start | bytes 1179648 | tf_op jit(solution)/shard_map/all_to_all | solution.py:218
  41.0 0.1 copy.12
  41.2 1.7 %fusion = bf16[1,384,2048]{2,1,0:T(8,128)(2,1)} fusion(bf16[256,384]{1,0:T(8,128)(2,1)S(1)} %get-tuple-element.24, bf16[256,2176]{1,0:T(8,128)(2,1)S(1)} %bitcast.25), kind=kOutput, calls=%fused_computation.3 | convolution fusion | flops 403439616 | bytes 2818048 | tf_op jit(solution)/shard_map/rh,rd->hd/dot_general | solution.py:227
  42.9 1.7 %fusion.1 = bf16[1,384,2048]{2,1,0:T(8,128)(2,1)} fusion(bf16[256,384]{1,0:T(8,128)(2,1)S(1)} %get-tuple-element.25, bf16[256,2176]{1,0:T(8,128)(2,1)S(1)} %bitcast.26), kind=kOutput, calls=%fused_computation.4 | convolution fusion | flops 403439616 | bytes 2818048 | tf_op jit(solution)/shard_map/rh,rd->hd/dot_general | solution.py:227
  44.6 1.7 %fusion.2 = bf16[1,384,2048]{2,1,0:T(8,128)(2,1)} fusion(bf16[256,384]{1,0:T(8,128)(2,1)S(1)} %get-tuple-element.26, bf16[256,2176]{1,0:T(8,128)(2,1)S(1)} %bitcast.27), kind=kOutput, calls=%fused_computation.5 | convolution fusion | flops 403439616 | bytes 2818048 | tf_op jit(solution)/shard_map/rh,rd->hd/dot_general | solution.py:227
  46.4 12.1 %all-to-all-done.1 = bf16[32,8,1152]{2,1,0:T(8,128)(2,1)S(1)} async-done(((bf16[32,8,1152]{2,1,0:T(8,128)(2,1)}), bf16[32,8,1152]{2,1,0:T(8,128)(2,1)S(1)}, u32[]{:S(2)}, u32[]{:S(2)}) %all-to-all-start.1) | async-done | bytes 589856 | tf_op jit(solution)/shard_map/all_to_all | solution.py:218
  58.5 0.8 %shard_map.114 = (bf16[16,2048]{1,0:T(8,128)(2,1)}, f32[1,16]{1,0:T(1,128)}) custom-call(bf16[32,256]{1,0:T(8,128)(2,1)S(1)} %bitcast.30, bf16[256,1152]{1,0:T(8,128)(2,1)S(1)} %bitcast.28), custom_call_target="tpu_custom_call" | custom-call | tf_op jit(solution)/shard_map/pallas_call | solution.py:161
  (2 shorter events, 0.0 us)
Async XLA Ops:
  1.6 9.6 %collective-permute-start = (bf16[32,2176]{1,0:T(8,128)(2,1)S(1)}, bf16[32,2176]{1,0:T(8,128)(2,1)S(1)}, u32[]{:S(2)}, u32[]{:S(2)}) collective-permute-start(bf16[32,2176]{1,0:T(8,128)(2,1)S(1)} %shard_map.110.refs_0_), channel_id=1, source_target_pairs={{0,8},{8,0},{1,9},{9,1},{2,10},{10,2},{3,11},{11,3},{4,12},{12,4},... | collective-permute-start | bytes 417800 | tf_op jit(solution)/shard_map/ppermute | solution.py:195
  36.8 21.6 %all-to-all-start.1 = ((bf16[32,8,1152]{2,1,0:T(8,128)(2,1)}), bf16[32,8,1152]{2,1,0:T(8,128)(2,1)S(1)}, u32[]{:S(2)}, u32[]{:S(2)}) async-start(bf16[32,8,1152]{2,1,0:T(8,128)(2,1)} %bitcast.8), calls=%async_computation.1 | async-start | bytes 1179648 | tf_op jit(solution)/shard_map/all_to_all | solution.py:218

commit v6 on v5

v6 whole, which is shorter than its diff:
```python
import math

import jax
import jax.numpy as jnp
from jax import lax
from jax.experimental import pallas as pl
from jax.experimental.pallas import tpu as pltpu
from jax.sharding import Mesh
from jax.sharding import PartitionSpec as P

HALF_AXES = ("dp", "low")
SWAP = [(0, 1), (1, 0)]
LANES = 128
NEAR_SIZE = 1 << 20
F32, BF16 = jnp.float32, jnp.bfloat16
VMEM = pl.BlockSpec(memory_space=pltpu.VMEM)
HBM = pl.BlockSpec(memory_space=pltpu.HBM)


def dot(a, b, dims):
    return lax.dot_general(a, b, ((dims[:1], dims[1:]), ((), ())), preferred_element_type=F32)


def square(size):
    return tuple(lax.broadcasted_iota(jnp.int32, (size, size), axis) for axis in (0, 1))


def join_kernel(route_hbm, prob_hbm, tok_hbm, cot_hbm, out_ref, route_v, prob_v, sems):
    tok_dev, features = tok_hbm.shape
    small = [
        pltpu.make_async_copy(route_hbm, route_v, sems.at[0]),
        pltpu.make_async_copy(prob_hbm, prob_v, sems.at[1]),
    ]
    large = [
        pltpu.make_async_copy(tok_hbm, out_ref.at[:, pl.ds(0, features)], sems.at[2]),
        pltpu.make_async_copy(cot_hbm, out_ref.at[:, pl.ds(features, features)], sems.at[3]),
    ]
    for copy in small + large:
        copy.start()
    own = lax.broadcasted_iota(jnp.int32, route_v.shape, 0) == lax.axis_index("dp")
    here, there = square(tok_dev)
    for copy in small:
        copy.wait()
    route = jnp.sum(jnp.where(own, route_v[...].astype(F32), 0.0), axis=0, keepdims=True)
    prob = jnp.sum(jnp.where(own, prob_v[...].astype(F32), 0.0), axis=0, keepdims=True)
    route = jnp.sum(jnp.where(here == there, route, 0.0), axis=1, keepdims=True)
    prob = jnp.sum(jnp.where(here == there, prob, 0.0), axis=1, keepdims=True)
    lane = lax.broadcasted_iota(jnp.int32, (tok_dev, LANES), 1)
    tail = jnp.where(lane == 0, prob, jnp.where(lane == 1, route, 0.0))
    out_ref[:, 2 * features :] = tail.astype(BF16)
    for copy in large:
        copy.wait()


def load_kernel(*refs):
    ins, outs, sems = refs[:3], refs[3:6], refs[6]
    copies = [pltpu.make_async_copy(a, b, sems.at[i]) for i, (a, b) in enumerate(zip(ins, outs))]
    for copy in copies:
        copy.start()
    for copy in copies:
        copy.wait()


def pack_kernel(slots, own_ref, other_ref, w0, w1, w2, send_ref, pick_ref):
    del w0, w1, w2
    tok_dev, width = own_ref.shape
    block = pick_ref.shape[0]
    groups = send_ref.shape[0] // block
    half = block // (2 * slots)
    top = lax.axis_index("top")
    here, there = square(tok_dev)
    place = lax.broadcasted_iota(jnp.int32, (block, tok_dev), 0)
    sent = jnp.zeros((block, width), F32)
    picks = []
    for rows_ref, origin in ((own_ref, top), (other_ref, 1 - top)):
        column = rows_ref[:, width - LANES + 1 : width - LANES + 2].astype(F32)
        row = jnp.sum(jnp.where(here == there, column, 0.0), axis=0, keepdims=True)
        rank = jnp.sum(jnp.where((column == row) & (here < there), 1.0, 0.0), axis=0, keepdims=True)
        low = row.astype(jnp.int32) - top * half
        target = low * (2 * slots) + origin * slots + rank.astype(jnp.int32)
        target = jnp.where((low >= 0) & (low < half), target, -1)
        pick = (place == target).astype(F32).astype(BF16)
        sent += dot(pick, rows_ref[...], (1, 0))
        picks.append(pick)
    pick_ref[:, :tok_dev] = picks[0]
    pick_ref[:, tok_dev:] = picks[1]
    sent = sent.astype(BF16)
    for g in range(groups):
        send_ref[g * block : (g + 1) * block, :] = sent


def expert_kernel(chunk, got_ref, gate_ref, up_ref, down_ref, reply_ref, dg_ref, du_ref, sa_ref):
    features = gate_ref.shape[1]
    mine = lax.axis_index("dp")
    lane = lax.broadcasted_iota(jnp.int32, (chunk, LANES), 1)

    @pl.loop(0, got_ref.shape[0] // chunk)
    def _(step):
        at = pl.ds(pl.multiple_of(step * chunk, chunk), chunk)
        rows_x = got_ref[at, :features]
        rows_dy = got_ref[at, features : 2 * features]
        weight = got_ref[at, 2 * features : 2 * features + 1].astype(F32)
        gate_pre = dot(rows_x, gate_ref[...], (1, 1))
        up_pre = dot(rows_x, up_ref[...], (1, 1))
        back_proj = dot(rows_dy, down_ref[...], (1, 1))
        sigma = jax.nn.sigmoid(gate_pre)
        swish = gate_pre * sigma
        slope = sigma * (1.0 + gate_pre * (1.0 - sigma))
        active = swish * up_pre
        d_active = weight * back_proj
        d_gate = (d_active * up_pre * slope).astype(BF16)
        d_up = (d_active * swish).astype(BF16)
        part = jnp.sum(active * back_proj, axis=1, keepdims=True)
        dg_ref[at, :] = d_gate
        du_ref[at, :] = d_up
        sa_ref[at, :] = (weight * active).astype(BF16)
        grad = dot(d_gate, gate_ref[...], (1, 0)) + dot(d_up, up_ref[...], (1, 0))
        reply_ref[at, :features] = grad.astype(BF16)
        reply_ref[at, features:] = jnp.where(lane == mine, part, 0.0).astype(BF16)


def combine_kernel(pick_ref, back_ref, own_ref, other_ref):
    total = dot(pick_ref[...], back_ref[...], (1, 0)).astype(BF16)
    own_ref[...] = total[: own_ref.shape[0]]
    other_ref[...] = total[own_ref.shape[0] :]


def finish_kernel(own_ref, other_ref, tok_ref, prob_ref):
    tok_dev, features = tok_ref.shape
    total = own_ref[...].astype(F32) + other_ref[...].astype(F32)
    tok_ref[...] = total[:, :features].astype(BF16)
    part = jnp.sum(total[:, features:], axis=1, keepdims=True)
    here, there = square(tok_dev)
    prob_ref[...] = jnp.sum(jnp.where(here == there, part, 0.0), axis=0, keepdims=True)


def near(shape, dtype=BF16):
    small = math.prod(shape) <= NEAR_SIZE
    return pltpu.VMEM(shape, dtype) if small else jax.ShapeDtypeStruct(shape, dtype)


def fetched(array):
    small = array.size <= NEAR_SIZE
    return pltpu.with_memory_space_constraint(array, pltpu.VMEM) if small else array


def far(*arrays):
    return [pltpu.with_memory_space_constraint(a, pltpu.HBM) for a in arrays]


def call(kernel, in_specs, outs, *args, scratch=(), cost=None):
    small = all(math.prod(out.shape) <= NEAR_SIZE for out in outs)
    return pl.pallas_call(
        kernel,
        in_specs=in_specs,
        scratch_shapes=scratch,
        out_specs=[VMEM] * len(outs),
        out_shape=outs,
        cost_estimate=cost,
        compiler_params=pltpu.CompilerParams(vmem_limit_bytes=(16 if small else 48) << 20),
    )(*args)


def body(tokens, cotangent, routes, gate_prob, w_gate, w_up, w_down):
    groups = lax.axis_size("dp")
    half = lax.axis_size("low")
    _, tok_dev, features = tokens.shape
    hidden = w_gate.shape[1]
    slots = tok_dev // 4
    block = half * 2 * slots
    rows = groups * block
    chunk = min(rows, 256)
    width = 2 * features + LANES

    (own,) = call(
        join_kernel,
        [HBM] * 4,
        [near((tok_dev, width))],
        *far(routes, gate_prob, tokens[0], cotangent[0]),
        scratch=[
            pltpu.VMEM(routes.shape, routes.dtype),
            pltpu.VMEM(gate_prob.shape, gate_prob.dtype),
            pltpu.SemaphoreType.DMA((4,)),
        ],
    )
    other = lax.ppermute(own, "top", SWAP)
    weights = call(
        load_kernel,
        [HBM] * 3,
        [near((hidden, features))] * 3,
        *far(w_gate[0], w_up[0], w_down[0]),
        scratch=[pltpu.SemaphoreType.DMA((3,))],
        cost=pl.CostEstimate(flops=0, transcendentals=0, bytes_accessed=12 * hidden * features),
    )
    weights = [fetched(a) for a in weights]
    send, pick = call(
        lambda *refs: pack_kernel(slots, *refs),
        [VMEM] * 5,
        [near((rows, width)), near((block, 2 * tok_dev))],
        fetched(own), fetched(other), *weights,
    )
    got = lax.all_to_all(send, HALF_AXES, split_axis=0, concat_axis=0, tiled=True)
    reply, d_gate, d_up, scaled_act = call(
        lambda *refs: expert_kernel(chunk, *refs),
        [VMEM] * 4,
        [near((rows, features + LANES))] + [near((rows, hidden))] * 3,
        fetched(got), *weights,
    )
    back = lax.all_to_all(reply, HALF_AXES, split_axis=0, concat_axis=0, tiled=True)
    kept, given = call(
        combine_kernel,
        [VMEM] * 2,
        [near((tok_dev, features + LANES))] * 2,
        jnp.tile(pick.T, (1, groups)), back,
    )
    grad_tokens, grad_prob = call(
        finish_kernel,
        [VMEM] * 2,
        [jax.ShapeDtypeStruct((tok_dev, features), BF16), jax.ShapeDtypeStruct((1, tok_dev), F32)],
        fetched(kept), fetched(lax.ppermute(given, "top", SWAP)),
    )
    rows_x, rows_dy = got[:, :features], got[:, features : 2 * features]
    weight_grads = [
        jnp.einsum("rh,rd->hd", left, right, preferred_element_type=F32).astype(BF16)[None]
        for left, right in ((d_gate, rows_x), (d_up, rows_x), (scaled_act, rows_dy))
    ]
    return (grad_tokens[None], grad_prob, *weight_grads)


def solution(mesh):
    groups, experts = (mesh.shape[axis] for axis in ("dp", "expert"))
    split = Mesh(mesh.devices.reshape(groups, 2, experts // 2), ("dp", "top", "low"))
    expert = ("top", "low")
    in_specs = (
        P("dp", expert, None),
        P("dp", expert, None),
        P(None, expert),
        P(None, expert),
        P(expert, "dp", None),
        P(expert, "dp", None),
        P(expert, "dp", None),
    )
    out_specs = (
        P("dp", expert, None),
        P("dp", expert),
        P(expert, "dp", None),
        P(expert, "dp", None),
        P(expert, "dp", None),
    )
    return jax.shard_map(body, mesh=split, in_specs=in_specs, out_specs=out_specs, check_vma=False)
```

time: 59.6 us -> 58.7 us (0.985)
  waiting for transfers between devices: 16.1 us -> 12.3 us
  starting transfers between devices: 7.44 us -> 10.3 us
    all_to_all x1, waiting for transfers between devices: 12.1 us -> 6.24 us  [body(): lax.all_to_all(reply, HALF_AXES, split_axis=0, concat_axis=0, tiled=True)]
    ppermute x1 -> x2, starting transfers between devices: 3.2 us -> 6.36 us  [the longest x1 3.2 us: body(): other = lax.ppermute(own, 'top', SWAP)]
    ppermute x1 -> x2, waiting for transfers between devices: 4 us -> 6.11 us  [the longest x1 3.82 us: body(): other = lax.ppermute(own, 'top', SWAP)]
    pallas_call x5 -> x6, Pallas kernels: 8.64 us -> 8.22 us  [call(): pl.pallas_call(kernel, in_specs=in_specs, scratch_shapes=scratch, out_spe...]
  transfers between devices with their start and end apart: 2 -> 3, of which waited for: 2 -> 3; matrix products, arithmetic and copies ran while one was open for 9% -> 9% of each run, Pallas kernels for 4% -> 4%
where the time goes in v6:
time: 58.7 us; the launch traced here: 57.9 us
  blocking collectives  21 us (36%)
  waiting for transfers between devices  12.3 us (21%)
  starting transfers between devices  10.3 us (18%)
  Pallas kernels  8.22 us (14%)
  matrix products  5.22 us (9%)
  between operations  0.68 us (1%)
    all_to_all x1, blocking collectives, body(): lax.all_to_all(send, HALF_AXES, split_axis=0, concat_axis=0, tiled=True)  21 us
    pallas_call x6, Pallas kernels, call(): pl.pallas_call(kernel, in_specs=in_specs, scratch_shapes=scratch, out_spe...  8.22 us
    all_to_all x1, waiting for transfers between devices, body(): lax.all_to_all(reply, HALF_AXES, split_axis=0, concat_axis=0, tiled=True)  6.24 us
    dot_general x3, matrix products, body(): jnp.einsum('rh,rd->hd', left, right, preferred_element_type=F32)  5.22 us
    all_to_all x1, starting transfers between devices, body(): lax.all_to_all(reply, HALF_AXES, split_axis=0, concat_axis=0, tiled=True)  3.92 us
    ppermute x1, waiting for transfers between devices, body(): other = lax.ppermute(own, 'top', SWAP)  3.82 us
    ppermute x1, starting transfers between devices, body(): other = lax.ppermute(own, 'top', SWAP)  3.2 us
    ppermute x1, starting transfers between devices, body(): lax.ppermute(given, 'top', SWAP)  3.16 us
  transfers between devices with their start and end apart: 3, of which 3 were waited for; matrix products, arithmetic and copies ran while one was open for 9% of the time, Pallas kernels for 4%

profile of v6, /device:TPU:1, one launch (start us, length us, event | category | flops | bytes accessed | tf_op | source)
XLA Modules:
  0.0 57.9 jit_solution(1341253377886505393)
XLA Ops:
  0.6 0.9 %shard_map.110.refs_0_ = bf16[16,4224]{1,0:T(8,128)(2,1)S(1)} custom-call(s32[2,16]{1,0:T(2,128)} %route_hbm.1, bf16[2,16]{1,0:T(2,128)(2,1)} %prob_hbm.1, bf16[16,2048]{1,0:T(8,128)(2,1)} %bitcast.30, bf16[16,2048]{1,0:T(8,128)(2,1)} %bitcast.31), custom_call_target="tpu_custom_call" | custom-call | tf_op jit(solution)/shard_map/pallas_call | solution.py:153
  1.6 3.2 %collective-permute-start = (bf16[16,4224]{1,0:T(8,128)(2,1)S(1)}, bf16[16,4224]{1,0:T(8,128)(2,1)S(1)}, u32[]{:S(2)}, u32[]{:S(2)}) collective-permute-start(bf16[16,4224]{1,0:T(8,128)(2,1)S(1)} %shard_map.110.refs_0_), channel_id=1, source_target_pairs={{0,8},{8,0},{1,9},{9,1},{2,10},{10,2},{3,11},{11,3},{4,12},{12,4},... | collective-permute-start | bytes 405512 | tf_op jit(solution)/shard_map/ppermute | solution.py:186
  4.8 2.4 %shard_map.111 = (bf16[384,2048]{1,0:T(8,128)(2,1)S(1)}, bf16[384,2048]{1,0:T(8,128)(2,1)S(1)}, bf16[384,2048]{1,0:T(8,128)(2,1)S(1)}) custom-call(bf16[384,2048]{1,0:T(8,128)(2,1)} %bitcast.27, bf16[384,2048]{1,0:T(8,128)(2,1)} %bitcast.28, bf16[384,2048]{1,0:T(8,128)(2,1)} %bitcast.29), custom_call_target="tpu_custom_call" | custom-call | bytes 9437184 | tf_op jit(solution)/shard_map/pallas_call | solution.py:153
  7.2 3.8 %collective-permute-done.refs_1_ = bf16[16,4224]{1,0:T(8,128)(2,1)S(1)} collective-permute-done((bf16[16,4224]{1,0:T(8,128)(2,1)S(1)}, bf16[16,4224]{1,0:T(8,128)(2,1)S(1)}, u32[]{:S(2)}, u32[]{:S(2)}) %collective-permute-start) | collective-permute-done | bytes 135200 | tf_op jit(solution)/shard_map/ppermute | solution.py:186
  11.0 0.5 shard_map.112
  11.5 21.0 %all_to_all.22 = bf16[16,8,4224]{2,1,0:T(8,128)(2,1)S(1)} all-to-all(bf16[16,8,4224]{2,1,0:T(8,128)(2,1)S(1)} %bitcast.25), channel_id=1, replica_groups=mesh['dp'=2,'top'=2,'low'=8] {'dp','low'}, dimensions={0} | all-to-all | bytes 2162688 | tf_op jit(solution)/shard_map/all_to_all | solution.py:202
  32.5 3.5 %shard_map.113 = (bf16[128,2176]{1,0:T(8,128)(2,1)}, bf16[128,384]{1,0:T(8,128)(2,1)S(1)}, bf16[128,384]{1,0:T(8,128)(2,1)S(1)}, bf16[128,384]{1,0:T(8,128)(2,1)S(1)}) custom-call(bf16[128,4224]{1,0:T(8,128)(2,1)S(1)} %bitcast.20, bf16[384,2048]{1,0:T(8,128)(2,1)S(1)} %get-tuple-element.18.refs_2_.refs_1_, ...), custom_call_target="tpu_custom_call" | custom-call | tf_op jit(solution)/shard_map/pallas_call | solution.py:153
  36.0 3.9 %all-to-all-start.1 = ((bf16[16,8,2176]{2,1,0:T(8,128)(2,1)}), bf16[16,8,2176]{2,1,0:T(8,128)(2,1)S(1)}, u32[]{:S(2)}, u32[]{:S(2)}) async-start(bf16[16,8,2176]{2,1,0:T(8,128)(2,1)} %bitcast.8), calls=%async_computation.1 | async-start | bytes 1114112 | tf_op jit(solution)/shard_map/all_to_all | solution.py:209
  39.9 0.1 copy.12
  40.0 0.1 tile.10.pick_ref
  40.1 1.7 %fusion = bf16[1,384,2048]{2,1,0:T(8,128)(2,1)} fusion(bf16[128,384]{1,0:T(8,128)(2,1)S(1)} %get-tuple-element.28, bf16[128,4224]{1,0:T(8,128)(2,1)S(1)} %bitcast.21), kind=kOutput, calls=%fused_computation.3 | convolution fusion | flops 202113024 | bytes 2195456 | tf_op jit(solution)/shard_map/rh,rd->hd/dot_general | solution.py:224
  41.9 1.7 %fusion.1 = bf16[1,384,2048]{2,1,0:T(8,128)(2,1)} fusion(bf16[128,384]{1,0:T(8,128)(2,1)S(1)} %get-tuple-element.29, bf16[128,4224]{1,0:T(8,128)(2,1)S(1)} %bitcast.22), kind=kOutput, calls=%fused_computation.4 | convolution fusion | flops 202113024 | bytes 2195456 | tf_op jit(solution)/shard_map/rh,rd->hd/dot_general | solution.py:224
  43.6 6.2 %all-to-all-done.1 = bf16[16,8,2176]{2,1,0:T(8,128)(2,1)S(1)} async-done(((bf16[16,8,2176]{2,1,0:T(8,128)(2,1)}), bf16[16,8,2176]{2,1,0:T(8,128)(2,1)S(1)}, u32[]{:S(2)}, u32[]{:S(2)}) %all-to-all-start.1) | async-done | bytes 557088 | tf_op jit(solution)/shard_map/all_to_all | solution.py:209
  49.8 0.2 shard_map.114
  50.1 3.2 %collective-permute-start.1 = (bf16[16,2176]{1,0:T(8,128)(2,1)S(1)}, bf16[16,2176]{1,0:T(8,128)(2,1)S(1)}, u32[]{:S(2)}, u32[]{:S(2)}) collective-permute-start(bf16[16,2176]{1,0:T(8,128)(2,1)S(1)} %get-tuple-element.25), channel_id=1, source_target_pairs={{0,8},{8,0},{1,9},{9,1},{2,10},{10,2},{3,11},{11,3},{4,12},{12,4},... | collective-permute-start | bytes 208904 | tf_op jit(solution)/shard_map/ppermute | solution.py:220
  53.2 1.7 %fusion.2 = bf16[1,384,2048]{2,1,0:T(8,128)(2,1)} fusion(bf16[128,384]{1,0:T(8,128)(2,1)S(1)} %get-tuple-element.30, bf16[128,4224]{1,0:T(8,128)(2,1)S(1)} %bitcast.23), kind=kOutput, calls=%fused_computation.5 | convolution fusion | flops 202113024 | bytes 2195456 | tf_op jit(solution)/shard_map/rh,rd->hd/dot_general | solution.py:224
  55.0 2.3 %collective-permute-done.1.other_ref = bf16[16,2176]{1,0:T(8,128)(2,1)S(1)} collective-permute-done((bf16[16,2176]{1,0:T(8,128)(2,1)S(1)}, bf16[16,2176]{1,0:T(8,128)(2,1)S(1)}, u32[]{:S(2)}, u32[]{:S(2)}) %collective-permute-start.1) | collective-permute-done | bytes 69664 | tf_op jit(solution)/shard_map/ppermute | solution.py:220
  57.2 0.7 %shard_map.115 = (bf16[16,2048]{1,0:T(8,128)(2,1)}, f32[1,16]{1,0:T(1,128)}) custom-call(bf16[16,2176]{1,0:T(8,128)(2,1)S(1)} %get-tuple-element.24.own_ref, bf16[16,2176]{1,0:T(8,128)(2,1)S(1)} %collective-permute-done.1.other_ref), custom_call_target="tpu_custom_call" | custom-call | tf_op jit(solution)/shard_map/pallas_call | solution.py:153
  (1 shorter events, 0.0 us)
Async XLA Ops:
  1.6 9.4 %collective-permute-start = (bf16[16,4224]{1,0:T(8,128)(2,1)S(1)}, bf16[16,4224]{1,0:T(8,128)(2,1)S(1)}, u32[]{:S(2)}, u32[]{:S(2)}) collective-permute-start(bf16[16,4224]{1,0:T(8,128)(2,1)S(1)} %shard_map.110.refs_0_), channel_id=1, source_target_pairs={{0,8},{8,0},{1,9},{9,1},{2,10},{10,2},{3,11},{11,3},{4,12},{12,4},... | collective-permute-start | bytes 405512 | tf_op jit(solution)/shard_map/ppermute | solution.py:186
  36.0 13.8 %all-to-all-start.1 = ((bf16[16,8,2176]{2,1,0:T(8,128)(2,1)}), bf16[16,8,2176]{2,1,0:T(8,128)(2,1)S(1)}, u32[]{:S(2)}, u32[]{:S(2)}) async-start(bf16[16,8,2176]{2,1,0:T(8,128)(2,1)} %bitcast.8), calls=%async_computation.1 | async-start | bytes 1114112 | tf_op jit(solution)/shard_map/all_to_all | solution.py:209
  50.1 7.2 %collective-permute-start.1 = (bf16[16,2176]{1,0:T(8,128)(2,1)S(1)}, bf16[16,2176]{1,0:T(8,128)(2,1)S(1)}, u32[]{:S(2)}, u32[]{:S(2)}) collective-permute-start(bf16[16,2176]{1,0:T(8,128)(2,1)S(1)} %get-tuple-element.25), channel_id=1, source_target_pairs={{0,8},{8,0},{1,9},{9,1},{2,10},{10,2},{3,11},{11,3},{4,12},{12,4},... | collective-permute-start | bytes 208904 | tf_op jit(solution)/shard_map/ppermute | solution.py:220

commit v7 on v6

--- a/solution.py
+++ b/solution.py
@@ -11,7 +11,7 @@
 HALF_AXES = ("dp", "low")
 SWAP = [(0, 1), (1, 0)]
 LANES = 128
-NEAR_SIZE = 1 << 20
+NEAR_SIZE = 2 << 20
 F32, BF16 = jnp.float32, jnp.bfloat16
 VMEM = pl.BlockSpec(memory_space=pltpu.VMEM)
 HBM = pl.BlockSpec(memory_space=pltpu.HBM)
@@ -52,17 +52,22 @@
         copy.wait()
 
 
-def load_kernel(*refs):
-    ins, outs, sems = refs[:3], refs[3:6], refs[6]
-    copies = [pltpu.make_async_copy(a, b, sems.at[i]) for i, (a, b) in enumerate(zip(ins, outs))]
+def load_kernel(gate_hbm, up_hbm, down_hbm, rows_ref, gate_t, up_t, down_t, down_v, sems):
+    hidden = gate_hbm.shape[0]
+    places = (rows_ref.at[pl.ds(0, hidden), :], rows_ref.at[pl.ds(hidden, hidden), :], down_v)
+    copies = [
+        pltpu.make_async_copy(a, b, sems.at[i])
+        for i, (a, b) in enumerate(zip((gate_hbm, up_hbm, down_hbm), places))
+    ]
     for copy in copies:
         copy.start()
-    for copy in copies:
+    for copy, place, turned in zip(copies, places, (gate_t, up_t, down_t)):
         copy.wait()
-
-
-def pack_kernel(slots, own_ref, other_ref, w0, w1, w2, send_ref, pick_ref):
-    del w0, w1, w2
+        turned[...] = place[...].T
+
+
+def pack_kernel(slots, own_ref, other_ref, w0, w1, w2, w3, send_ref, pick_ref):
+    del w0, w1, w2, w3
     tok_dev, width = own_ref.shape
     block = pick_ref.shape[0]
     groups = send_ref.shape[0] // block
@@ -89,8 +94,8 @@
         send_ref[g * block : (g + 1) * block, :] = sent
 
 
-def expert_kernel(chunk, got_ref, gate_ref, up_ref, down_ref, reply_ref, dg_ref, du_ref, sa_ref):
-    features = gate_ref.shape[1]
+def expert_kernel(chunk, got_ref, rows_ref, gate_t, up_t, down_t, reply_ref, dg_ref, du_ref, sa_ref):
+    features = rows_ref.shape[1]
     mine = lax.axis_index("dp")
     lane = lax.broadcasted_iota(jnp.int32, (chunk, LANES), 1)
 
@@ -100,9 +105,9 @@
         rows_x = got_ref[at, :features]
         rows_dy = got_ref[at, features : 2 * features]
         weight = got_ref[at, 2 * features : 2 * features + 1].astype(F32)
-        gate_pre = dot(rows_x, gate_ref[...], (1, 1))
-        up_pre = dot(rows_x, up_ref[...], (1, 1))
-        back_proj = dot(rows_dy, down_ref[...], (1, 1))
+        gate_pre = dot(rows_x, gate_t[...], (1, 0))
+        up_pre = dot(rows_x, up_t[...], (1, 0))
+        back_proj = dot(rows_dy, down_t[...], (1, 0))
         sigma = jax.nn.sigmoid(gate_pre)
         swish = gate_pre * sigma
         slope = sigma * (1.0 + gate_pre * (1.0 - sigma))
@@ -114,7 +119,7 @@
         dg_ref[at, :] = d_gate
         du_ref[at, :] = d_up
         sa_ref[at, :] = (weight * active).astype(BF16)
-        grad = dot(d_gate, gate_ref[...], (1, 0)) + dot(d_up, up_ref[...], (1, 0))
+        grad = dot(jnp.concatenate([d_gate, d_up], axis=1), rows_ref[...], (1, 0))
         reply_ref[at, :features] = grad.astype(BF16)
         reply_ref[at, features:] = jnp.where(lane == mine, part, 0.0).astype(BF16)
 
@@ -187,22 +192,22 @@
     weights = call(
         load_kernel,
         [HBM] * 3,
-        [near((hidden, features))] * 3,
+        [near((2 * hidden, features))] + [near((features, hidden))] * 3,
         *far(w_gate[0], w_up[0], w_down[0]),
-        scratch=[pltpu.SemaphoreType.DMA((3,))],
-        cost=pl.CostEstimate(flops=0, transcendentals=0, bytes_accessed=12 * hidden * features),
+        scratch=[pltpu.VMEM((hidden, features), BF16), pltpu.SemaphoreType.DMA((3,))],
+        cost=pl.CostEstimate(flops=0, transcendentals=0, bytes_accessed=16 * hidden * features),
     )
     weights = [fetched(a) for a in weights]
     send, pick = call(
         lambda *refs: pack_kernel(slots, *refs),
-        [VMEM] * 5,
+        [VMEM] * 6,
         [near((rows, width)), near((block, 2 * tok_dev))],
         fetched(own), fetched(other), *weights,
     )
     got = lax.all_to_all(send, HALF_AXES, split_axis=0, concat_axis=0, tiled=True)
     reply, d_gate, d_up, scaled_act = call(
         lambda *refs: expert_kernel(chunk, *refs),
-        [VMEM] * 4,
+        [VMEM] * 5,
         [near((rows, features + LANES))] + [near((rows, hidden))] * 3,
         fetched(got), *weights,
     )

time: 58.7 us -> 57.6 us (0.981)
  Pallas kernels: 8.22 us -> 7.51 us
    pallas_call x6, Pallas kernels: 8.22 us -> 7.51 us  [call(): pl.pallas_call(kernel, in_specs=in_specs, scratch_shapes=scratch, out_spe...]
  transfers between devices with their start and end apart: 3 -> 3, of which waited for: 3 -> 3; matrix products, arithmetic and copies ran while one was open for 9% -> 10% of each run, Pallas kernels for 4% -> 5%
where the time goes in v7:
time: 57.6 us; the launch traced here: 56.7 us
  blocking collectives  21 us (36%)
  waiting for transfers between devices  11.9 us (21%)
  starting transfers between devices  10.3 us (18%)
  Pallas kernels  7.51 us (13%)
  matrix products  5.22 us (9%)
  between operations  0.68 us (1%)
    all_to_all x1, blocking collectives, body(): lax.all_to_all(send, HALF_AXES, split_axis=0, concat_axis=0, tiled=True)  21 us
    pallas_call x6, Pallas kernels, call(): pl.pallas_call(kernel, in_specs=in_specs, scratch_shapes=scratch, out_spe...  7.51 us
    all_to_all x1, waiting for transfers between devices, body(): lax.all_to_all(reply, HALF_AXES, split_axis=0, concat_axis=0, tiled=True)  6.24 us
    dot_general x3, matrix products, body(): jnp.einsum('rh,rd->hd', left, right, preferred_element_type=F32)  5.22 us
    all_to_all x1, starting transfers between devices, body(): lax.all_to_all(reply, HALF_AXES, split_axis=0, concat_axis=0, tiled=True)  3.94 us
    ppermute x1, waiting for transfers between devices, body(): other = lax.ppermute(own, 'top', SWAP)  3.36 us
    ppermute x1, starting transfers between devices, body(): other = lax.ppermute(own, 'top', SWAP)  3.2 us
    ppermute x1, starting transfers between devices, body(): lax.ppermute(given, 'top', SWAP)  3.16 us
  transfers between devices with their start and end apart: 3, of which 3 were waited for; matrix products, arithmetic and copies ran while one was open for 10% of the time, Pallas kernels for 5%

profile of v7, /device:TPU:1, one launch (start us, length us, event | category | flops | bytes accessed | tf_op | source)
XLA Modules:
  0.0 56.7 jit_solution(15723475343789660024)
XLA Ops:
  0.6 0.9 %shard_map.110.refs_0_ = bf16[16,4224]{1,0:T(8,128)(2,1)S(1)} custom-call(s32[2,16]{1,0:T(2,128)} %route_hbm.1, bf16[2,16]{1,0:T(2,128)(2,1)} %prob_hbm.1, bf16[16,2048]{1,0:T(8,128)(2,1)} %bitcast.30, bf16[16,2048]{1,0:T(8,128)(2,1)} %bitcast.31), custom_call_target="tpu_custom_call" | custom-call | tf_op jit(solution)/shard_map/pallas_call | solution.py:158
  1.6 3.2 %collective-permute-start = (bf16[16,4224]{1,0:T(8,128)(2,1)S(1)}, bf16[16,4224]{1,0:T(8,128)(2,1)S(1)}, u32[]{:S(2)}, u32[]{:S(2)}) collective-permute-start(bf16[16,4224]{1,0:T(8,128)(2,1)S(1)} %shard_map.110.refs_0_), channel_id=1, source_target_pairs={{0,8},{8,0},{1,9},{9,1},{2,10},{10,2},{3,11},{11,3},{4,12},{12,4},... | collective-permute-start | bytes 405512 | tf_op jit(solution)/shard_map/ppermute | solution.py:191
  4.8 2.8 %shard_map.111 = (bf16[768,2048]{1,0:T(8,128)(2,1)S(1)}, bf16[2048,384]{1,0:T(8,128)(2,1)S(1)}, bf16[2048,384]{1,0:T(8,128)(2,1)S(1)}, bf16[2048,384]{1,0:T(8,128)(2,1)S(1)}) custom-call(bf16[384,2048]{1,0:T(8,128)(2,1)} %bitcast.27, bf16[384,2048]{1,0:T(8,128)(2,1)} %bitcast.28, bf16[384,2048]{1,0:T(8,128)(2,1)} %bitcast.29), custom_call_target="tpu_custom_call" | custom-call | bytes 12582912 | tf_op jit(solution)/shard_map/pallas_call | solution.py:158
  7.6 3.4 %collective-permute-done.refs_1_ = bf16[16,4224]{1,0:T(8,128)(2,1)S(1)} collective-permute-done((bf16[16,4224]{1,0:T(8,128)(2,1)S(1)}, bf16[16,4224]{1,0:T(8,128)(2,1)S(1)}, u32[]{:S(2)}, u32[]{:S(2)}) %collective-permute-start) | collective-permute-done | bytes 135200 | tf_op jit(solution)/shard_map/ppermute | solution.py:191
  11.0 0.5 shard_map.112
  11.5 21.0 %all_to_all.22 = bf16[16,8,4224]{2,1,0:T(8,128)(2,1)S(1)} all-to-all(bf16[16,8,4224]{2,1,0:T(8,128)(2,1)S(1)} %bitcast.25), channel_id=1, replica_groups=mesh['dp'=2,'top'=2,'low'=8] {'dp','low'}, dimensions={0} | all-to-all | bytes 2162688 | tf_op jit(solution)/shard_map/all_to_all | solution.py:207
  32.5 2.4 %shard_map.113 = (bf16[128,2176]{1,0:T(8,128)(2,1)}, bf16[128,384]{1,0:T(8,128)(2,1)S(1)}, bf16[128,384]{1,0:T(8,128)(2,1)S(1)}, bf16[128,384]{1,0:T(8,128)(2,1)S(1)}) custom-call(bf16[128,4224]{1,0:T(8,128)(2,1)S(1)} %bitcast.20, bf16[768,2048]{1,0:T(8,128)(2,1)S(1)} %get-tuple-element.19.refs_2_.refs_1_, ...), custom_call_target="tpu_custom_call" | custom-call | tf_op jit(solution)/shard_map/pallas_call | solution.py:158
  34.8 3.9 %all-to-all-start.1 = ((bf16[16,8,2176]{2,1,0:T(8,128)(2,1)}), bf16[16,8,2176]{2,1,0:T(8,128)(2,1)S(1)}, u32[]{:S(2)}, u32[]{:S(2)}) async-start(bf16[16,8,2176]{2,1,0:T(8,128)(2,1)} %bitcast.8), calls=%async_computation.1 | async-start | bytes 1114112 | tf_op jit(solution)/shard_map/all_to_all | solution.py:214
  38.8 0.1 copy.12
  38.9 0.1 tile.10.pick_ref
  39.0 1.7 %fusion = bf16[1,384,2048]{2,1,0:T(8,128)(2,1)} fusion(bf16[128,384]{1,0:T(8,128)(2,1)S(1)} %get-tuple-element.30, bf16[128,4224]{1,0:T(8,128)(2,1)S(1)} %bitcast.21), kind=kOutput, calls=%fused_computation.3 | convolution fusion | flops 202113024 | bytes 2195456 | tf_op jit(solution)/shard_map/rh,rd->hd/dot_general | solution.py:229
  40.7 1.7 %fusion.1 = bf16[1,384,2048]{2,1,0:T(8,128)(2,1)} fusion(bf16[128,384]{1,0:T(8,128)(2,1)S(1)} %get-tuple-element.31, bf16[128,4224]{1,0:T(8,128)(2,1)S(1)} %bitcast.22), kind=kOutput, calls=%fused_computation.4 | convolution fusion | flops 202113024 | bytes 2195456 | tf_op jit(solution)/shard_map/rh,rd->hd/dot_general | solution.py:229
  42.5 6.2 %all-to-all-done.1 = bf16[16,8,2176]{2,1,0:T(8,128)(2,1)S(1)} async-done(((bf16[16,8,2176]{2,1,0:T(8,128)(2,1)}), bf16[16,8,2176]{2,1,0:T(8,128)(2,1)S(1)}, u32[]{:S(2)}, u32[]{:S(2)}) %all-to-all-start.1) | async-done | bytes 557088 | tf_op jit(solution)/shard_map/all_to_all | solution.py:214
  48.7 0.2 shard_map.114
  48.9 3.2 %collective-permute-start.1 = (bf16[16,2176]{1,0:T(8,128)(2,1)S(1)}, bf16[16,2176]{1,0:T(8,128)(2,1)S(1)}, u32[]{:S(2)}, u32[]{:S(2)}) collective-permute-start(bf16[16,2176]{1,0:T(8,128)(2,1)S(1)} %get-tuple-element.27), channel_id=1, source_target_pairs={{0,8},{8,0},{1,9},{9,1},{2,10},{10,2},{3,11},{11,3},{4,12},{12,4},... | collective-permute-start | bytes 208904 | tf_op jit(solution)/shard_map/ppermute | solution.py:225
  52.1 1.7 %fusion.2 = bf16[1,384,2048]{2,1,0:T(8,128)(2,1)} fusion(bf16[128,384]{1,0:T(8,128)(2,1)S(1)} %get-tuple-element.32, bf16[128,4224]{1,0:T(8,128)(2,1)S(1)} %bitcast.23), kind=kOutput, calls=%fused_computation.5 | convolution fusion | flops 202113024 | bytes 2195456 | tf_op jit(solution)/shard_map/rh,rd->hd/dot_general | solution.py:229
  53.8 2.3 %collective-permute-done.1.other_ref = bf16[16,2176]{1,0:T(8,128)(2,1)S(1)} collective-permute-done((bf16[16,2176]{1,0:T(8,128)(2,1)S(1)}, bf16[16,2176]{1,0:T(8,128)(2,1)S(1)}, u32[]{:S(2)}, u32[]{:S(2)}) %collective-permute-start.1) | collective-permute-done | bytes 69664 | tf_op jit(solution)/shard_map/ppermute | solution.py:225
  56.1 0.7 %shard_map.115 = (bf16[16,2048]{1,0:T(8,128)(2,1)}, f32[1,16]{1,0:T(1,128)}) custom-call(bf16[16,2176]{1,0:T(8,128)(2,1)S(1)} %get-tuple-element.26.own_ref, bf16[16,2176]{1,0:T(8,128)(2,1)S(1)} %collective-permute-done.1.other_ref), custom_call_target="tpu_custom_call" | custom-call | tf_op jit(solution)/shard_map/pallas_call | solution.py:158
  (1 shorter events, 0.0 us)
Async XLA Ops:
  1.6 9.4 %collective-permute-start = (bf16[16,4224]{1,0:T(8,128)(2,1)S(1)}, bf16[16,4224]{1,0:T(8,128)(2,1)S(1)}, u32[]{:S(2)}, u32[]{:S(2)}) collective-permute-start(bf16[16,4224]{1,0:T(8,128)(2,1)S(1)} %shard_map.110.refs_0_), channel_id=1, source_target_pairs={{0,8},{8,0},{1,9},{9,1},{2,10},{10,2},{3,11},{11,3},{4,12},{12,4},... | collective-permute-start | bytes 405512 | tf_op jit(solution)/shard_map/ppermute | solution.py:191
  34.8 13.9 %all-to-all-start.1 = ((bf16[16,8,2176]{2,1,0:T(8,128)(2,1)}), bf16[16,8,2176]{2,1,0:T(8,128)(2,1)S(1)}, u32[]{:S(2)}, u32[]{:S(2)}) async-start(bf16[16,8,2176]{2,1,0:T(8,128)(2,1)} %bitcast.8), calls=%async_computation.1 | async-start | bytes 1114112 | tf_op jit(solution)/shard_map/all_to_all | solution.py:214
  48.9 7.2 %collective-permute-start.1 = (bf16[16,2176]{1,0:T(8,128)(2,1)S(1)}, bf16[16,2176]{1,0:T(8,128)(2,1)S(1)}, u32[]{:S(2)}, u32[]{:S(2)}) collective-permute-start(bf16[16,2176]{1,0:T(8,128)(2,1)S(1)} %get-tuple-element.27), channel_id=1, source_target_pairs={{0,8},{8,0},{1,9},{9,1},{2,10},{10,2},{3,11},{11,3},{4,12},{12,4},... | collective-permute-start | bytes 208904 | tf_op jit(solution)/shard_map/ppermute | solution.py:225

commit v8 on v7

--- a/solution.py
+++ b/solution.py
@@ -25,73 +25,68 @@
     return tuple(lax.broadcasted_iota(jnp.int32, (size, size), axis) for axis in (0, 1))
 
 
-def join_kernel(route_hbm, prob_hbm, tok_hbm, cot_hbm, out_ref, route_v, prob_v, sems):
-    tok_dev, features = tok_hbm.shape
-    small = [
+def tail_kernel(route_hbm, prob_hbm, out_ref, route_v, prob_v, sems):
+    tok_dev = out_ref.shape[0]
+    copies = [
         pltpu.make_async_copy(route_hbm, route_v, sems.at[0]),
         pltpu.make_async_copy(prob_hbm, prob_v, sems.at[1]),
     ]
-    large = [
-        pltpu.make_async_copy(tok_hbm, out_ref.at[:, pl.ds(0, features)], sems.at[2]),
-        pltpu.make_async_copy(cot_hbm, out_ref.at[:, pl.ds(features, features)], sems.at[3]),
-    ]
-    for copy in small + large:
+    for copy in copies:
         copy.start()
     own = lax.broadcasted_iota(jnp.int32, route_v.shape, 0) == lax.axis_index("dp")
     here, there = square(tok_dev)
-    for copy in small:
+    for copy in copies:
         copy.wait()
     route = jnp.sum(jnp.where(own, route_v[...].astype(F32), 0.0), axis=0, keepdims=True)
     prob = jnp.sum(jnp.where(own, prob_v[...].astype(F32), 0.0), axis=0, keepdims=True)
     route = jnp.sum(jnp.where(here == there, route, 0.0), axis=1, keepdims=True)
     prob = jnp.sum(jnp.where(here == there, prob, 0.0), axis=1, keepdims=True)
     lane = lax.broadcasted_iota(jnp.int32, (tok_dev, LANES), 1)
-    tail = jnp.where(lane == 0, prob, jnp.where(lane == 1, route, 0.0))
-    out_ref[:, 2 * features :] = tail.astype(BF16)
-    for copy in large:
+    out_ref[...] = jnp.where(lane == 0, prob, jnp.where(lane == 1, route, 0.0)).astype(BF16)
+
+
+def load_kernel(*refs):
+    ins, outs, down_v, sems = refs[:5], refs[5:11], refs[11], refs[12]
+    hidden = ins[2].shape[0]
+    joined = outs[2]
+    places = (*outs[:2], joined.at[pl.ds(0, hidden), :], joined.at[pl.ds(hidden, hidden), :], down_v)
+    copies = [pltpu.make_async_copy(a, b, sems.at[i]) for i, (a, b) in enumerate(zip(ins, places))]
+    for copy in copies:
+        copy.start()
+    for copy in copies:
         copy.wait()
-
-
-def load_kernel(gate_hbm, up_hbm, down_hbm, rows_ref, gate_t, up_t, down_t, down_v, sems):
-    hidden = gate_hbm.shape[0]
-    places = (rows_ref.at[pl.ds(0, hidden), :], rows_ref.at[pl.ds(hidden, hidden), :], down_v)
-    copies = [
-        pltpu.make_async_copy(a, b, sems.at[i])
-        for i, (a, b) in enumerate(zip((gate_hbm, up_hbm, down_hbm), places))
-    ]
-    for copy in copies:
-        copy.start()
-    for copy, place, turned in zip(copies, places, (gate_t, up_t, down_t)):
-        copy.wait()
+    for place, turned in zip(places[2:], outs[3:]):
         turned[...] = place[...].T
 
 
-def pack_kernel(slots, own_ref, other_ref, w0, w1, w2, w3, send_ref, pick_ref):
-    del w0, w1, w2, w3
-    tok_dev, width = own_ref.shape
+def pack_kernel(slots, *refs):
+    own, other, (send_ref, pick_ref) = refs[:3], refs[3:6], refs[-2:]
+    tok_dev, features = own[0].shape
     block = pick_ref.shape[0]
     groups = send_ref.shape[0] // block
     half = block // (2 * slots)
     top = lax.axis_index("top")
     here, there = square(tok_dev)
     place = lax.broadcasted_iota(jnp.int32, (block, tok_dev), 0)
-    sent = jnp.zeros((block, width), F32)
     picks = []
-    for rows_ref, origin in ((own_ref, top), (other_ref, 1 - top)):
-        column = rows_ref[:, width - LANES + 1 : width - LANES + 2].astype(F32)
+    for tail_ref, origin in ((own[2], top), (other[2], 1 - top)):
+        column = tail_ref[:, 1:2].astype(F32)
         row = jnp.sum(jnp.where(here == there, column, 0.0), axis=0, keepdims=True)
         rank = jnp.sum(jnp.where((column == row) & (here < there), 1.0, 0.0), axis=0, keepdims=True)
         low = row.astype(jnp.int32) - top * half
         target = low * (2 * slots) + origin * slots + rank.astype(jnp.int32)
         target = jnp.where((low >= 0) & (low < half), target, -1)
-        pick = (place == target).astype(F32).astype(BF16)
-        sent += dot(pick, rows_ref[...], (1, 0))
-        picks.append(pick)
+        picks.append((place == target).astype(F32).astype(BF16))
     pick_ref[:, :tok_dev] = picks[0]
     pick_ref[:, tok_dev:] = picks[1]
-    sent = sent.astype(BF16)
-    for g in range(groups):
-        send_ref[g * block : (g + 1) * block, :] = sent
+    start = 0
+    for own_ref, other_ref in zip(own, other):
+        end = start + own_ref.shape[1]
+        sent = dot(picks[0], own_ref[...], (1, 0)) + dot(picks[1], other_ref[...], (1, 0))
+        sent = sent.astype(BF16)
+        for g in range(groups):
+            send_ref[g * block : (g + 1) * block, start:end] = sent
+        start = end
 
 
 def expert_kernel(chunk, got_ref, rows_ref, gate_t, up_t, down_t, reply_ref, dg_ref, du_ref, sa_ref):
@@ -177,32 +172,36 @@
     chunk = min(rows, 256)
     width = 2 * features + LANES
 
-    (own,) = call(
-        join_kernel,
-        [HBM] * 4,
-        [near((tok_dev, width))],
-        *far(routes, gate_prob, tokens[0], cotangent[0]),
+    x, dy = tokens[0], cotangent[0]
+    others = [lax.ppermute(a, "top", SWAP) for a in (x, dy)]
+    (tail,) = call(
+        tail_kernel,
+        [HBM] * 2,
+        [near((tok_dev, LANES))],
+        *far(routes, gate_prob),
         scratch=[
             pltpu.VMEM(routes.shape, routes.dtype),
             pltpu.VMEM(gate_prob.shape, gate_prob.dtype),
-            pltpu.SemaphoreType.DMA((4,)),
+            pltpu.SemaphoreType.DMA((2,)),
         ],
     )
-    other = lax.ppermute(own, "top", SWAP)
-    weights = call(
+    others.append(lax.ppermute(tail, "top", SWAP))
+    *own, joined, gate_t, up_t, down_t = call(
         load_kernel,
-        [HBM] * 3,
-        [near((2 * hidden, features))] + [near((features, hidden))] * 3,
-        *far(w_gate[0], w_up[0], w_down[0]),
-        scratch=[pltpu.VMEM((hidden, features), BF16), pltpu.SemaphoreType.DMA((3,))],
+        [HBM] * 5,
+        [near((tok_dev, features))] * 2
+        + [near((2 * hidden, features))]
+        + [near((features, hidden))] * 3,
+        *far(x, dy, w_gate[0], w_up[0], w_down[0]),
+        scratch=[pltpu.VMEM((hidden, features), BF16), pltpu.SemaphoreType.DMA((5,))],
         cost=pl.CostEstimate(flops=0, transcendentals=0, bytes_accessed=16 * hidden * features),
     )
-    weights = [fetched(a) for a in weights]
+    weights = [fetched(a) for a in (joined, gate_t, up_t, down_t)]
     send, pick = call(
         lambda *refs: pack_kernel(slots, *refs),
-        [VMEM] * 6,
+        [VMEM] * 10,
         [near((rows, width)), near((block, 2 * tok_dev))],
-        fetched(own), fetched(other), *weights,
+        *[fetched(a) for a in (*own, tail, *others)], *weights,
     )
     got = lax.all_to_all(send, HALF_AXES, split_axis=0, concat_axis=0, tiled=True)
     reply, d_gate, d_up, scaled_act = call(

time: 57.6 us -> 57.8 us (level)
  waiting for transfers between devices: 11.9 us -> 9.52 us
  blocking collectives: 21 us -> 22.1 us
  Pallas kernels: 7.51 us -> 8.22 us
  starting transfers between devices: 10.3 us -> 11 us
    ppermute x1 -> x3, waiting for transfers between devices: 3.36 us -> 0.01 us  [the longest x2 0.01 us: body(): others = [lax.ppermute(a, 'top', SWAP) for a in (x, dy)]]
    ppermute x1 -> x3, starting transfers between devices: 3.2 us -> 5.63 us  [the longest x2 3.28 us: body(): others = [lax.ppermute(a, 'top', SWAP) for a in (x, dy)]]
    ppermute x1, starting transfers between devices: 3.16 us -> 1.44 us  [body(): lax.ppermute(given, 'top', SWAP)]
    all_to_all x1, blocking collectives: 21 us -> 22.1 us  [body(): lax.all_to_all(send, HALF_AXES, split_axis=0, concat_axis=0, tiled=True)]
    ppermute x1, waiting for transfers between devices: 2.29 us -> 3.27 us  [body(): lax.ppermute(given, 'top', SWAP)]
    pallas_call x6, Pallas kernels: 7.51 us -> 8.22 us  [call(): pl.pallas_call(kernel, in_specs=in_specs, scratch_shapes=scratch, out_spe...]
  transfers between devices with their start and end apart: 3 -> 5, of which waited for: 3 -> 2; matrix products, arithmetic and copies ran while one was open for 10% -> 9% of each run, Pallas kernels for 5% -> 8%
where the time goes in v8:
time: 57.8 us; the launch traced here: 57 us
  blocking collectives  22.1 us (38%)
  starting transfers between devices  11 us (19%)
  waiting for transfers between devices  9.52 us (16%)
  Pallas kernels  8.22 us (14%)
  matrix products  5.22 us (9%)
  between operations  0.7 us (1%)
    all_to_all x1, blocking collectives, body(): lax.all_to_all(send, HALF_AXES, split_axis=0, concat_axis=0, tiled=True)  22.1 us
    pallas_call x6, Pallas kernels, call(): pl.pallas_call(kernel, in_specs=in_specs, scratch_shapes=scratch, out_spe...  8.22 us
    all_to_all x1, waiting for transfers between devices, body(): lax.all_to_all(reply, HALF_AXES, split_axis=0, concat_axis=0, tiled=True)  6.24 us
    dot_general x3, matrix products, body(): jnp.einsum('rh,rd->hd', left, right, preferred_element_type=F32)  5.22 us
    all_to_all x1, starting transfers between devices, body(): lax.all_to_all(reply, HALF_AXES, split_axis=0, concat_axis=0, tiled=True)  3.94 us
    ppermute x2, starting transfers between devices, body(): others = [lax.ppermute(a, 'top', SWAP) for a in (x, dy)]  3.28 us
    ppermute x1, waiting for transfers between devices, body(): lax.ppermute(given, 'top', SWAP)  3.27 us
    ppermute x1, starting transfers between devices, body(): others.append(lax.ppermute(tail, 'top', SWAP))  2.35 us
  transfers between devices with their start and end apart: 5, of which 2 were waited for; matrix products, arithmetic and copies ran while one was open for 9% of the time, Pallas kernels for 8%

profile of v8, /device:TPU:1, one launch (start us, length us, event | category | flops | bytes accessed | tf_op | source)
XLA Modules:
  0.0 57.0 jit_solution(8217990439837935552)
XLA Ops:
  0.6 3.2 %collective-permute-start = (bf16[16,2048]{1,0:T(8,128)(2,1)}, bf16[16,2048]{1,0:T(8,128)(2,1)S(1)}, u32[]{:S(2)}, u32[]{:S(2)}) collective-permute-start(bf16[16,2048]{1,0:T(8,128)(2,1)} %bitcast.30), channel_id=1, source_target_pairs={{0,8},{8,0},{1,9},{9,1},{2,10},{10,2},{3,11},{11,3},{4,12},{12,4},... | collective-permute-start | bytes 196616 | tf_op jit(solution)/shard_map/ppermute | solution.py:176
  3.8 0.1 collective-permute-start.1
  3.9 0.8 %shard_map.111.refs_2_ = bf16[16,128]{1,0:T(8,128)(2,1)S(1)} custom-call(s32[2,16]{1,0:T(2,128)} %route_hbm.1, bf16[2,16]{1,0:T(2,128)(2,1)} %prob_hbm.1), custom_call_target="tpu_custom_call" | custom-call | tf_op jit(solution)/shard_map/pallas_call | solution.py:153
  4.7 2.3 %collective-permute-start.2 = (bf16[16,128]{1,0:T(8,128)(2,1)S(1)}, bf16[16,128]{1,0:T(8,128)(2,1)S(1)}, u32[]{:S(2)}, u32[]{:S(2)}) collective-permute-start(bf16[16,128]{1,0:T(8,128)(2,1)S(1)} %shard_map.111.refs_2_), channel_id=1, source_target_pairs={{0,8},{8,0},{1,9},{9,1},{2,10},{10,2},{3,11},{11,3},{4,12},{12,4},... | collective-permute-start | bytes 12296 | tf_op jit(solution)/shard_map/ppermute | solution.py:188
  7.1 3.7 %shard_map.110 = (bf16[16,2048]{1,0:T(8,128)(2,1)S(1)}, bf16[16,2048]{1,0:T(8,128)(2,1)S(1)}, bf16[768,2048]{1,0:T(8,128)(2,1)S(1)}, bf16[2048,384]{1,0:T(8,128)...) custom-call(bf16[16,2048]{1,0:T(8,128)(2,1)} %bitcast.31, bf16[16,2048]{1,0:T(8,128)(2,1)} %bitcast.33, ...), custom_call_target="tpu_custom_call" | custom-call | bytes 12582912 | tf_op jit(solution)/shard_map/pallas_call | solution.py:153
  10.8 0.0 collective-permute-done.2.refs_5_
  10.8 0.0 collective-permute-done.refs_3_
  10.8 0.0 collective-permute-done.1.refs_4_
  10.8 0.5 shard_map.112
  11.4 22.1 %all_to_all.22 = bf16[16,8,4224]{2,1,0:T(8,128)(2,1)S(1)} all-to-all(bf16[16,8,4224]{2,1,0:T(8,128)(2,1)S(1)} %bitcast.25), channel_id=1, replica_groups=mesh['dp'=2,'top'=2,'low'=8] {'dp','low'}, dimensions={0} | all-to-all | bytes 2162688 | tf_op jit(solution)/shard_map/all_to_all | solution.py:206
  33.5 2.3 %shard_map.113 = (bf16[128,2176]{1,0:T(8,128)(2,1)}, bf16[128,384]{1,0:T(8,128)(2,1)S(1)}, bf16[128,384]{1,0:T(8,128)(2,1)S(1)}, bf16[128,384]{1,0:T(8,128)(2,1)S(1)}) custom-call(bf16[128,4224]{1,0:T(8,128)(2,1)S(1)} %bitcast.20, bf16[768,2048]{1,0:T(8,128)(2,1)S(1)} %get-tuple-element.23.refs_6_.refs_1_, ...), custom_call_target="tpu_custom_call" | custom-call | tf_op jit(solution)/shard_map/pallas_call | solution.py:153
  35.8 3.9 %all-to-all-start.1 = ((bf16[16,8,2176]{2,1,0:T(8,128)(2,1)}), bf16[16,8,2176]{2,1,0:T(8,128)(2,1)S(1)}, u32[]{:S(2)}, u32[]{:S(2)}) async-start(bf16[16,8,2176]{2,1,0:T(8,128)(2,1)} %bitcast.8), calls=%async_computation.1 | async-start | bytes 1114112 | tf_op jit(solution)/shard_map/all_to_all | solution.py:213
  39.7 0.1 copy.12
  39.8 0.1 tile.10.pick_ref
  39.9 1.7 %fusion = bf16[1,384,2048]{2,1,0:T(8,128)(2,1)} fusion(bf16[128,384]{1,0:T(8,128)(2,1)S(1)} %get-tuple-element.34, bf16[128,4224]{1,0:T(8,128)(2,1)S(1)} %bitcast.21), kind=kOutput, calls=%fused_computation.3 | convolution fusion | flops 202113024 | bytes 2195456 | tf_op jit(solution)/shard_map/rh,rd->hd/dot_general | solution.py:228
  41.7 1.7 %fusion.1 = bf16[1,384,2048]{2,1,0:T(8,128)(2,1)} fusion(bf16[128,384]{1,0:T(8,128)(2,1)S(1)} %get-tuple-element.35, bf16[128,4224]{1,0:T(8,128)(2,1)S(1)} %bitcast.22), kind=kOutput, calls=%fused_computation.4 | convolution fusion | flops 202113024 | bytes 2195456 | tf_op jit(solution)/shard_map/rh,rd->hd/dot_general | solution.py:228
  43.4 6.2 %all-to-all-done.1 = bf16[16,8,2176]{2,1,0:T(8,128)(2,1)S(1)} async-done(((bf16[16,8,2176]{2,1,0:T(8,128)(2,1)}), bf16[16,8,2176]{2,1,0:T(8,128)(2,1)S(1)}, u32[]{:S(2)}, u32[]{:S(2)}) %all-to-all-start.1) | async-done | bytes 557088 | tf_op jit(solution)/shard_map/all_to_all | solution.py:213
  49.6 0.2 shard_map.114
  49.9 1.4 %collective-permute-start.3 = (bf16[16,2176]{1,0:T(8,128)(2,1)S(1)}, bf16[16,2176]{1,0:T(8,128)(2,1)S(1)}, u32[]{:S(2)}, u32[]{:S(2)}) collective-permute-start(bf16[16,2176]{1,0:T(8,128)(2,1)S(1)} %get-tuple-element.31), channel_id=1, source_target_pairs={{0,8},{8,0},{1,9},{9,1},{2,10},{10,2},{3,11},{11,3},{4,12},{12,4},... | collective-permute-start | bytes 208904 | tf_op jit(solution)/shard_map/ppermute | solution.py:224
  51.3 1.7 %fusion.2 = bf16[1,384,2048]{2,1,0:T(8,128)(2,1)} fusion(bf16[128,384]{1,0:T(8,128)(2,1)S(1)} %get-tuple-element.36, bf16[128,4224]{1,0:T(8,128)(2,1)S(1)} %bitcast.23), kind=kOutput, calls=%fused_computation.5 | convolution fusion | flops 202113024 | bytes 2195456 | tf_op jit(solution)/shard_map/rh,rd->hd/dot_general | solution.py:228
  53.0 3.3 %collective-permute-done.3.other_ref = bf16[16,2176]{1,0:T(8,128)(2,1)S(1)} collective-permute-done((bf16[16,2176]{1,0:T(8,128)(2,1)S(1)}, bf16[16,2176]{1,0:T(8,128)(2,1)S(1)}, u32[]{:S(2)}, u32[]{:S(2)}) %collective-permute-start.3) | collective-permute-done | bytes 69664 | tf_op jit(solution)/shard_map/ppermute | solution.py:224
  56.3 0.7 %shard_map.115 = (bf16[16,2048]{1,0:T(8,128)(2,1)}, f32[1,16]{1,0:T(1,128)}) custom-call(bf16[16,2176]{1,0:T(8,128)(2,1)S(1)} %get-tuple-element.30.own_ref, bf16[16,2176]{1,0:T(8,128)(2,1)S(1)} %collective-permute-done.3.other_ref), custom_call_target="tpu_custom_call" | custom-call | tf_op jit(solution)/shard_map/pallas_call | solution.py:153
  (1 shorter events, 0.0 us)
Async XLA Ops:
  0.6 10.2 %collective-permute-start = (bf16[16,2048]{1,0:T(8,128)(2,1)}, bf16[16,2048]{1,0:T(8,128)(2,1)S(1)}, u32[]{:S(2)}, u32[]{:S(2)}) collective-permute-start(bf16[16,2048]{1,0:T(8,128)(2,1)} %bitcast.30), channel_id=1, source_target_pairs={{0,8},{8,0},{1,9},{9,1},{2,10},{10,2},{3,11},{11,3},{4,12},{12,4},... | collective-permute-start | bytes 196616 | tf_op jit(solution)/shard_map/ppermute | solution.py:176
  3.8 7.0 %collective-permute-start.1 = (bf16[16,2048]{1,0:T(8,128)(2,1)}, bf16[16,2048]{1,0:T(8,128)(2,1)S(1)}, u32[]{:S(2)}, u32[]{:S(2)}) collective-permute-start(bf16[16,2048]{1,0:T(8,128)(2,1)} %bitcast.32), channel_id=1, source_target_pairs={{0,8},{8,0},{1,9},{9,1},{2,10},{10,2},{3,11},{11,3},{4,12},{12,4},... | collective-permute-start | bytes 196616 | tf_op jit(solution)/shard_map/ppermute | solution.py:176
  4.7 6.1 %collective-permute-start.2 = (bf16[16,128]{1,0:T(8,128)(2,1)S(1)}, bf16[16,128]{1,0:T(8,128)(2,1)S(1)}, u32[]{:S(2)}, u32[]{:S(2)}) collective-permute-start(bf16[16,128]{1,0:T(8,128)(2,1)S(1)} %shard_map.111.refs_2_), channel_id=1, source_target_pairs={{0,8},{8,0},{1,9},{9,1},{2,10},{10,2},{3,11},{11,3},{4,12},{12,4},... | collective-permute-start | bytes 12296 | tf_op jit(solution)/shard_map/ppermute | solution.py:188
  35.8 13.9 %all-to-all-start.1 = ((bf16[16,8,2176]{2,1,0:T(8,128)(2,1)}), bf16[16,8,2176]{2,1,0:T(8,128)(2,1)S(1)}, u32[]{:S(2)}, u32[]{:S(2)}) async-start(bf16[16,8,2176]{2,1,0:T(8,128)(2,1)} %bitcast.8), calls=%async_computation.1 | async-start | bytes 1114112 | tf_op jit(solution)/shard_map/all_to_all | solution.py:213
  49.9 6.4 %collective-permute-start.3 = (bf16[16,2176]{1,0:T(8,128)(2,1)S(1)}, bf16[16,2176]{1,0:T(8,128)(2,1)S(1)}, u32[]{:S(2)}, u32[]{:S(2)}) collective-permute-start(bf16[16,2176]{1,0:T(8,128)(2,1)S(1)} %get-tuple-element.31), channel_id=1, source_target_pairs={{0,8},{8,0},{1,9},{9,1},{2,10},{10,2},{3,11},{11,3},{4,12},{12,4},... | collective-permute-start | bytes 208904 | tf_op jit(solution)/shard_map/ppermute | solution.py:224

commit v9 on v7

--- a/solution.py
+++ b/solution.py
@@ -9,6 +9,7 @@
 from jax.sharding import PartitionSpec as P
 
 HALF_AXES = ("dp", "low")
+ALL_AXES = ("dp", "low", "top")
 SWAP = [(0, 1), (1, 0)]
 LANES = 128
 NEAR_SIZE = 2 << 20
@@ -76,7 +77,6 @@
     here, there = square(tok_dev)
     place = lax.broadcasted_iota(jnp.int32, (block, tok_dev), 0)
     sent = jnp.zeros((block, width), F32)
-    picks = []
     for rows_ref, origin in ((own_ref, top), (other_ref, 1 - top)):
         column = rows_ref[:, width - LANES + 1 : width - LANES + 2].astype(F32)
         row = jnp.sum(jnp.where(here == there, column, 0.0), axis=0, keepdims=True)
@@ -86,15 +86,18 @@
         target = jnp.where((low >= 0) & (low < half), target, -1)
         pick = (place == target).astype(F32).astype(BF16)
         sent += dot(pick, rows_ref[...], (1, 0))
-        picks.append(pick)
-    pick_ref[:, :tok_dev] = picks[0]
-    pick_ref[:, tok_dev:] = picks[1]
+        if rows_ref is own_ref:
+            upper = ((low >= half) | (low < 0)).astype(jnp.int32)
+            upper = jnp.where(upper == 1, 1 - top, top)
+            low = low + (top - upper) * half
+            target = (low * 2 + upper) * slots + rank.astype(jnp.int32)
+            pick_ref[...] = (place == target).astype(F32).astype(BF16)
     sent = sent.astype(BF16)
     for g in range(groups):
         send_ref[g * block : (g + 1) * block, :] = sent
 
 
-def expert_kernel(chunk, got_ref, rows_ref, gate_t, up_t, down_t, reply_ref, dg_ref, du_ref, sa_ref):
+def expert_kernel(slots, chunk, got_ref, rows_ref, gate_t, up_t, down_t, reply_ref, dg_ref, du_ref, sa_ref):
     features = rows_ref.shape[1]
     mine = lax.axis_index("dp")
     lane = lax.broadcasted_iota(jnp.int32, (chunk, LANES), 1)
@@ -120,19 +123,16 @@
         du_ref[at, :] = d_up
         sa_ref[at, :] = (weight * active).astype(BF16)
         grad = dot(jnp.concatenate([d_gate, d_up], axis=1), rows_ref[...], (1, 0))
-        reply_ref[at, :features] = grad.astype(BF16)
-        reply_ref[at, features:] = jnp.where(lane == mine, part, 0.0).astype(BF16)
-
-
-def combine_kernel(pick_ref, back_ref, own_ref, other_ref):
-    total = dot(pick_ref[...], back_ref[...], (1, 0)).astype(BF16)
-    own_ref[...] = total[: own_ref.shape[0]]
-    other_ref[...] = total[own_ref.shape[0] :]
-
-
-def finish_kernel(own_ref, other_ref, tok_ref, prob_ref):
+        tail = jnp.where(lane == mine, part, 0.0)
+        for i in range(chunk // slots):
+            to, rows = step * (chunk // slots) + i, slice(i * slots, (i + 1) * slots)
+            reply_ref[to, :, :features] = grad[rows].astype(BF16)
+            reply_ref[to, :, features:] = tail[rows].astype(BF16)
+
+
+def unpack_kernel(pick_ref, back_ref, tok_ref, prob_ref):
     tok_dev, features = tok_ref.shape
-    total = own_ref[...].astype(F32) + other_ref[...].astype(F32)
+    total = dot(pick_ref[...], back_ref[...], (1, 0))
     tok_ref[...] = total[:, :features].astype(BF16)
     part = jnp.sum(total[:, features:], axis=1, keepdims=True)
     here, there = square(tok_dev)
@@ -201,28 +201,22 @@
     send, pick = call(
         lambda *refs: pack_kernel(slots, *refs),
         [VMEM] * 6,
-        [near((rows, width)), near((block, 2 * tok_dev))],
+        [near((rows, width)), near((block, tok_dev))],
         fetched(own), fetched(other), *weights,
     )
     got = lax.all_to_all(send, HALF_AXES, split_axis=0, concat_axis=0, tiled=True)
     reply, d_gate, d_up, scaled_act = call(
-        lambda *refs: expert_kernel(chunk, *refs),
+        lambda *refs: expert_kernel(slots, chunk, *refs),
         [VMEM] * 5,
-        [near((rows, features + LANES))] + [near((rows, hidden))] * 3,
+        [near((rows // slots, slots, features + LANES))] + [near((rows, hidden))] * 3,
         fetched(got), *weights,
     )
-    back = lax.all_to_all(reply, HALF_AXES, split_axis=0, concat_axis=0, tiled=True)
-    kept, given = call(
-        combine_kernel,
-        [VMEM] * 2,
-        [near((tok_dev, features + LANES))] * 2,
-        jnp.tile(pick.T, (1, groups)), back,
-    )
+    back = lax.all_to_all(reply, ALL_AXES, split_axis=0, concat_axis=0, tiled=True)
     grad_tokens, grad_prob = call(
-        finish_kernel,
+        unpack_kernel,
         [VMEM] * 2,
         [jax.ShapeDtypeStruct((tok_dev, features), BF16), jax.ShapeDtypeStruct((1, tok_dev), F32)],
-        fetched(kept), fetched(lax.ppermute(given, "top", SWAP)),
+        jnp.tile(pick.T, (1, groups)), back.reshape(rows, features + LANES),
     )
     rows_x, rows_dy = got[:, :features], got[:, features : 2 * features]
     weight_grads = [

time: 57.6 us -> 56.9 us (0.988); the launches traced: 56.7 us -> 56.6 us
  starting transfers between devices: 10.3 us -> 7.25 us
  waiting for transfers between devices: 11.9 us -> 14.7 us
    all_to_all x1, waiting for transfers between devices: 6.24 us -> 11.3 us  [body(): lax.all_to_all(reply, ALL_AXES, split_axis=0, concat_axis=0, tiled=True)]
    ppermute x1 -> x0, starting transfers between devices: 3.16 us -> none  [body(): lax.ppermute(given, 'top', SWAP)]
    ppermute x1 -> x0, waiting for transfers between devices: 2.29 us -> none  [body(): lax.ppermute(given, 'top', SWAP)]
    pallas_call x6 -> x5, Pallas kernels: 7.51 us -> 7.51 us  [call(): pl.pallas_call(kernel, in_specs=in_specs, scratch_shapes=scratch, out_spe...]
  transfers between devices with their start and end apart: 3 -> 2, of which waited for: 3 -> 2; matrix products, arithmetic and copies ran while one was open for 10% -> 10% of each run, Pallas kernels for 5% -> 5%
where the time goes in v9:
time: 56.9 us; the launch traced here: 56.6 us
  blocking collectives  21 us (37%)
  waiting for transfers between devices  14.7 us (26%)
  Pallas kernels  7.51 us (13%)
  starting transfers between devices  7.25 us (13%)
  matrix products  5.22 us (9%)
  between operations  0.68 us (1%)
    all_to_all x1, blocking collectives, body(): lax.all_to_all(send, HALF_AXES, split_axis=0, concat_axis=0, tiled=True)  21 us
    all_to_all x1, waiting for transfers between devices, body(): lax.all_to_all(reply, ALL_AXES, split_axis=0, concat_axis=0, tiled=True)  11.3 us
    pallas_call x5, Pallas kernels, call(): pl.pallas_call(kernel, in_specs=in_specs, scratch_shapes=scratch, out_spe...  7.51 us
    dot_general x3, matrix products, body(): jnp.einsum('rh,rd->hd', left, right, preferred_element_type=F32)  5.22 us
    all_to_all x1, starting transfers between devices, body(): lax.all_to_all(reply, ALL_AXES, split_axis=0, concat_axis=0, tiled=True)  4.05 us
    ppermute x1, waiting for transfers between devices, body(): other = lax.ppermute(own, 'top', SWAP)  3.36 us
    ppermute x1, starting transfers between devices, body(): other = lax.ppermute(own, 'top', SWAP)  3.2 us
  transfers between devices with their start and end apart: 2, of which 2 were waited for; matrix products, arithmetic and copies ran while one was open for 10% of the time, Pallas kernels for 5%

profile of v9, /device:TPU:1, one launch (start us, length us, event | category | flops | bytes accessed | tf_op | source)
XLA Modules:
  0.0 56.6 jit_solution(11583946758004431019)
XLA Ops:
  0.6 0.9 %shard_map.110.refs_0_ = bf16[16,4224]{1,0:T(8,128)(2,1)S(1)} custom-call(s32[2,16]{1,0:T(2,128)} %route_hbm.1, bf16[2,16]{1,0:T(2,128)(2,1)} %prob_hbm.1, bf16[16,2048]{1,0:T(8,128)(2,1)} %bitcast.27, bf16[16,2048]{1,0:T(8,128)(2,1)} %bitcast.28), custom_call_target="tpu_custom_call" | custom-call | tf_op jit(solution)/shard_map/pallas_call | solution.py:158
  1.6 3.2 %collective-permute-start = (bf16[16,4224]{1,0:T(8,128)(2,1)S(1)}, bf16[16,4224]{1,0:T(8,128)(2,1)S(1)}, u32[]{:S(2)}, u32[]{:S(2)}) collective-permute-start(bf16[16,4224]{1,0:T(8,128)(2,1)S(1)} %shard_map.110.refs_0_), channel_id=1, source_target_pairs={{0,8},{8,0},{1,9},{9,1},{2,10},{10,2},{3,11},{11,3},{4,12},{12,4},... | collective-permute-start | bytes 405512 | tf_op jit(solution)/shard_map/ppermute | solution.py:191
  4.8 2.8 %shard_map.111 = (bf16[768,2048]{1,0:T(8,128)(2,1)S(1)}, bf16[2048,384]{1,0:T(8,128)(2,1)S(1)}, bf16[2048,384]{1,0:T(8,128)(2,1)S(1)}, bf16[2048,384]{1,0:T(8,128)(2,1)S(1)}) custom-call(bf16[384,2048]{1,0:T(8,128)(2,1)} %bitcast.24, bf16[384,2048]{1,0:T(8,128)(2,1)} %bitcast.25, bf16[384,2048]{1,0:T(8,128)(2,1)} %bitcast.26), custom_call_target="tpu_custom_call" | custom-call | bytes 12582912 | tf_op jit(solution)/shard_map/pallas_call | solution.py:158
  7.6 3.4 %collective-permute-done.refs_1_ = bf16[16,4224]{1,0:T(8,128)(2,1)S(1)} collective-permute-done((bf16[16,4224]{1,0:T(8,128)(2,1)S(1)}, bf16[16,4224]{1,0:T(8,128)(2,1)S(1)}, u32[]{:S(2)}, u32[]{:S(2)}) %collective-permute-start) | collective-permute-done | bytes 135200 | tf_op jit(solution)/shard_map/ppermute | solution.py:191
  11.0 0.5 shard_map.112
  11.5 21.0 %all_to_all.16 = bf16[16,8,4224]{2,1,0:T(8,128)(2,1)S(1)} all-to-all(bf16[16,8,4224]{2,1,0:T(8,128)(2,1)S(1)} %bitcast.22), channel_id=1, replica_groups=mesh['dp'=2,'top'=2,'low'=8] {'dp','low'}, dimensions={0} | all-to-all | bytes 2162688 | tf_op jit(solution)/shard_map/all_to_all | solution.py:207
  32.5 2.4 %shard_map.113 = (bf16[32,4,2176]{2,1,0:T(4,128)(2,1)}, bf16[128,384]{1,0:T(8,128)(2,1)S(1)}, bf16[128,384]{1,0:T(8,128)(2,1)S(1)}, bf16[128,384]{1,0:T(8,128)(2,1)S(1)}) custom-call(bf16[128,4224]{1,0:T(8,128)(2,1)S(1)} %bitcast.18, bf16[768,2048]{1,0:T(8,128)(2,1)S(1)} %get-tuple-element.17.refs_2_.refs_1_, ...), custom_call_target="tpu_custom_call" | custom-call | tf_op jit(solution)/shard_map/pallas_call | solution.py:158
  34.9 4.1 %all-to-all-start.1 = ((bf16[32,4,2176]{2,1,0:T(4,128)(2,1)}), bf16[32,4,2176]{2,1,0:T(4,128)(2,1)S(1)}, u32[]{:S(2)}, u32[]{:S(2)}) async-start(bf16[32,4,2176]{2,1,0:T(4,128)(2,1)} %get-tuple-element.23), calls=%async_computation.1 | async-start | bytes 1114112 | tf_op jit(solution)/shard_map/all_to_all | solution.py:214
  38.9 0.1 copy.12
  39.0 0.1 tile.10.pick_ref
  39.1 1.7 %fusion = bf16[1,384,2048]{2,1,0:T(8,128)(2,1)} fusion(bf16[128,384]{1,0:T(8,128)(2,1)S(1)} %get-tuple-element.26, bf16[128,4224]{1,0:T(8,128)(2,1)S(1)} %bitcast.19), kind=kOutput, calls=%fused_computation.3 | convolution fusion | flops 202113024 | bytes 2195456 | tf_op jit(solution)/shard_map/rh,rd->hd/dot_general | solution.py:223
  40.8 1.7 %fusion.1 = bf16[1,384,2048]{2,1,0:T(8,128)(2,1)} fusion(bf16[128,384]{1,0:T(8,128)(2,1)S(1)} %get-tuple-element.27, bf16[128,4224]{1,0:T(8,128)(2,1)S(1)} %bitcast.20), kind=kOutput, calls=%fused_computation.4 | convolution fusion | flops 202113024 | bytes 2195456 | tf_op jit(solution)/shard_map/rh,rd->hd/dot_general | solution.py:223
  42.6 1.7 %fusion.2 = bf16[1,384,2048]{2,1,0:T(8,128)(2,1)} fusion(bf16[128,384]{1,0:T(8,128)(2,1)S(1)} %get-tuple-element.28, bf16[128,4224]{1,0:T(8,128)(2,1)S(1)} %bitcast.21), kind=kOutput, calls=%fused_computation.5 | convolution fusion | flops 202113024 | bytes 2195456 | tf_op jit(solution)/shard_map/rh,rd->hd/dot_general | solution.py:223
  44.3 11.3 %all-to-all-done.1 = bf16[32,4,2176]{2,1,0:T(4,128)(2,1)S(1)} async-done(((bf16[32,4,2176]{2,1,0:T(4,128)(2,1)}), bf16[32,4,2176]{2,1,0:T(4,128)(2,1)S(1)}, u32[]{:S(2)}, u32[]{:S(2)}) %all-to-all-start.1) | async-done | bytes 557088 | tf_op jit(solution)/shard_map/all_to_all | solution.py:214
  55.7 0.1 reshape.19.back_ref
  55.8 0.8 %shard_map.114 = (bf16[16,2048]{1,0:T(8,128)(2,1)}, f32[1,16]{1,0:T(1,128)}) custom-call(bf16[16,128]{1,0:T(8,128)(2,1)S(1)} %tile.10.pick_ref, bf16[128,2176]{1,0:T(8,128)(2,1)S(1)} %reshape.19.back_ref), custom_call_target="tpu_custom_call" | custom-call | tf_op jit(solution)/shard_map/pallas_call | solution.py:158
  (1 shorter events, 0.0 us)
Async XLA Ops:
  1.6 9.4 %collective-permute-start = (bf16[16,4224]{1,0:T(8,128)(2,1)S(1)}, bf16[16,4224]{1,0:T(8,128)(2,1)S(1)}, u32[]{:S(2)}, u32[]{:S(2)}) collective-permute-start(bf16[16,4224]{1,0:T(8,128)(2,1)S(1)} %shard_map.110.refs_0_), channel_id=1, source_target_pairs={{0,8},{8,0},{1,9},{9,1},{2,10},{10,2},{3,11},{11,3},{4,12},{12,4},... | collective-permute-start | bytes 405512 | tf_op jit(solution)/shard_map/ppermute | solution.py:191
  34.9 20.8 %all-to-all-start.1 = ((bf16[32,4,2176]{2,1,0:T(4,128)(2,1)}), bf16[32,4,2176]{2,1,0:T(4,128)(2,1)S(1)}, u32[]{:S(2)}, u32[]{:S(2)}) async-start(bf16[32,4,2176]{2,1,0:T(4,128)(2,1)} %get-tuple-element.23), calls=%async_computation.1 | async-start | bytes 1114112 | tf_op jit(solution)/shard_map/all_to_all | solution.py:214

commit v10 on v8

--- a/solution.py
+++ b/solution.py
@@ -9,6 +9,7 @@
 from jax.sharding import PartitionSpec as P
 
 HALF_AXES = ("dp", "low")
+ALL_AXES = ("dp", "low", "top")
 SWAP = [(0, 1), (1, 0)]
 LANES = 128
 NEAR_SIZE = 2 << 20
@@ -53,10 +54,11 @@
     copies = [pltpu.make_async_copy(a, b, sems.at[i]) for i, (a, b) in enumerate(zip(ins, places))]
     for copy in copies:
         copy.start()
-    for copy in copies:
+    for copy, place, turned in zip(copies[2:], places[2:], outs[3:]):
         copy.wait()
-    for place, turned in zip(places[2:], outs[3:]):
         turned[...] = place[...].T
+    for copy in copies[:2]:
+        copy.wait()
 
 
 def pack_kernel(slots, *refs):
@@ -73,12 +75,16 @@
         column = tail_ref[:, 1:2].astype(F32)
         row = jnp.sum(jnp.where(here == there, column, 0.0), axis=0, keepdims=True)
         rank = jnp.sum(jnp.where((column == row) & (here < there), 1.0, 0.0), axis=0, keepdims=True)
+        rank = rank.astype(jnp.int32)
         low = row.astype(jnp.int32) - top * half
-        target = low * (2 * slots) + origin * slots + rank.astype(jnp.int32)
-        target = jnp.where((low >= 0) & (low < half), target, -1)
+        inside = (low >= 0) & (low < half)
+        target = jnp.where(inside, low * (2 * slots) + origin * slots + rank, -1)
         picks.append((place == target).astype(F32).astype(BF16))
-    pick_ref[:, :tok_dev] = picks[0]
-    pick_ref[:, tok_dev:] = picks[1]
+        if tail_ref is own[2]:
+            upper = jnp.where(inside, top, 1 - top)
+            low = low + (top - upper) * half
+            target = (low * 2 + upper) * slots + rank
+            pick_ref[...] = (place == target).astype(F32).astype(BF16)
     start = 0
     for own_ref, other_ref in zip(own, other):
         end = start + own_ref.shape[1]
@@ -89,7 +95,7 @@
         start = end
 
 
-def expert_kernel(chunk, got_ref, rows_ref, gate_t, up_t, down_t, reply_ref, dg_ref, du_ref, sa_ref):
+def expert_kernel(slots, chunk, got_ref, rows_ref, gate_t, up_t, down_t, reply_ref, dg_ref, du_ref, sa_ref):
     features = rows_ref.shape[1]
     mine = lax.axis_index("dp")
     lane = lax.broadcasted_iota(jnp.int32, (chunk, LANES), 1)
@@ -115,19 +121,16 @@
         du_ref[at, :] = d_up
         sa_ref[at, :] = (weight * active).astype(BF16)
         grad = dot(jnp.concatenate([d_gate, d_up], axis=1), rows_ref[...], (1, 0))
-        reply_ref[at, :features] = grad.astype(BF16)
-        reply_ref[at, features:] = jnp.where(lane == mine, part, 0.0).astype(BF16)
-
-
-def combine_kernel(pick_ref, back_ref, own_ref, other_ref):
-    total = dot(pick_ref[...], back_ref[...], (1, 0)).astype(BF16)
-    own_ref[...] = total[: own_ref.shape[0]]
-    other_ref[...] = total[own_ref.shape[0] :]
-
-
-def finish_kernel(own_ref, other_ref, tok_ref, prob_ref):
+        tail = jnp.where(lane == mine, part, 0.0)
+        for i in range(chunk // slots):
+            to, rows = step * (chunk // slots) + i, slice(i * slots, (i + 1) * slots)
+            reply_ref[to, :, :features] = grad[rows].astype(BF16)
+            reply_ref[to, :, features:] = tail[rows].astype(BF16)
+
+
+def unpack_kernel(pick_ref, back_ref, tok_ref, prob_ref):
     tok_dev, features = tok_ref.shape
-    total = own_ref[...].astype(F32) + other_ref[...].astype(F32)
+    total = dot(pick_ref[...], back_ref[...], (1, 0))
     tok_ref[...] = total[:, :features].astype(BF16)
     part = jnp.sum(total[:, features:], axis=1, keepdims=True)
     here, there = square(tok_dev)
@@ -200,28 +203,22 @@
     send, pick = call(
         lambda *refs: pack_kernel(slots, *refs),
         [VMEM] * 10,
-        [near((rows, width)), near((block, 2 * tok_dev))],
+        [near((rows, width)), near((block, tok_dev))],
         *[fetched(a) for a in (*own, tail, *others)], *weights,
     )
     got = lax.all_to_all(send, HALF_AXES, split_axis=0, concat_axis=0, tiled=True)
     reply, d_gate, d_up, scaled_act = call(
-        lambda *refs: expert_kernel(chunk, *refs),
+        lambda *refs: expert_kernel(slots, chunk, *refs),
         [VMEM] * 5,
-        [near((rows, features + LANES))] + [near((rows, hidden))] * 3,
+        [near((rows // slots, slots, features + LANES))] + [near((rows, hidden))] * 3,
         fetched(got), *weights,
     )
-    back = lax.all_to_all(reply, HALF_AXES, split_axis=0, concat_axis=0, tiled=True)
-    kept, given = call(
-        combine_kernel,
-        [VMEM] * 2,
-        [near((tok_dev, features + LANES))] * 2,
-        jnp.tile(pick.T, (1, groups)), back,
-    )
+    back = lax.all_to_all(reply, ALL_AXES, split_axis=0, concat_axis=0, tiled=True)
     grad_tokens, grad_prob = call(
-        finish_kernel,
+        unpack_kernel,
         [VMEM] * 2,
         [jax.ShapeDtypeStruct((tok_dev, features), BF16), jax.ShapeDtypeStruct((1, tok_dev), F32)],
-        fetched(kept), fetched(lax.ppermute(given, "top", SWAP)),
+        jnp.tile(pick.T, (1, groups)), back.reshape(rows, features + LANES),
     )
     rows_x, rows_dy = got[:, :features], got[:, features : 2 * features]
     weight_grads = [

time: 57.8 us -> 56.1 us (0.971); the launches traced: 57 us -> 55.8 us
  starting transfers between devices: 11 us -> 8.77 us
  waiting for transfers between devices: 9.52 us -> 11.3 us
  Pallas kernels: 8.22 us -> 7.42 us
    all_to_all x1, waiting for transfers between devices: 6.24 us -> 11.3 us  [body(): lax.all_to_all(reply, ALL_AXES, split_axis=0, concat_axis=0, tiled=True)]
    ppermute x1 -> x0, waiting for transfers between devices: 3.27 us -> none  [body(): lax.ppermute(given, 'top', SWAP)]
    ppermute x1 -> x0, starting transfers between devices: 1.44 us -> none  [body(): lax.ppermute(given, 'top', SWAP)]
    pallas_call x6 -> x5, Pallas kernels: 8.22 us -> 7.42 us  [call(): pl.pallas_call(kernel, in_specs=in_specs, scratch_shapes=scratch, out_spe...]
    all_to_all x1, starting transfers between devices: 3.94 us -> 3.14 us  [body(): lax.all_to_all(reply, ALL_AXES, split_axis=0, concat_axis=0, tiled=True)]
  transfers between devices with their start and end apart: 5 -> 4, of which waited for: 2 -> 1; matrix products, arithmetic and copies ran while one was open for 9% -> 10% of each run, Pallas kernels for 8% -> 7%
where the time goes in v10:
time: 56.1 us; the launch traced here: 55.8 us
  blocking collectives  22.1 us (39%)
  waiting for transfers between devices  11.3 us (20%)
  starting transfers between devices  8.77 us (16%)
  Pallas kernels  7.42 us (13%)
  matrix products  5.22 us (9%)
  between operations  0.7 us (1%)
    all_to_all x1, blocking collectives, body(): lax.all_to_all(send, HALF_AXES, split_axis=0, concat_axis=0, tiled=True)  22.1 us
    all_to_all x1, waiting for transfers between devices, body(): lax.all_to_all(reply, ALL_AXES, split_axis=0, concat_axis=0, tiled=True)  11.3 us
    pallas_call x5, Pallas kernels, call(): pl.pallas_call(kernel, in_specs=in_specs, scratch_shapes=scratch, out_spe...  7.42 us
    dot_general x3, matrix products, body(): jnp.einsum('rh,rd->hd', left, right, preferred_element_type=F32)  5.22 us
    ppermute x2, starting transfers between devices, body(): others = [lax.ppermute(a, 'top', SWAP) for a in (x, dy)]  3.28 us
    all_to_all x1, starting transfers between devices, body(): lax.all_to_all(reply, ALL_AXES, split_axis=0, concat_axis=0, tiled=True)  3.14 us
    ppermute x1, starting transfers between devices, body(): others.append(lax.ppermute(tail, 'top', SWAP))  2.35 us
  transfers between devices with their start and end apart: 4, of which 1 were waited for; matrix products, arithmetic and copies ran while one was open for 10% of the time, Pallas kernels for 7%

profile of v10, /device:TPU:1, one launch (start us, length us, event | category | flops | bytes accessed | tf_op | source)
XLA Modules:
  0.0 55.8 jit_solution(11610330153551838095)
XLA Ops:
  0.6 3.2 %collective-permute-start = (bf16[16,2048]{1,0:T(8,128)(2,1)}, bf16[16,2048]{1,0:T(8,128)(2,1)S(1)}, u32[]{:S(2)}, u32[]{:S(2)}) collective-permute-start(bf16[16,2048]{1,0:T(8,128)(2,1)} %bitcast.27), channel_id=1, source_target_pairs={{0,8},{8,0},{1,9},{9,1},{2,10},{10,2},{3,11},{11,3},{4,12},{12,4},... | collective-permute-start | bytes 196616 | tf_op jit(solution)/shard_map/ppermute | solution.py:179
  3.8 0.1 collective-permute-start.1
  3.9 0.8 %shard_map.111.refs_2_ = bf16[16,128]{1,0:T(8,128)(2,1)S(1)} custom-call(s32[2,16]{1,0:T(2,128)} %route_hbm.1, bf16[2,16]{1,0:T(2,128)(2,1)} %prob_hbm.1), custom_call_target="tpu_custom_call" | custom-call | tf_op jit(solution)/shard_map/pallas_call | solution.py:156
  4.7 2.3 %collective-permute-start.2 = (bf16[16,128]{1,0:T(8,128)(2,1)S(1)}, bf16[16,128]{1,0:T(8,128)(2,1)S(1)}, u32[]{:S(2)}, u32[]{:S(2)}) collective-permute-start(bf16[16,128]{1,0:T(8,128)(2,1)S(1)} %shard_map.111.refs_2_), channel_id=1, source_target_pairs={{0,8},{8,0},{1,9},{9,1},{2,10},{10,2},{3,11},{11,3},{4,12},{12,4},... | collective-permute-start | bytes 12296 | tf_op jit(solution)/shard_map/ppermute | solution.py:191
  7.1 2.9 %shard_map.110 = (bf16[16,2048]{1,0:T(8,128)(2,1)S(1)}, bf16[16,2048]{1,0:T(8,128)(2,1)S(1)}, bf16[768,2048]{1,0:T(8,128)(2,1)S(1)}, bf16[2048,384]{1,0:T(8,128)...) custom-call(bf16[16,2048]{1,0:T(8,128)(2,1)} %bitcast.28, bf16[16,2048]{1,0:T(8,128)(2,1)} %bitcast.30, ...), custom_call_target="tpu_custom_call" | custom-call | bytes 12582912 | tf_op jit(solution)/shard_map/pallas_call | solution.py:156
  10.0 0.0 collective-permute-done.2.refs_5_
  10.0 0.0 collective-permute-done.refs_3_
  10.0 0.0 collective-permute-done.1.refs_4_
  10.0 0.5 shard_map.112
  10.6 22.1 %all_to_all.16 = bf16[16,8,4224]{2,1,0:T(8,128)(2,1)S(1)} all-to-all(bf16[16,8,4224]{2,1,0:T(8,128)(2,1)S(1)} %bitcast.22), channel_id=1, replica_groups=mesh['dp'=2,'top'=2,'low'=8] {'dp','low'}, dimensions={0} | all-to-all | bytes 2162688 | tf_op jit(solution)/shard_map/all_to_all | solution.py:209
  32.7 2.3 %shard_map.113 = (bf16[32,4,2176]{2,1,0:T(4,128)(2,1)}, bf16[128,384]{1,0:T(8,128)(2,1)S(1)}, bf16[128,384]{1,0:T(8,128)(2,1)S(1)}, bf16[128,384]{1,0:T(8,128)(2,1)S(1)}) custom-call(bf16[128,4224]{1,0:T(8,128)(2,1)S(1)} %bitcast.18, bf16[768,2048]{1,0:T(8,128)(2,1)S(1)} %get-tuple-element.21.refs_6_.refs_1_, ...), custom_call_target="tpu_custom_call" | custom-call | tf_op jit(solution)/shard_map/pallas_call | solution.py:156
  35.0 3.1 %all-to-all-start.1 = ((bf16[32,4,2176]{2,1,0:T(4,128)(2,1)}), bf16[32,4,2176]{2,1,0:T(4,128)(2,1)S(1)}, u32[]{:S(2)}, u32[]{:S(2)}) async-start(bf16[32,4,2176]{2,1,0:T(4,128)(2,1)} %get-tuple-element.27), calls=%async_computation.1 | async-start | bytes 1114112 | tf_op jit(solution)/shard_map/all_to_all | solution.py:216
  38.1 0.1 copy.12
  38.2 0.1 tile.10.pick_ref
  38.3 1.7 %fusion = bf16[1,384,2048]{2,1,0:T(8,128)(2,1)} fusion(bf16[128,384]{1,0:T(8,128)(2,1)S(1)} %get-tuple-element.30, bf16[128,4224]{1,0:T(8,128)(2,1)S(1)} %bitcast.19), kind=kOutput, calls=%fused_computation.3 | convolution fusion | flops 202113024 | bytes 2195456 | tf_op jit(solution)/shard_map/rh,rd->hd/dot_general | solution.py:225
  40.1 1.7 %fusion.1 = bf16[1,384,2048]{2,1,0:T(8,128)(2,1)} fusion(bf16[128,384]{1,0:T(8,128)(2,1)S(1)} %get-tuple-element.31, bf16[128,4224]{1,0:T(8,128)(2,1)S(1)} %bitcast.20), kind=kOutput, calls=%fused_computation.4 | convolution fusion | flops 202113024 | bytes 2195456 | tf_op jit(solution)/shard_map/rh,rd->hd/dot_general | solution.py:225
  41.8 1.7 %fusion.2 = bf16[1,384,2048]{2,1,0:T(8,128)(2,1)} fusion(bf16[128,384]{1,0:T(8,128)(2,1)S(1)} %get-tuple-element.32, bf16[128,4224]{1,0:T(8,128)(2,1)S(1)} %bitcast.21), kind=kOutput, calls=%fused_computation.5 | convolution fusion | flops 202113024 | bytes 2195456 | tf_op jit(solution)/shard_map/rh,rd->hd/dot_general | solution.py:225
  43.5 11.3 %all-to-all-done.1 = bf16[32,4,2176]{2,1,0:T(4,128)(2,1)S(1)} async-done(((bf16[32,4,2176]{2,1,0:T(4,128)(2,1)}), bf16[32,4,2176]{2,1,0:T(4,128)(2,1)S(1)}, u32[]{:S(2)}, u32[]{:S(2)}) %all-to-all-start.1) | async-done | bytes 557088 | tf_op jit(solution)/shard_map/all_to_all | solution.py:216
  54.9 0.1 reshape.19.back_ref
  55.0 0.8 %shard_map.114 = (bf16[16,2048]{1,0:T(8,128)(2,1)}, f32[1,16]{1,0:T(1,128)}) custom-call(bf16[16,128]{1,0:T(8,128)(2,1)S(1)} %tile.10.pick_ref, bf16[128,2176]{1,0:T(8,128)(2,1)S(1)} %reshape.19.back_ref), custom_call_target="tpu_custom_call" | custom-call | tf_op jit(solution)/shard_map/pallas_call | solution.py:156
  (1 shorter events, 0.0 us)
Async XLA Ops:
  0.6 9.4 %collective-permute-start = (bf16[16,2048]{1,0:T(8,128)(2,1)}, bf16[16,2048]{1,0:T(8,128)(2,1)S(1)}, u32[]{:S(2)}, u32[]{:S(2)}) collective-permute-start(bf16[16,2048]{1,0:T(8,128)(2,1)} %bitcast.27), channel_id=1, source_target_pairs={{0,8},{8,0},{1,9},{9,1},{2,10},{10,2},{3,11},{11,3},{4,12},{12,4},... | collective-permute-start | bytes 196616 | tf_op jit(solution)/shard_map/ppermute | solution.py:179
  3.8 6.2 %collective-permute-start.1 = (bf16[16,2048]{1,0:T(8,128)(2,1)}, bf16[16,2048]{1,0:T(8,128)(2,1)S(1)}, u32[]{:S(2)}, u32[]{:S(2)}) collective-permute-start(bf16[16,2048]{1,0:T(8,128)(2,1)} %bitcast.29), channel_id=1, source_target_pairs={{0,8},{8,0},{1,9},{9,1},{2,10},{10,2},{3,11},{11,3},{4,12},{12,4},... | collective-permute-start | bytes 196616 | tf_op jit(solution)/shard_map/ppermute | solution.py:179
  4.7 5.3 %collective-permute-start.2 = (bf16[16,128]{1,0:T(8,128)(2,1)S(1)}, bf16[16,128]{1,0:T(8,128)(2,1)S(1)}, u32[]{:S(2)}, u32[]{:S(2)}) collective-permute-start(bf16[16,128]{1,0:T(8,128)(2,1)S(1)} %shard_map.111.refs_2_), channel_id=1, source_target_pairs={{0,8},{8,0},{1,9},{9,1},{2,10},{10,2},{3,11},{11,3},{4,12},{12,4},... | collective-permute-start | bytes 12296 | tf_op jit(solution)/shard_map/ppermute | solution.py:191
  35.0 19.9 %all-to-all-start.1 = ((bf16[32,4,2176]{2,1,0:T(4,128)(2,1)}), bf16[32,4,2176]{2,1,0:T(4,128)(2,1)S(1)}, u32[]{:S(2)}, u32[]{:S(2)}) async-start(bf16[32,4,2176]{2,1,0:T(4,128)(2,1)} %get-tuple-element.27), calls=%async_computation.1 | async-start | bytes 1114112 | tf_op jit(solution)/shard_map/all_to_all | solution.py:216

commit v11 on v10

--- a/solution.py
+++ b/solution.py
@@ -47,15 +47,17 @@
 
 
 def load_kernel(*refs):
-    ins, outs, down_v, sems = refs[:5], refs[5:11], refs[11], refs[12]
+    ins, outs, down_v, sems = refs[:5], refs[5:10], refs[10], refs[11]
     hidden = ins[2].shape[0]
     joined = outs[2]
     places = (*outs[:2], joined.at[pl.ds(0, hidden), :], joined.at[pl.ds(hidden, hidden), :], down_v)
     copies = [pltpu.make_async_copy(a, b, sems.at[i]) for i, (a, b) in enumerate(zip(ins, places))]
     for copy in copies:
         copy.start()
-    for copy, place, turned in zip(copies[2:], places[2:], outs[3:]):
+    both_t, down_t = outs[3:]
+    for i, (copy, place) in enumerate(zip(copies[2:], places[2:])):
         copy.wait()
+        turned = down_t if i == 2 else both_t.at[:, pl.ds(i * hidden, hidden)]
         turned[...] = place[...].T
     for copy in copies[:2]:
         copy.wait()
@@ -79,24 +81,26 @@
         low = row.astype(jnp.int32) - top * half
         inside = (low >= 0) & (low < half)
         target = jnp.where(inside, low * (2 * slots) + origin * slots + rank, -1)
-        picks.append((place == target).astype(F32).astype(BF16))
+        picks.append((place == target).astype(F32))
         if tail_ref is own[2]:
             upper = jnp.where(inside, top, 1 - top)
             low = low + (top - upper) * half
             target = (low * 2 + upper) * slots + rank
             pick_ref[...] = (place == target).astype(F32).astype(BF16)
+    picks = jnp.concatenate(picks, axis=1).astype(BF16)
     start = 0
     for own_ref, other_ref in zip(own, other):
         end = start + own_ref.shape[1]
-        sent = dot(picks[0], own_ref[...], (1, 0)) + dot(picks[1], other_ref[...], (1, 0))
-        sent = sent.astype(BF16)
+        both = jnp.concatenate([own_ref[...], other_ref[...]], axis=0)
+        sent = dot(picks, both, (1, 0)).astype(BF16)
         for g in range(groups):
             send_ref[g * block : (g + 1) * block, start:end] = sent
         start = end
 
 
-def expert_kernel(slots, chunk, got_ref, rows_ref, gate_t, up_t, down_t, reply_ref, dg_ref, du_ref, sa_ref):
+def expert_kernel(slots, chunk, got_ref, rows_ref, both_t, down_t, reply_ref, dg_ref, du_ref, sa_ref):
     features = rows_ref.shape[1]
+    hidden = dg_ref.shape[1]
     mine = lax.axis_index("dp")
     lane = lax.broadcasted_iota(jnp.int32, (chunk, LANES), 1)
 
@@ -106,8 +110,8 @@
         rows_x = got_ref[at, :features]
         rows_dy = got_ref[at, features : 2 * features]
         weight = got_ref[at, 2 * features : 2 * features + 1].astype(F32)
-        gate_pre = dot(rows_x, gate_t[...], (1, 0))
-        up_pre = dot(rows_x, up_t[...], (1, 0))
+        both_pre = dot(rows_x, both_t[...], (1, 0))
+        gate_pre, up_pre = both_pre[:, :hidden], both_pre[:, hidden:]
         back_proj = dot(rows_dy, down_t[...], (1, 0))
         sigma = jax.nn.sigmoid(gate_pre)
         swish = gate_pre * sigma
@@ -189,27 +193,26 @@
         ],
     )
     others.append(lax.ppermute(tail, "top", SWAP))
-    *own, joined, gate_t, up_t, down_t = call(
+    *own, joined, both_t, down_t = call(
         load_kernel,
         [HBM] * 5,
         [near((tok_dev, features))] * 2
-        + [near((2 * hidden, features))]
-        + [near((features, hidden))] * 3,
+        + [near((2 * hidden, features)), near((features, 2 * hidden)), near((features, hidden))],
         *far(x, dy, w_gate[0], w_up[0], w_down[0]),
         scratch=[pltpu.VMEM((hidden, features), BF16), pltpu.SemaphoreType.DMA((5,))],
         cost=pl.CostEstimate(flops=0, transcendentals=0, bytes_accessed=16 * hidden * features),
     )
-    weights = [fetched(a) for a in (joined, gate_t, up_t, down_t)]
+    weights = [fetched(a) for a in (joined, both_t, down_t)]
     send, pick = call(
         lambda *refs: pack_kernel(slots, *refs),
-        [VMEM] * 10,
+        [VMEM] * 9,
         [near((rows, width)), near((block, tok_dev))],
         *[fetched(a) for a in (*own, tail, *others)], *weights,
     )
     got = lax.all_to_all(send, HALF_AXES, split_axis=0, concat_axis=0, tiled=True)
     reply, d_gate, d_up, scaled_act = call(
         lambda *refs: expert_kernel(slots, chunk, *refs),
-        [VMEM] * 5,
+        [VMEM] * 4,
         [near((rows // slots, slots, features + LANES))] + [near((rows, hidden))] * 3,
         fetched(got), *weights,
     )

time: 56.1 us -> 55.9 us (level)
  no operation moved by 1% of the time
where the time goes in v11:
time: 55.9 us; the launch traced here: 55.6 us
  blocking collectives  22.1 us (40%)
  waiting for transfers between devices  11.3 us (20%)
  starting transfers between devices  8.77 us (16%)
  Pallas kernels  7.2 us (13%)
  matrix products  5.22 us (9%)
  between operations  0.71 us (1%)
    all_to_all x1, blocking collectives, body(): lax.all_to_all(send, HALF_AXES, split_axis=0, concat_axis=0, tiled=True)  22.1 us
    all_to_all x1, waiting for transfers between devices, body(): lax.all_to_all(reply, ALL_AXES, split_axis=0, concat_axis=0, tiled=True)  11.3 us
    pallas_call x5, Pallas kernels, call(): pl.pallas_call(kernel, in_specs=in_specs, scratch_shapes=scratch, out_spe...  7.2 us
    dot_general x3, matrix products, body(): jnp.einsum('rh,rd->hd', left, right, preferred_element_type=F32)  5.22 us
    ppermute x2, starting transfers between devices, body(): others = [lax.ppermute(a, 'top', SWAP) for a in (x, dy)]  3.28 us
    all_to_all x1, starting transfers between devices, body(): lax.all_to_all(reply, ALL_AXES, split_axis=0, concat_axis=0, tiled=True)  3.14 us
    ppermute x1, starting transfers between devices, body(): others.append(lax.ppermute(tail, 'top', SWAP))  2.35 us
  transfers between devices with their start and end apart: 4, of which 1 were waited for; matrix products, arithmetic and copies ran while one was open for 10% of the time, Pallas kernels for 7%

profile of v11, /device:TPU:1, one launch (start us, length us, event | category | flops | bytes accessed | tf_op | source)
XLA Modules:
  0.0 55.6 jit_solution(12041979984584653648)
XLA Ops:
  0.6 3.2 %collective-permute-start = (bf16[16,2048]{1,0:T(8,128)(2,1)}, bf16[16,2048]{1,0:T(8,128)(2,1)S(1)}, u32[]{:S(2)}, u32[]{:S(2)}) collective-permute-start(bf16[16,2048]{1,0:T(8,128)(2,1)} %bitcast.27), channel_id=1, source_target_pairs={{0,8},{8,0},{1,9},{9,1},{2,10},{10,2},{3,11},{11,3},{4,12},{12,4},... | collective-permute-start | bytes 196616 | tf_op jit(solution)/shard_map/ppermute | solution.py:183
  3.8 0.1 collective-permute-start.1
  3.9 0.8 %shard_map.111.refs_2_ = bf16[16,128]{1,0:T(8,128)(2,1)S(1)} custom-call(s32[2,16]{1,0:T(2,128)} %route_hbm.1, bf16[2,16]{1,0:T(2,128)(2,1)} %prob_hbm.1), custom_call_target="tpu_custom_call" | custom-call | tf_op jit(solution)/shard_map/pallas_call | solution.py:160
  4.7 2.3 %collective-permute-start.2 = (bf16[16,128]{1,0:T(8,128)(2,1)S(1)}, bf16[16,128]{1,0:T(8,128)(2,1)S(1)}, u32[]{:S(2)}, u32[]{:S(2)}) collective-permute-start(bf16[16,128]{1,0:T(8,128)(2,1)S(1)} %shard_map.111.refs_2_), channel_id=1, source_target_pairs={{0,8},{8,0},{1,9},{9,1},{2,10},{10,2},{3,11},{11,3},{4,12},{12,4},... | collective-permute-start | bytes 12296 | tf_op jit(solution)/shard_map/ppermute | solution.py:195
  7.1 2.9 %shard_map.110 = (bf16[16,2048]{1,0:T(8,128)(2,1)S(1)}, bf16[16,2048]{1,0:T(8,128)(2,1)S(1)}, bf16[768,2048]{1,0:T(8,128)(2,1)S(1)}, bf16[2048,768]{1,0:T(8,128)(2,1)S(1)}, bf16[2048,384]{1,0:T(8,128)(2,1)S(1)}) custom-call(bf16[16,2048]{1,0:T(8,128)(2,1)} %bitcast.28, bf16[16,2048]{1,0:T(8,128)(2,1)} %bitcast.30, bf16[384,2048]{1,0:T(8,128)(2,1)} %bitcast.24, ...), custom_call_target="tpu_custom_call" | custom-call | bytes 12582912 | tf_op jit(solution)/shard_map/pallas_call | solution.py:160
  10.0 0.0 collective-permute-done.2.refs_5_
  10.0 0.0 collective-permute-done.refs_3_
  10.0 0.0 collective-permute-done.1.refs_4_
  10.0 0.4 shard_map.112
  10.5 22.1 %all_to_all.16 = bf16[16,8,4224]{2,1,0:T(8,128)(2,1)S(1)} all-to-all(bf16[16,8,4224]{2,1,0:T(8,128)(2,1)S(1)} %bitcast.22), channel_id=1, replica_groups=mesh['dp'=2,'top'=2,'low'=8] {'dp','low'}, dimensions={0} | all-to-all | bytes 2162688 | tf_op jit(solution)/shard_map/all_to_all | solution.py:212
  32.6 2.2 %shard_map.113 = (bf16[32,4,2176]{2,1,0:T(4,128)(2,1)}, bf16[128,384]{1,0:T(8,128)(2,1)S(1)}, bf16[128,384]{1,0:T(8,128)(2,1)S(1)}, bf16[128,384]{1,0:T(8,128)(2,1)S(1)}) custom-call(bf16[128,4224]{1,0:T(8,128)(2,1)S(1)} %bitcast.18, bf16[768,2048]{1,0:T(8,128)(2,1)S(1)} %get-tuple-element.20.refs_6_.refs_1_, ...), custom_call_target="tpu_custom_call" | custom-call | tf_op jit(solution)/shard_map/pallas_call | solution.py:160
  34.8 3.1 %all-to-all-start.1 = ((bf16[32,4,2176]{2,1,0:T(4,128)(2,1)}), bf16[32,4,2176]{2,1,0:T(4,128)(2,1)S(1)}, u32[]{:S(2)}, u32[]{:S(2)}) async-start(bf16[32,4,2176]{2,1,0:T(4,128)(2,1)} %get-tuple-element.25), calls=%async_computation.1 | async-start | bytes 1114112 | tf_op jit(solution)/shard_map/all_to_all | solution.py:219
  37.9 0.1 copy.12
  38.0 0.1 tile.10.pick_ref
  38.1 1.7 %fusion = bf16[1,384,2048]{2,1,0:T(8,128)(2,1)} fusion(bf16[128,384]{1,0:T(8,128)(2,1)S(1)} %get-tuple-element.28, bf16[128,4224]{1,0:T(8,128)(2,1)S(1)} %bitcast.19), kind=kOutput, calls=%fused_computation.3 | convolution fusion | flops 202113024 | bytes 2195456 | tf_op jit(solution)/shard_map/rh,rd->hd/dot_general | solution.py:228
  39.9 1.7 %fusion.1 = bf16[1,384,2048]{2,1,0:T(8,128)(2,1)} fusion(bf16[128,384]{1,0:T(8,128)(2,1)S(1)} %get-tuple-element.29, bf16[128,4224]{1,0:T(8,128)(2,1)S(1)} %bitcast.20), kind=kOutput, calls=%fused_computation.4 | convolution fusion | flops 202113024 | bytes 2195456 | tf_op jit(solution)/shard_map/rh,rd->hd/dot_general | solution.py:228
  41.6 1.7 %fusion.2 = bf16[1,384,2048]{2,1,0:T(8,128)(2,1)} fusion(bf16[128,384]{1,0:T(8,128)(2,1)S(1)} %get-tuple-element.30, bf16[128,4224]{1,0:T(8,128)(2,1)S(1)} %bitcast.21), kind=kOutput, calls=%fused_computation.5 | convolution fusion | flops 202113024 | bytes 2195456 | tf_op jit(solution)/shard_map/rh,rd->hd/dot_general | solution.py:228
  43.3 11.3 %all-to-all-done.1 = bf16[32,4,2176]{2,1,0:T(4,128)(2,1)S(1)} async-done(((bf16[32,4,2176]{2,1,0:T(4,128)(2,1)}), bf16[32,4,2176]{2,1,0:T(4,128)(2,1)S(1)}, u32[]{:S(2)}, u32[]{:S(2)}) %all-to-all-start.1) | async-done | bytes 557088 | tf_op jit(solution)/shard_map/all_to_all | solution.py:219
  54.7 0.1 reshape.19.back_ref
  54.8 0.8 %shard_map.114 = (bf16[16,2048]{1,0:T(8,128)(2,1)}, f32[1,16]{1,0:T(1,128)}) custom-call(bf16[16,128]{1,0:T(8,128)(2,1)S(1)} %tile.10.pick_ref, bf16[128,2176]{1,0:T(8,128)(2,1)S(1)} %reshape.19.back_ref), custom_call_target="tpu_custom_call" | custom-call | tf_op jit(solution)/shard_map/pallas_call | solution.py:160
  (1 shorter events, 0.0 us)
Async XLA Ops:
  0.6 9.4 %collective-permute-start = (bf16[16,2048]{1,0:T(8,128)(2,1)}, bf16[16,2048]{1,0:T(8,128)(2,1)S(1)}, u32[]{:S(2)}, u32[]{:S(2)}) collective-permute-start(bf16[16,2048]{1,0:T(8,128)(2,1)} %bitcast.27), channel_id=1, source_target_pairs={{0,8},{8,0},{1,9},{9,1},{2,10},{10,2},{3,11},{11,3},{4,12},{12,4},... | collective-permute-start | bytes 196616 | tf_op jit(solution)/shard_map/ppermute | solution.py:183
  3.8 6.2 %collective-permute-start.1 = (bf16[16,2048]{1,0:T(8,128)(2,1)}, bf16[16,2048]{1,0:T(8,128)(2,1)S(1)}, u32[]{:S(2)}, u32[]{:S(2)}) collective-permute-start(bf16[16,2048]{1,0:T(8,128)(2,1)} %bitcast.29), channel_id=1, source_target_pairs={{0,8},{8,0},{1,9},{9,1},{2,10},{10,2},{3,11},{11,3},{4,12},{12,4},... | collective-permute-start | bytes 196616 | tf_op jit(solution)/shard_map/ppermute | solution.py:183
  4.7 5.3 %collective-permute-start.2 = (bf16[16,128]{1,0:T(8,128)(2,1)S(1)}, bf16[16,128]{1,0:T(8,128)(2,1)S(1)}, u32[]{:S(2)}, u32[]{:S(2)}) collective-permute-start(bf16[16,128]{1,0:T(8,128)(2,1)S(1)} %shard_map.111.refs_2_), channel_id=1, source_target_pairs={{0,8},{8,0},{1,9},{9,1},{2,10},{10,2},{3,11},{11,3},{4,12},{12,4},... | collective-permute-start | bytes 12296 | tf_op jit(solution)/shard_map/ppermute | solution.py:195
  34.8 19.9 %all-to-all-start.1 = ((bf16[32,4,2176]{2,1,0:T(4,128)(2,1)}), bf16[32,4,2176]{2,1,0:T(4,128)(2,1)S(1)}, u32[]{:S(2)}, u32[]{:S(2)}) async-start(bf16[32,4,2176]{2,1,0:T(4,128)(2,1)} %get-tuple-element.25), calls=%async_computation.1 | async-start | bytes 1114112 | tf_op jit(solution)/shard_map/all_to_all | solution.py:219

commit v12 on v11

--- a/solution.py
+++ b/solution.py
@@ -26,45 +26,25 @@
     return tuple(lax.broadcasted_iota(jnp.int32, (size, size), axis) for axis in (0, 1))
 
 
-def tail_kernel(route_hbm, prob_hbm, out_ref, route_v, prob_v, sems):
-    tok_dev = out_ref.shape[0]
-    copies = [
-        pltpu.make_async_copy(route_hbm, route_v, sems.at[0]),
-        pltpu.make_async_copy(prob_hbm, prob_v, sems.at[1]),
-    ]
-    for copy in copies:
-        copy.start()
-    own = lax.broadcasted_iota(jnp.int32, route_v.shape, 0) == lax.axis_index("dp")
-    here, there = square(tok_dev)
-    for copy in copies:
-        copy.wait()
-    route = jnp.sum(jnp.where(own, route_v[...].astype(F32), 0.0), axis=0, keepdims=True)
-    prob = jnp.sum(jnp.where(own, prob_v[...].astype(F32), 0.0), axis=0, keepdims=True)
-    route = jnp.sum(jnp.where(here == there, route, 0.0), axis=1, keepdims=True)
-    prob = jnp.sum(jnp.where(here == there, prob, 0.0), axis=1, keepdims=True)
-    lane = lax.broadcasted_iota(jnp.int32, (tok_dev, LANES), 1)
-    out_ref[...] = jnp.where(lane == 0, prob, jnp.where(lane == 1, route, 0.0)).astype(BF16)
-
-
 def load_kernel(*refs):
-    ins, outs, down_v, sems = refs[:5], refs[5:10], refs[10], refs[11]
-    hidden = ins[2].shape[0]
-    joined = outs[2]
-    places = (*outs[:2], joined.at[pl.ds(0, hidden), :], joined.at[pl.ds(hidden, hidden), :], down_v)
+    ins, outs, down_v, sems = refs[:7], refs[7:14], refs[14], refs[15]
+    hidden = ins[4].shape[0]
+    joined = outs[4]
+    places = (*outs[:4], joined.at[pl.ds(0, hidden), :], joined.at[pl.ds(hidden, hidden), :], down_v)
     copies = [pltpu.make_async_copy(a, b, sems.at[i]) for i, (a, b) in enumerate(zip(ins, places))]
     for copy in copies:
         copy.start()
-    both_t, down_t = outs[3:]
-    for i, (copy, place) in enumerate(zip(copies[2:], places[2:])):
+    both_t, down_t = outs[5:]
+    for i, (copy, place) in enumerate(zip(copies[4:], places[4:])):
         copy.wait()
         turned = down_t if i == 2 else both_t.at[:, pl.ds(i * hidden, hidden)]
         turned[...] = place[...].T
-    for copy in copies[:2]:
+    for copy in copies[:4]:
         copy.wait()
 
 
 def pack_kernel(slots, *refs):
-    own, other, (send_ref, pick_ref) = refs[:3], refs[3:6], refs[-2:]
+    own, other, (send_ref, pick_ref) = refs[:4], refs[4:8], refs[-2:]
     tok_dev, features = own[0].shape
     block = pick_ref.shape[0]
     groups = send_ref.shape[0] // block
@@ -72,30 +52,33 @@
     top = lax.axis_index("top")
     here, there = square(tok_dev)
     place = lax.broadcasted_iota(jnp.int32, (block, tok_dev), 0)
-    picks = []
-    for tail_ref, origin in ((own[2], top), (other[2], 1 - top)):
-        column = tail_ref[:, 1:2].astype(F32)
-        row = jnp.sum(jnp.where(here == there, column, 0.0), axis=0, keepdims=True)
+    mine = lax.broadcasted_iota(jnp.int32, own[2].shape, 0) == lax.axis_index("dp")
+    picks, weights = [], 0.0
+    for (_, _, route_ref, prob_ref), origin in ((own, top), (other, 1 - top)):
+        row = jnp.sum(jnp.where(mine, route_ref[...].astype(F32), 0.0), axis=0, keepdims=True)
+        prob = jnp.sum(jnp.where(mine, prob_ref[...].astype(F32), 0.0), axis=0, keepdims=True)
+        column = jnp.sum(jnp.where(here == there, row, 0.0), axis=1, keepdims=True)
         rank = jnp.sum(jnp.where((column == row) & (here < there), 1.0, 0.0), axis=0, keepdims=True)
         rank = rank.astype(jnp.int32)
         low = row.astype(jnp.int32) - top * half
         inside = (low >= 0) & (low < half)
         target = jnp.where(inside, low * (2 * slots) + origin * slots + rank, -1)
         picks.append((place == target).astype(F32))
-        if tail_ref is own[2]:
+        weights += jnp.sum(picks[-1] * prob, axis=1, keepdims=True)
+        if route_ref is own[2]:
             upper = jnp.where(inside, top, 1 - top)
             low = low + (top - upper) * half
             target = (low * 2 + upper) * slots + rank
             pick_ref[...] = (place == target).astype(F32).astype(BF16)
     picks = jnp.concatenate(picks, axis=1).astype(BF16)
-    start = 0
-    for own_ref, other_ref in zip(own, other):
-        end = start + own_ref.shape[1]
-        both = jnp.concatenate([own_ref[...], other_ref[...]], axis=0)
+    weights = jnp.broadcast_to(weights, (block, LANES)).astype(BF16)
+    for g in range(groups):
+        send_ref[g * block : (g + 1) * block, 2 * features :] = weights
+    for i in range(2):
+        both = jnp.concatenate([own[i][...], other[i][...]], axis=0)
         sent = dot(picks, both, (1, 0)).astype(BF16)
         for g in range(groups):
-            send_ref[g * block : (g + 1) * block, start:end] = sent
-        start = end
+            send_ref[g * block : (g + 1) * block, i * features : (i + 1) * features] = sent
 
 
 def expert_kernel(slots, chunk, got_ref, rows_ref, both_t, down_t, reply_ref, dg_ref, du_ref, sa_ref):
@@ -179,35 +162,23 @@
     chunk = min(rows, 256)
     width = 2 * features + LANES
 
-    x, dy = tokens[0], cotangent[0]
-    others = [lax.ppermute(a, "top", SWAP) for a in (x, dy)]
-    (tail,) = call(
-        tail_kernel,
-        [HBM] * 2,
-        [near((tok_dev, LANES))],
-        *far(routes, gate_prob),
-        scratch=[
-            pltpu.VMEM(routes.shape, routes.dtype),
-            pltpu.VMEM(gate_prob.shape, gate_prob.dtype),
-            pltpu.SemaphoreType.DMA((2,)),
-        ],
-    )
-    others.append(lax.ppermute(tail, "top", SWAP))
+    rows_in = (tokens[0], cotangent[0], routes, gate_prob)
+    others = [lax.ppermute(a, "top", SWAP) for a in rows_in]
     *own, joined, both_t, down_t = call(
         load_kernel,
-        [HBM] * 5,
-        [near((tok_dev, features))] * 2
+        [HBM] * 7,
+        [near(a.shape, a.dtype) for a in rows_in]
         + [near((2 * hidden, features)), near((features, 2 * hidden)), near((features, hidden))],
-        *far(x, dy, w_gate[0], w_up[0], w_down[0]),
-        scratch=[pltpu.VMEM((hidden, features), BF16), pltpu.SemaphoreType.DMA((5,))],
+        *far(*rows_in, w_gate[0], w_up[0], w_down[0]),
+        scratch=[pltpu.VMEM((hidden, features), BF16), pltpu.SemaphoreType.DMA((7,))],
         cost=pl.CostEstimate(flops=0, transcendentals=0, bytes_accessed=16 * hidden * features),
     )
     weights = [fetched(a) for a in (joined, both_t, down_t)]
     send, pick = call(
         lambda *refs: pack_kernel(slots, *refs),
-        [VMEM] * 9,
+        [VMEM] * 11,
         [near((rows, width)), near((block, tok_dev))],
-        *[fetched(a) for a in (*own, tail, *others)], *weights,
+        *[fetched(a) for a in (*own, *others)], *weights,
     )
     got = lax.all_to_all(send, HALF_AXES, split_axis=0, concat_axis=0, tiled=True)
     reply, d_gate, d_up, scaled_act = call(

time: 55.9 us -> 56.5 us (1.011)
  waiting for transfers between devices: 11.3 us -> 12.2 us
  blocking collectives: 22.1 us -> 22.9 us
  Pallas kernels: 7.2 us -> 6.52 us
    all_to_all x1, blocking collectives: 22.1 us -> 22.9 us  [body(): lax.all_to_all(send, HALF_AXES, split_axis=0, concat_axis=0, tiled=True)]
    ppermute x3 -> x4, waiting for transfers between devices: 0.01 us -> 0.76 us  [body(): others = [lax.ppermute(a, 'top', SWAP) for a in rows_in]]
    pallas_call x5 -> x4, Pallas kernels: 7.2 us -> 6.52 us  [call(): pl.pallas_call(kernel, in_specs=in_specs, scratch_shapes=scratch, out_spe...]
    ppermute x3 -> x4, starting transfers between devices: 5.63 us -> 5.65 us  [body(): others = [lax.ppermute(a, 'top', SWAP) for a in rows_in]]
  transfers between devices with their start and end apart: 4 -> 5, of which waited for: 1 -> 3; matrix products, arithmetic and copies ran while one was open for 10% -> 10% of each run, Pallas kernels for 7% -> 5%
where the time goes in v12:
time: 56.5 us; the launch traced here: 56.3 us
  blocking collectives  22.9 us (41%)
  waiting for transfers between devices  12.2 us (22%)
  starting transfers between devices  8.42 us (15%)
  Pallas kernels  6.52 us (12%)
  matrix products  5.22 us (9%)
  between operations  0.68 us (1%)
    all_to_all x1, blocking collectives, body(): lax.all_to_all(send, HALF_AXES, split_axis=0, concat_axis=0, tiled=True)  22.9 us
    all_to_all x1, waiting for transfers between devices, body(): lax.all_to_all(reply, ALL_AXES, split_axis=0, concat_axis=0, tiled=True)  11.5 us
    pallas_call x4, Pallas kernels, call(): pl.pallas_call(kernel, in_specs=in_specs, scratch_shapes=scratch, out_spe...  6.52 us
    ppermute x4, starting transfers between devices, body(): others = [lax.ppermute(a, 'top', SWAP) for a in rows_in]  5.65 us
    dot_general x3, matrix products, body(): jnp.einsum('rh,rd->hd', left, right, preferred_element_type=F32)  5.22 us
    all_to_all x1, starting transfers between devices, body(): lax.all_to_all(reply, ALL_AXES, split_axis=0, concat_axis=0, tiled=True)  2.78 us
  transfers between devices with their start and end apart: 5, of which 3 were waited for; matrix products, arithmetic and copies ran while one was open for 10% of the time, Pallas kernels for 5%

profile of v12, /device:TPU:1, one launch (start us, length us, event | category | flops | bytes accessed | tf_op | source)
XLA Modules:
  0.0 56.3 jit_solution(7957936576040021074)
XLA Ops:
  0.6 3.2 %collective-permute-start = (bf16[16,2048]{1,0:T(8,128)(2,1)}, bf16[16,2048]{1,0:T(8,128)(2,1)S(1)}, u32[]{:S(2)}, u32[]{:S(2)}) collective-permute-start(bf16[16,2048]{1,0:T(8,128)(2,1)} %bitcast.27), channel_id=1, source_target_pairs={{0,8},{8,0},{1,9},{9,1},{2,10},{10,2},{3,11},{11,3},{4,12},{12,4},... | collective-permute-start | bytes 196616 | tf_op jit(solution)/shard_map/ppermute | solution.py:166
  3.8 0.1 collective-permute-start.1
  3.9 2.3 %collective-permute-start.3 = (bf16[2,16]{1,0:T(2,128)(2,1)}, bf16[2,16]{1,0:T(2,128)(2,1)S(1)}, u32[]{:S(2)}, u32[]{:S(2)}) collective-permute-start(bf16[2,16]{1,0:T(2,128)(2,1)} %refs_3_.1), channel_id=1, source_target_pairs={{0,8},{8,0},{1,9},{9,1},{2,10},{10,2},{3,11},{11,3},{4,12},{12,4},... | collective-permute-start | bytes 200 | tf_op jit(solution)/shard_map/ppermute | solution.py:166
  6.2 0.1 collective-permute-start.2
  6.3 3.0 %shard_map.110 = (bf16[16,2048]{1,0:T(8,128)(2,1)S(1)}, bf16[16,2048]{1,0:T(8,128)(2,1)S(1)}, s32[2,16]{1,0:T(2,128)S(1)}, bf16[2,16]{1,0:T(2,128)(2,1)S(1)}, bf...) custom-call(bf16[16,2048]{1,0:T(8,128)(2,1)} %bitcast.28, ...), custom_call_target="tpu_custom_call" | custom-call | bytes 12582912 | tf_op jit(solution)/shard_map/pallas_call | solution.py:143
  9.3 0.5 collective-permute-done.3.refs_7_
  9.8 0.2 collective-permute-done.2.refs_6_
  10.0 0.0 collective-permute-done.refs_4_
  10.0 0.0 collective-permute-done.1.refs_5_
  10.0 0.4 shard_map.111
  10.5 22.9 %all_to_all.16 = bf16[16,8,4224]{2,1,0:T(8,128)(2,1)S(1)} all-to-all(bf16[16,8,4224]{2,1,0:T(8,128)(2,1)S(1)} %bitcast.22), channel_id=1, replica_groups=mesh['dp'=2,'top'=2,'low'=8] {'dp','low'}, dimensions={0} | all-to-all | bytes 2162688 | tf_op jit(solution)/shard_map/all_to_all | solution.py:183
  33.4 2.2 %shard_map.112 = (bf16[32,4,2176]{2,1,0:T(4,128)(2,1)}, bf16[128,384]{1,0:T(8,128)(2,1)S(1)}, bf16[128,384]{1,0:T(8,128)(2,1)S(1)}, bf16[128,384]{1,0:T(8,128)(2,1)S(1)}) custom-call(bf16[128,4224]{1,0:T(8,128)(2,1)S(1)} %bitcast.18, bf16[768,2048]{1,0:T(8,128)(2,1)S(1)} %get-tuple-element.24.refs_8_.refs_1_, ...), custom_call_target="tpu_custom_call" | custom-call | tf_op jit(solution)/shard_map/pallas_call | solution.py:143
  35.7 2.8 %all-to-all-start.1 = ((bf16[32,4,2176]{2,1,0:T(4,128)(2,1)}), bf16[32,4,2176]{2,1,0:T(4,128)(2,1)S(1)}, u32[]{:S(2)}, u32[]{:S(2)}) async-start(bf16[32,4,2176]{2,1,0:T(4,128)(2,1)} %get-tuple-element.29), calls=%async_computation.1 | async-start | bytes 1114112 | tf_op jit(solution)/shard_map/all_to_all | solution.py:190
  38.5 0.1 copy.12
  38.6 0.1 tile.10.pick_ref
  38.6 1.7 %fusion = bf16[1,384,2048]{2,1,0:T(8,128)(2,1)} fusion(bf16[128,384]{1,0:T(8,128)(2,1)S(1)} %get-tuple-element.32, bf16[128,4224]{1,0:T(8,128)(2,1)S(1)} %bitcast.19), kind=kOutput, calls=%fused_computation.3 | convolution fusion | flops 202113024 | bytes 2195456 | tf_op jit(solution)/shard_map/rh,rd->hd/dot_general | solution.py:199
  40.4 1.7 %fusion.1 = bf16[1,384,2048]{2,1,0:T(8,128)(2,1)} fusion(bf16[128,384]{1,0:T(8,128)(2,1)S(1)} %get-tuple-element.33, bf16[128,4224]{1,0:T(8,128)(2,1)S(1)} %bitcast.20), kind=kOutput, calls=%fused_computation.4 | convolution fusion | flops 202113024 | bytes 2195456 | tf_op jit(solution)/shard_map/rh,rd->hd/dot_general | solution.py:199
  42.1 1.7 %fusion.2 = bf16[1,384,2048]{2,1,0:T(8,128)(2,1)} fusion(bf16[128,384]{1,0:T(8,128)(2,1)S(1)} %get-tuple-element.34, bf16[128,4224]{1,0:T(8,128)(2,1)S(1)} %bitcast.21), kind=kOutput, calls=%fused_computation.5 | convolution fusion | flops 202113024 | bytes 2195456 | tf_op jit(solution)/shard_map/rh,rd->hd/dot_general | solution.py:199
  43.9 11.5 %all-to-all-done.1 = bf16[32,4,2176]{2,1,0:T(4,128)(2,1)S(1)} async-done(((bf16[32,4,2176]{2,1,0:T(4,128)(2,1)}), bf16[32,4,2176]{2,1,0:T(4,128)(2,1)S(1)}, u32[]{:S(2)}, u32[]{:S(2)}) %all-to-all-start.1) | async-done | bytes 557088 | tf_op jit(solution)/shard_map/all_to_all | solution.py:190
  55.3 0.1 reshape.19.back_ref
  55.5 0.8 %shard_map.113 = (bf16[16,2048]{1,0:T(8,128)(2,1)}, f32[1,16]{1,0:T(1,128)}) custom-call(bf16[16,128]{1,0:T(8,128)(2,1)S(1)} %tile.10.pick_ref, bf16[128,2176]{1,0:T(8,128)(2,1)S(1)} %reshape.19.back_ref), custom_call_target="tpu_custom_call" | custom-call | tf_op jit(solution)/shard_map/pallas_call | solution.py:143
  (1 shorter events, 0.0 us)
Async XLA Ops:
  0.6 9.4 %collective-permute-start = (bf16[16,2048]{1,0:T(8,128)(2,1)}, bf16[16,2048]{1,0:T(8,128)(2,1)S(1)}, u32[]{:S(2)}, u32[]{:S(2)}) collective-permute-start(bf16[16,2048]{1,0:T(8,128)(2,1)} %bitcast.27), channel_id=1, source_target_pairs={{0,8},{8,0},{1,9},{9,1},{2,10},{10,2},{3,11},{11,3},{4,12},{12,4},... | collective-permute-start | bytes 196616 | tf_op jit(solution)/shard_map/ppermute | solution.py:166
  3.8 6.2 %collective-permute-start.1 = (bf16[16,2048]{1,0:T(8,128)(2,1)}, bf16[16,2048]{1,0:T(8,128)(2,1)S(1)}, u32[]{:S(2)}, u32[]{:S(2)}) collective-permute-start(bf16[16,2048]{1,0:T(8,128)(2,1)} %bitcast.29), channel_id=1, source_target_pairs={{0,8},{8,0},{1,9},{9,1},{2,10},{10,2},{3,11},{11,3},{4,12},{12,4},... | collective-permute-start | bytes 196616 | tf_op jit(solution)/shard_map/ppermute | solution.py:166
  3.9 5.9 %collective-permute-start.3 = (bf16[2,16]{1,0:T(2,128)(2,1)}, bf16[2,16]{1,0:T(2,128)(2,1)S(1)}, u32[]{:S(2)}, u32[]{:S(2)}) collective-permute-start(bf16[2,16]{1,0:T(2,128)(2,1)} %refs_3_.1), channel_id=1, source_target_pairs={{0,8},{8,0},{1,9},{9,1},{2,10},{10,2},{3,11},{11,3},{4,12},{12,4},... | collective-permute-start | bytes 200 | tf_op jit(solution)/shard_map/ppermute | solution.py:166
  6.2 3.8 %collective-permute-start.2 = (s32[2,16]{1,0:T(2,128)}, s32[2,16]{1,0:T(2,128)S(1)}, u32[]{:S(2)}, u32[]{:S(2)}) collective-permute-start(s32[2,16]{1,0:T(2,128)} %refs_2_.1), channel_id=1, source_target_pairs={{0,8},{8,0},{1,9},{9,1},{2,10},{10,2},{3,11},{11,3},{4,12},{12,4},... | collective-permute-start | bytes 392 | tf_op jit(solution)/shard_map/ppermute | solution.py:166
  35.7 19.7 %all-to-all-start.1 = ((bf16[32,4,2176]{2,1,0:T(4,128)(2,1)}), bf16[32,4,2176]{2,1,0:T(4,128)(2,1)S(1)}, u32[]{:S(2)}, u32[]{:S(2)}) async-start(bf16[32,4,2176]{2,1,0:T(4,128)(2,1)} %get-tuple-element.29), calls=%async_computation.1 | async-start | bytes 1114112 | tf_op jit(solution)/shard_map/all_to_all | solution.py:190

commit v13 on v11

--- a/solution.py
+++ b/solution.py
@@ -132,13 +132,22 @@
             reply_ref[to, :, features:] = tail[rows].astype(BF16)
 
 
-def unpack_kernel(pick_ref, back_ref, tok_ref, prob_ref):
-    tok_dev, features = tok_ref.shape
-    total = dot(pick_ref[...], back_ref[...], (1, 0))
-    tok_ref[...] = total[:, :features].astype(BF16)
-    part = jnp.sum(total[:, features:], axis=1, keepdims=True)
+def unpack_kernel(pick_ref, back_ref, tok_hbm, prob_hbm, tok_v, prob_v, sems):
+    tok_dev, features = tok_v.shape
+    half = features // 2
+    part = dot(pick_ref[...], back_ref[:, features:], (1, 0))
+    part = jnp.sum(part, axis=1, keepdims=True)
     here, there = square(tok_dev)
-    prob_ref[...] = jnp.sum(jnp.where(here == there, part, 0.0), axis=0, keepdims=True)
+    prob_v[...] = jnp.sum(jnp.where(here == there, part, 0.0), axis=0, keepdims=True)
+    copies = [pltpu.make_async_copy(prob_v, prob_hbm, sems.at[0])]
+    copies[0].start()
+    for i in range(2):
+        at = pl.ds(i * half, half)
+        tok_v[:, at] = dot(pick_ref[...], back_ref[:, at], (1, 0)).astype(BF16)
+        copies.append(pltpu.make_async_copy(tok_v.at[:, at], tok_hbm.at[:, at], sems.at[i + 1]))
+        copies[-1].start()
+    for copy in copies:
+        copy.wait()
 
 
 def near(shape, dtype=BF16):
@@ -155,13 +164,13 @@
     return [pltpu.with_memory_space_constraint(a, pltpu.HBM) for a in arrays]
 
 
-def call(kernel, in_specs, outs, *args, scratch=(), cost=None):
+def call(kernel, in_specs, outs, *args, scratch=(), cost=None, out_spec=VMEM):
     small = all(math.prod(out.shape) <= NEAR_SIZE for out in outs)
     return pl.pallas_call(
         kernel,
         in_specs=in_specs,
         scratch_shapes=scratch,
-        out_specs=[VMEM] * len(outs),
+        out_specs=[out_spec] * len(outs),
         out_shape=outs,
         cost_estimate=cost,
         compiler_params=pltpu.CompilerParams(vmem_limit_bytes=(16 if small else 48) << 20),
@@ -222,6 +231,12 @@
         [VMEM] * 2,
         [jax.ShapeDtypeStruct((tok_dev, features), BF16), jax.ShapeDtypeStruct((1, tok_dev), F32)],
         jnp.tile(pick.T, (1, groups)), back.reshape(rows, features + LANES),
+        scratch=[
+            pltpu.VMEM((tok_dev, features), BF16),
+            pltpu.VMEM((1, tok_dev), F32),
+            pltpu.SemaphoreType.DMA((3,)),
+        ],
+        out_spec=HBM,
     )
     rows_x, rows_dy = got[:, :features], got[:, features : 2 * features]
     weight_grads = [

time: 55.9 us -> 55.9 us (level)
  no operation moved by 1% of the time
where the time goes in v13:
time: 55.9 us; the launch traced here: 55.7 us
  blocking collectives  22.1 us (40%)
  waiting for transfers between devices  11.3 us (20%)
  starting transfers between devices  8.77 us (16%)
  Pallas kernels  7.23 us (13%)
  matrix products  5.22 us (9%)
  between operations  0.71 us (1%)
    all_to_all x1, blocking collectives, body(): lax.all_to_all(send, HALF_AXES, split_axis=0, concat_axis=0, tiled=True)  22.1 us
    all_to_all x1, waiting for transfers between devices, body(): lax.all_to_all(reply, ALL_AXES, split_axis=0, concat_axis=0, tiled=True)  11.3 us
    pallas_call x5, Pallas kernels, call(): pl.pallas_call(kernel, in_specs=in_specs, scratch_shapes=scratch, out_spe...  7.23 us
    dot_general x3, matrix products, body(): jnp.einsum('rh,rd->hd', left, right, preferred_element_type=F32)  5.22 us
    ppermute x2, starting transfers between devices, body(): others = [lax.ppermute(a, 'top', SWAP) for a in (x, dy)]  3.28 us
    all_to_all x1, starting transfers between devices, body(): lax.all_to_all(reply, ALL_AXES, split_axis=0, concat_axis=0, tiled=True)  3.14 us
    ppermute x1, starting transfers between devices, body(): others.append(lax.ppermute(tail, 'top', SWAP))  2.35 us
  transfers between devices with their start and end apart: 4, of which 1 were waited for; matrix products, arithmetic and copies ran while one was open for 10% of the time, Pallas kernels for 7%

profile of v13, /device:TPU:1, one launch (start us, length us, event | category | flops | bytes accessed | tf_op | source)
XLA Modules:
  0.0 55.7 jit_solution(7619205575362938117)
XLA Ops:
  0.6 3.2 %collective-permute-start = (bf16[16,2048]{1,0:T(8,128)(2,1)}, bf16[16,2048]{1,0:T(8,128)(2,1)S(1)}, u32[]{:S(2)}, u32[]{:S(2)}) collective-permute-start(bf16[16,2048]{1,0:T(8,128)(2,1)} %bitcast.27), channel_id=1, source_target_pairs={{0,8},{8,0},{1,9},{9,1},{2,10},{10,2},{3,11},{11,3},{4,12},{12,4},... | collective-permute-start | bytes 196616 | tf_op jit(solution)/shard_map/ppermute | solution.py:192
  3.8 0.1 collective-permute-start.1
  3.9 0.8 %shard_map.111.refs_2_ = bf16[16,128]{1,0:T(8,128)(2,1)S(1)} custom-call(s32[2,16]{1,0:T(2,128)} %route_hbm.1, bf16[2,16]{1,0:T(2,128)(2,1)} %prob_hbm.1), custom_call_target="tpu_custom_call" | custom-call | tf_op jit(solution)/shard_map/pallas_call | solution.py:169
  4.7 2.3 %collective-permute-start.2 = (bf16[16,128]{1,0:T(8,128)(2,1)S(1)}, bf16[16,128]{1,0:T(8,128)(2,1)S(1)}, u32[]{:S(2)}, u32[]{:S(2)}) collective-permute-start(bf16[16,128]{1,0:T(8,128)(2,1)S(1)} %shard_map.111.refs_2_), channel_id=1, source_target_pairs={{0,8},{8,0},{1,9},{9,1},{2,10},{10,2},{3,11},{11,3},{4,12},{12,4},... | collective-permute-start | bytes 12296 | tf_op jit(solution)/shard_map/ppermute | solution.py:204
  7.1 2.9 %shard_map.110 = (bf16[16,2048]{1,0:T(8,128)(2,1)S(1)}, bf16[16,2048]{1,0:T(8,128)(2,1)S(1)}, bf16[768,2048]{1,0:T(8,128)(2,1)S(1)}, bf16[2048,768]{1,0:T(8,128)(2,1)S(1)}, bf16[2048,384]{1,0:T(8,128)(2,1)S(1)}) custom-call(bf16[16,2048]{1,0:T(8,128)(2,1)} %bitcast.28, bf16[16,2048]{1,0:T(8,128)(2,1)} %bitcast.30, bf16[384,2048]{1,0:T(8,128)(2,1)} %bitcast.24, ...), custom_call_target="tpu_custom_call" | custom-call | bytes 12582912 | tf_op jit(solution)/shard_map/pallas_call | solution.py:169
  10.0 0.0 collective-permute-done.2.refs_5_
  10.0 0.0 collective-permute-done.refs_3_
  10.0 0.0 collective-permute-done.1.refs_4_
  10.0 0.4 shard_map.112
  10.5 22.1 %all_to_all.16 = bf16[16,8,4224]{2,1,0:T(8,128)(2,1)S(1)} all-to-all(bf16[16,8,4224]{2,1,0:T(8,128)(2,1)S(1)} %bitcast.22), channel_id=1, replica_groups=mesh['dp'=2,'top'=2,'low'=8] {'dp','low'}, dimensions={0} | all-to-all | bytes 2162688 | tf_op jit(solution)/shard_map/all_to_all | solution.py:221
  32.6 2.2 %shard_map.113 = (bf16[32,4,2176]{2,1,0:T(4,128)(2,1)}, bf16[128,384]{1,0:T(8,128)(2,1)S(1)}, bf16[128,384]{1,0:T(8,128)(2,1)S(1)}, bf16[128,384]{1,0:T(8,128)(2,1)S(1)}) custom-call(bf16[128,4224]{1,0:T(8,128)(2,1)S(1)} %bitcast.18, bf16[768,2048]{1,0:T(8,128)(2,1)S(1)} %get-tuple-element.20.refs_6_.refs_1_, ...), custom_call_target="tpu_custom_call" | custom-call | tf_op jit(solution)/shard_map/pallas_call | solution.py:169
  34.8 3.1 %all-to-all-start.1 = ((bf16[32,4,2176]{2,1,0:T(4,128)(2,1)}), bf16[32,4,2176]{2,1,0:T(4,128)(2,1)S(1)}, u32[]{:S(2)}, u32[]{:S(2)}) async-start(bf16[32,4,2176]{2,1,0:T(4,128)(2,1)} %get-tuple-element.25), calls=%async_computation.1 | async-start | bytes 1114112 | tf_op jit(solution)/shard_map/all_to_all | solution.py:228
  37.9 0.1 copy.12
  38.0 0.1 tile.10.pick_ref
  38.1 1.7 %fusion = bf16[1,384,2048]{2,1,0:T(8,128)(2,1)} fusion(bf16[128,384]{1,0:T(8,128)(2,1)S(1)} %get-tuple-element.28, bf16[128,4224]{1,0:T(8,128)(2,1)S(1)} %bitcast.19), kind=kOutput, calls=%fused_computation.3 | convolution fusion | flops 202113024 | bytes 2195456 | tf_op jit(solution)/shard_map/rh,rd->hd/dot_general | solution.py:243
  39.9 1.7 %fusion.1 = bf16[1,384,2048]{2,1,0:T(8,128)(2,1)} fusion(bf16[128,384]{1,0:T(8,128)(2,1)S(1)} %get-tuple-element.29, bf16[128,4224]{1,0:T(8,128)(2,1)S(1)} %bitcast.20), kind=kOutput, calls=%fused_computation.4 | convolution fusion | flops 202113024 | bytes 2195456 | tf_op jit(solution)/shard_map/rh,rd->hd/dot_general | solution.py:243
  41.6 1.7 %fusion.2 = bf16[1,384,2048]{2,1,0:T(8,128)(2,1)} fusion(bf16[128,384]{1,0:T(8,128)(2,1)S(1)} %get-tuple-element.30, bf16[128,4224]{1,0:T(8,128)(2,1)S(1)} %bitcast.21), kind=kOutput, calls=%fused_computation.5 | convolution fusion | flops 202113024 | bytes 2195456 | tf_op jit(solution)/shard_map/rh,rd->hd/dot_general | solution.py:243
  43.3 11.3 %all-to-all-done.1 = bf16[32,4,2176]{2,1,0:T(4,128)(2,1)S(1)} async-done(((bf16[32,4,2176]{2,1,0:T(4,128)(2,1)}), bf16[32,4,2176]{2,1,0:T(4,128)(2,1)S(1)}, u32[]{:S(2)}, u32[]{:S(2)}) %all-to-all-start.1) | async-done | bytes 557088 | tf_op jit(solution)/shard_map/all_to_all | solution.py:228
  54.7 0.1 reshape.19.back_ref
  54.8 0.9 %shard_map.114 = (bf16[16,2048]{1,0:T(8,128)(2,1)}, f32[1,16]{1,0:T(1,128)}) custom-call(bf16[16,128]{1,0:T(8,128)(2,1)S(1)} %tile.10.pick_ref, bf16[128,2176]{1,0:T(8,128)(2,1)S(1)} %reshape.19.back_ref), custom_call_target="tpu_custom_call" | custom-call | tf_op jit(solution)/shard_map/pallas_call | solution.py:169
  (1 shorter events, 0.0 us)
Async XLA Ops:
  0.6 9.4 %collective-permute-start = (bf16[16,2048]{1,0:T(8,128)(2,1)}, bf16[16,2048]{1,0:T(8,128)(2,1)S(1)}, u32[]{:S(2)}, u32[]{:S(2)}) collective-permute-start(bf16[16,2048]{1,0:T(8,128)(2,1)} %bitcast.27), channel_id=1, source_target_pairs={{0,8},{8,0},{1,9},{9,1},{2,10},{10,2},{3,11},{11,3},{4,12},{12,4},... | collective-permute-start | bytes 196616 | tf_op jit(solution)/shard_map/ppermute | solution.py:192
  3.8 6.2 %collective-permute-start.1 = (bf16[16,2048]{1,0:T(8,128)(2,1)}, bf16[16,2048]{1,0:T(8,128)(2,1)S(1)}, u32[]{:S(2)}, u32[]{:S(2)}) collective-permute-start(bf16[16,2048]{1,0:T(8,128)(2,1)} %bitcast.29), channel_id=1, source_target_pairs={{0,8},{8,0},{1,9},{9,1},{2,10},{10,2},{3,11},{11,3},{4,12},{12,4},... | collective-permute-start | bytes 196616 | tf_op jit(solution)/shard_map/ppermute | solution.py:192
  4.7 5.3 %collective-permute-start.2 = (bf16[16,128]{1,0:T(8,128)(2,1)S(1)}, bf16[16,128]{1,0:T(8,128)(2,1)S(1)}, u32[]{:S(2)}, u32[]{:S(2)}) collective-permute-start(bf16[16,128]{1,0:T(8,128)(2,1)S(1)} %shard_map.111.refs_2_), channel_id=1, source_target_pairs={{0,8},{8,0},{1,9},{9,1},{2,10},{10,2},{3,11},{11,3},{4,12},{12,4},... | collective-permute-start | bytes 12296 | tf_op jit(solution)/shard_map/ppermute | solution.py:204
  34.8 19.9 %all-to-all-start.1 = ((bf16[32,4,2176]{2,1,0:T(4,128)(2,1)}), bf16[32,4,2176]{2,1,0:T(4,128)(2,1)S(1)}, u32[]{:S(2)}, u32[]{:S(2)}) async-start(bf16[32,4,2176]{2,1,0:T(4,128)(2,1)} %get-tuple-element.25), calls=%async_computation.1 | async-start | bytes 1114112 | tf_op jit(solution)/shard_map/all_to_all | solution.py:228

commit v14 on v11

--- a/solution.py
+++ b/solution.py
@@ -134,7 +134,8 @@
 
 def unpack_kernel(pick_ref, back_ref, tok_ref, prob_ref):
     tok_dev, features = tok_ref.shape
-    total = dot(pick_ref[...], back_ref[...], (1, 0))
+    back = back_ref[...].reshape(pick_ref.shape[1], back_ref.shape[2])
+    total = dot(pick_ref[...], back, (1, 0))
     tok_ref[...] = total[:, :features].astype(BF16)
     part = jnp.sum(total[:, features:], axis=1, keepdims=True)
     here, there = square(tok_dev)
@@ -221,7 +222,7 @@
         unpack_kernel,
         [VMEM] * 2,
         [jax.ShapeDtypeStruct((tok_dev, features), BF16), jax.ShapeDtypeStruct((1, tok_dev), F32)],
-        jnp.tile(pick.T, (1, groups)), back.reshape(rows, features + LANES),
+        jnp.tile(pick.T, (1, groups)), back,
     )
     rows_x, rows_dy = got[:, :features], got[:, features : 2 * features]
     weight_grads = [

time: 55.9 us -> 55.7 us (level)
  no operation moved by 1% of the time
where the time goes in v14:
time: 55.7 us; the launch traced here: 55.5 us
  blocking collectives  22.1 us (40%)
  waiting for transfers between devices  11.3 us (20%)
  starting transfers between devices  8.77 us (16%)
  Pallas kernels  7.21 us (13%)
  matrix products  5.22 us (9%)
  between operations  0.7 us (1%)
    all_to_all x1, blocking collectives, body(): lax.all_to_all(send, HALF_AXES, split_axis=0, concat_axis=0, tiled=True)  22.1 us
    all_to_all x1, waiting for transfers between devices, body(): lax.all_to_all(reply, ALL_AXES, split_axis=0, concat_axis=0, tiled=True)  11.3 us
    pallas_call x5, Pallas kernels, call(): pl.pallas_call(kernel, in_specs=in_specs, scratch_shapes=scratch, out_spe...  7.21 us
    dot_general x3, matrix products, body(): jnp.einsum('rh,rd->hd', left, right, preferred_element_type=F32)  5.22 us
    ppermute x2, starting transfers between devices, body(): others = [lax.ppermute(a, 'top', SWAP) for a in (x, dy)]  3.28 us
    all_to_all x1, starting transfers between devices, body(): lax.all_to_all(reply, ALL_AXES, split_axis=0, concat_axis=0, tiled=True)  3.14 us
    ppermute x1, starting transfers between devices, body(): others.append(lax.ppermute(tail, 'top', SWAP))  2.35 us
  transfers between devices with their start and end apart: 4, of which 1 were waited for; matrix products, arithmetic and copies ran while one was open for 10% of the time, Pallas kernels for 7%

profile of v14, /device:TPU:1, one launch (start us, length us, event | category | flops | bytes accessed | tf_op | source)
XLA Modules:
  0.0 55.5 jit_solution(4695800587399363549)
XLA Ops:
  0.6 3.2 %collective-permute-start = (bf16[16,2048]{1,0:T(8,128)(2,1)}, bf16[16,2048]{1,0:T(8,128)(2,1)S(1)}, u32[]{:S(2)}, u32[]{:S(2)}) collective-permute-start(bf16[16,2048]{1,0:T(8,128)(2,1)} %bitcast.27), channel_id=1, source_target_pairs={{0,8},{8,0},{1,9},{9,1},{2,10},{10,2},{3,11},{11,3},{4,12},{12,4},... | collective-permute-start | bytes 196616 | tf_op jit(solution)/shard_map/ppermute | solution.py:184
  3.8 0.1 collective-permute-start.1
  3.9 0.8 %shard_map.111.refs_2_ = bf16[16,128]{1,0:T(8,128)(2,1)S(1)} custom-call(s32[2,16]{1,0:T(2,128)} %route_hbm.1, bf16[2,16]{1,0:T(2,128)(2,1)} %prob_hbm.1), custom_call_target="tpu_custom_call" | custom-call | tf_op jit(solution)/shard_map/pallas_call | solution.py:161
  4.7 2.3 %collective-permute-start.2 = (bf16[16,128]{1,0:T(8,128)(2,1)S(1)}, bf16[16,128]{1,0:T(8,128)(2,1)S(1)}, u32[]{:S(2)}, u32[]{:S(2)}) collective-permute-start(bf16[16,128]{1,0:T(8,128)(2,1)S(1)} %shard_map.111.refs_2_), channel_id=1, source_target_pairs={{0,8},{8,0},{1,9},{9,1},{2,10},{10,2},{3,11},{11,3},{4,12},{12,4},... | collective-permute-start | bytes 12296 | tf_op jit(solution)/shard_map/ppermute | solution.py:196
  7.1 2.9 %shard_map.110 = (bf16[16,2048]{1,0:T(8,128)(2,1)S(1)}, bf16[16,2048]{1,0:T(8,128)(2,1)S(1)}, bf16[768,2048]{1,0:T(8,128)(2,1)S(1)}, bf16[2048,768]{1,0:T(8,128)(2,1)S(1)}, bf16[2048,384]{1,0:T(8,128)(2,1)S(1)}) custom-call(bf16[16,2048]{1,0:T(8,128)(2,1)} %bitcast.28, bf16[16,2048]{1,0:T(8,128)(2,1)} %bitcast.30, bf16[384,2048]{1,0:T(8,128)(2,1)} %bitcast.24, ...), custom_call_target="tpu_custom_call" | custom-call | bytes 12582912 | tf_op jit(solution)/shard_map/pallas_call | solution.py:161
  10.0 0.0 collective-permute-done.2.refs_5_
  10.0 0.0 collective-permute-done.refs_3_
  10.0 0.0 collective-permute-done.1.refs_4_
  10.0 0.4 shard_map.112
  10.5 22.1 %all_to_all.16 = bf16[16,8,4224]{2,1,0:T(8,128)(2,1)S(1)} all-to-all(bf16[16,8,4224]{2,1,0:T(8,128)(2,1)S(1)} %bitcast.22), channel_id=1, replica_groups=mesh['dp'=2,'top'=2,'low'=8] {'dp','low'}, dimensions={0} | all-to-all | bytes 2162688 | tf_op jit(solution)/shard_map/all_to_all | solution.py:213
  32.6 2.2 %shard_map.113 = (bf16[32,4,2176]{2,1,0:T(4,128)(2,1)}, bf16[128,384]{1,0:T(8,128)(2,1)S(1)}, bf16[128,384]{1,0:T(8,128)(2,1)S(1)}, bf16[128,384]{1,0:T(8,128)(2,1)S(1)}) custom-call(bf16[128,4224]{1,0:T(8,128)(2,1)S(1)} %bitcast.18, bf16[768,2048]{1,0:T(8,128)(2,1)S(1)} %get-tuple-element.20.refs_6_.refs_1_, ...), custom_call_target="tpu_custom_call" | custom-call | tf_op jit(solution)/shard_map/pallas_call | solution.py:161
  34.8 3.1 %all-to-all-start.1 = ((bf16[32,4,2176]{2,1,0:T(4,128)(2,1)}), bf16[32,4,2176]{2,1,0:T(4,128)(2,1)S(1)}, u32[]{:S(2)}, u32[]{:S(2)}) async-start(bf16[32,4,2176]{2,1,0:T(4,128)(2,1)} %get-tuple-element.25), calls=%async_computation.1 | async-start | bytes 1114112 | tf_op jit(solution)/shard_map/all_to_all | solution.py:220
  37.9 0.1 copy.12
  38.0 0.1 tile.10.pick_ref
  38.1 1.7 %fusion = bf16[1,384,2048]{2,1,0:T(8,128)(2,1)} fusion(bf16[128,384]{1,0:T(8,128)(2,1)S(1)} %get-tuple-element.28, bf16[128,4224]{1,0:T(8,128)(2,1)S(1)} %bitcast.19), kind=kOutput, calls=%fused_computation.3 | convolution fusion | flops 202113024 | bytes 2195456 | tf_op jit(solution)/shard_map/rh,rd->hd/dot_general | solution.py:229
  39.9 1.7 %fusion.1 = bf16[1,384,2048]{2,1,0:T(8,128)(2,1)} fusion(bf16[128,384]{1,0:T(8,128)(2,1)S(1)} %get-tuple-element.29, bf16[128,4224]{1,0:T(8,128)(2,1)S(1)} %bitcast.20), kind=kOutput, calls=%fused_computation.4 | convolution fusion | flops 202113024 | bytes 2195456 | tf_op jit(solution)/shard_map/rh,rd->hd/dot_general | solution.py:229
  41.6 1.7 %fusion.2 = bf16[1,384,2048]{2,1,0:T(8,128)(2,1)} fusion(bf16[128,384]{1,0:T(8,128)(2,1)S(1)} %get-tuple-element.30, bf16[128,4224]{1,0:T(8,128)(2,1)S(1)} %bitcast.21), kind=kOutput, calls=%fused_computation.5 | convolution fusion | flops 202113024 | bytes 2195456 | tf_op jit(solution)/shard_map/rh,rd->hd/dot_general | solution.py:229
  43.3 11.3 %all-to-all-done.1.back_ref = bf16[32,4,2176]{2,1,0:T(4,128)(2,1)S(1)} async-done(((bf16[32,4,2176]{2,1,0:T(4,128)(2,1)}), bf16[32,4,2176]{2,1,0:T(4,128)(2,1)S(1)}, u32[]{:S(2)}, u32[]{:S(2)}) %all-to-all-start.1) | async-done | bytes 557088 | tf_op jit(solution)/shard_map/all_to_all | solution.py:220
  54.7 0.9 %shard_map.114 = (bf16[16,2048]{1,0:T(8,128)(2,1)}, f32[1,16]{1,0:T(1,128)}) custom-call(bf16[16,128]{1,0:T(8,128)(2,1)S(1)} %tile.10.pick_ref, bf16[32,4,2176]{2,1,0:T(4,128)(2,1)S(1)} %all-to-all-done.1.back_ref), custom_call_target="tpu_custom_call" | custom-call | tf_op jit(solution)/shard_map/pallas_call | solution.py:161
  (1 shorter events, 0.0 us)
Async XLA Ops:
  0.6 9.4 %collective-permute-start = (bf16[16,2048]{1,0:T(8,128)(2,1)}, bf16[16,2048]{1,0:T(8,128)(2,1)S(1)}, u32[]{:S(2)}, u32[]{:S(2)}) collective-permute-start(bf16[16,2048]{1,0:T(8,128)(2,1)} %bitcast.27), channel_id=1, source_target_pairs={{0,8},{8,0},{1,9},{9,1},{2,10},{10,2},{3,11},{11,3},{4,12},{12,4},... | collective-permute-start | bytes 196616 | tf_op jit(solution)/shard_map/ppermute | solution.py:184
  3.8 6.2 %collective-permute-start.1 = (bf16[16,2048]{1,0:T(8,128)(2,1)}, bf16[16,2048]{1,0:T(8,128)(2,1)S(1)}, u32[]{:S(2)}, u32[]{:S(2)}) collective-permute-start(bf16[16,2048]{1,0:T(8,128)(2,1)} %bitcast.29), channel_id=1, source_target_pairs={{0,8},{8,0},{1,9},{9,1},{2,10},{10,2},{3,11},{11,3},{4,12},{12,4},... | collective-permute-start | bytes 196616 | tf_op jit(solution)/shard_map/ppermute | solution.py:184
  4.7 5.3 %collective-permute-start.2 = (bf16[16,128]{1,0:T(8,128)(2,1)S(1)}, bf16[16,128]{1,0:T(8,128)(2,1)S(1)}, u32[]{:S(2)}, u32[]{:S(2)}) collective-permute-start(bf16[16,128]{1,0:T(8,128)(2,1)S(1)} %shard_map.111.refs_2_), channel_id=1, source_target_pairs={{0,8},{8,0},{1,9},{9,1},{2,10},{10,2},{3,11},{11,3},{4,12},{12,4},... | collective-permute-start | bytes 12296 | tf_op jit(solution)/shard_map/ppermute | solution.py:196
  34.8 19.9 %all-to-all-start.1 = ((bf16[32,4,2176]{2,1,0:T(4,128)(2,1)}), bf16[32,4,2176]{2,1,0:T(4,128)(2,1)S(1)}, u32[]{:S(2)}, u32[]{:S(2)}) async-start(bf16[32,4,2176]{2,1,0:T(4,128)(2,1)} %get-tuple-element.25), calls=%async_computation.1 | async-start | bytes 1114112 | tf_op jit(solution)/shard_map/all_to_all | solution.py:220
